TPU v7x, 32 devices: a whole 2x2x4 slice. The times are simulated.
32 devices in a mesh: ctx: 16 (over z, x, core), fs: 2 (over y).
Axes of the slice: x: 2, y: 2, z: 4, core: 2. Of those that a mesh axis runs over, the one named last changes fastest.
Arguments:
- tokens: bfloat16 [2, 4096, 1280], P('fs', 'ctx'), may hold values from -6 to 6
- query_weight: bfloat16 [1280, 1280], P('fs'), may hold values from -0.15625 to 0.15625
- key_weight: bfloat16 [1280, 1280], P('fs'), may hold values from -0.15625 to 0.15625
- value_weight: bfloat16 [1280, 1280], P('fs'), may hold values from -0.15625 to 0.15625
- out_weight: bfloat16 [1280, 1280], P('fs'), may hold values from -0.625 to 0.625
- inner_weight: bfloat16 [1280, 1280], P('fs'), may hold values from -0.15625 to 0.15625
- outer_weight: bfloat16 [1280, 1280], P('fs'), may hold values from -0.15625 to 0.15625
- attn_gain: bfloat16 [1280], P('fs'), may hold values from 0.099609375 to 1.8984375
- mlp_gain: bfloat16 [1280], P('fs'), may hold values from 0.099609375 to 1.8984375
- query_scale: float32 [80], replicated, may hold values from 0.5 to 2
- doc_starts: int32 [2, 8], P('fs'), may hold values from 0 to 4095, as said below
- cotangent: bfloat16 [2, 4096, 1280], P('fs', 'ctx'), may hold values from -6 to 6
Outputs:
- output: bfloat16 [2, 4096, 1280], P('fs', 'ctx')
- tokens_grad: bfloat16 [2, 4096, 1280], P('fs', 'ctx')
- query_grad: float32 [1280, 1280], P('fs')
- key_grad: float32 [1280, 1280], P('fs')
- value_grad: float32 [1280, 1280], P('fs')
- out_grad: float32 [1280, 1280], P('fs')
- inner_grad: float32 [1280, 1280], P('fs')
- outer_grad: float32 [1280, 1280], P('fs')
- attn_gain_grad: float32 [1280], P('fs')
- mlp_gain_grad: float32 [1280], P('fs')
- query_scale_grad: float32 [80], replicated
Inputs may be any that keep to these rules, and one draw needn't show every extreme that they name: `doc_starts`: within a stream the starts rise strictly, the first is 0 and the last is 4095. In every stream one document begins in the first 256 positions and ends in the last 256.
All inputs are finite; a program needn't handle non-finite values.
Results may differ from a plain program's by a relative error of at most 0.024.
Values may be sent and summed in bfloat16 or wider, within the bound.
A program may use at most 128 MiB of HBM per device.

v0:
```python
import math

import jax
import jax.numpy as jnp
from jax import lax
from jax.sharding import PartitionSpec as P

H = 16
HD = 80


epsilon = 1e-06
neg_big = -1e30


def passed_along(block, axis, distance):
    devices = range(lax.axis_size(axis))
    route = [((i - distance) % len(devices), i) for i in devices]
    return lax.ppermute(block, axis, route)


def shifted(value, axis, steps):
    count = lax.axis_size(axis)
    leading, last = (max(0, -steps), min(count, count - steps))
    return lax.ppermute(value, axis, [(source, source + steps) for source in range(leading, last)])


def rms_scale(values_in):
    return lax.rsqrt(jnp.mean(values_in * values_in, axis=-1, keepdims=True) + epsilon)


def norm_back(grad_normed, normed, scale_rows):
    inner_mean = jnp.mean(grad_normed * normed, axis=-1, keepdims=True)
    return scale_rows * (grad_normed - normed * inner_mean)


def segment_of(positions, starts_row):
    return jnp.sum((starts_row[None, :] <= positions[:, None]).astype(jnp.int32), axis=1) - 1


def block_mask(query_pos, query_seg, key_pos, key_seg):
    return (key_pos[None, :] <= query_pos[:, None]) & (key_seg[None, :] == query_seg[:, None])


def scores_of(query_block, key_block):
    return jnp.einsum("qhd,khd->hqk", query_block, key_block, preferred_element_type=jnp.float32)


def pass_grads(grad_key_acc, grad_value_acc):
    return (
        passed_along(grad_key_acc.astype(jnp.bfloat16), "ctx", 1).astype(grad_key_acc.dtype),
        passed_along(grad_value_acc.astype(jnp.bfloat16), "ctx", 1).astype(grad_value_acc.dtype),
    )


def local(
    tokens,
    query_weight,
    key_weight,
    value_weight,
    out_weight,
    inner_weight,
    outer_weight,
    attn_gain,
    mlp_gain,
    query_scale,
    doc_starts,
    cotangent,
):
    row_count = tokens.shape[1]
    model_width = tokens.shape[2]
    ctx_count = lax.axis_size("ctx")
    ctx_place = lax.axis_index("ctx")
    (
        query_full,
        key_full,
        value_full,
        out_full,
        inner_full,
        outer_full,
        attn_gain_full,
        mlp_gain_full,
    ) = (
        lax.all_gather(query_weight, "fs", axis=0, tiled=True),
        lax.all_gather(key_weight, "fs", axis=0, tiled=True),
        lax.all_gather(value_weight, "fs", axis=0, tiled=True),
        lax.all_gather(out_weight, "fs", axis=0, tiled=True),
        lax.all_gather(inner_weight, "fs", axis=0, tiled=True),
        lax.all_gather(outer_weight, "fs", axis=0, tiled=True),
        lax.all_gather(attn_gain, "fs", axis=0, tiled=True),
        lax.all_gather(mlp_gain, "fs", axis=0, tiled=True),
    )
    starts_row = doc_starts[0]
    local_pos = ctx_place * row_count + jnp.arange(row_count, dtype=jnp.int32)
    local_seg = segment_of(local_pos, starts_row)

    def heads_of(flat_block):
        return flat_block.reshape(row_count, H, HD)

    token_rows = tokens[0].astype(jnp.float32)
    scale_one = rms_scale(token_rows)
    normed_one = token_rows * scale_one
    gain_one = attn_gain_full.astype(jnp.float32)
    hidden_one = (normed_one * gain_one).astype(jnp.bfloat16)
    query_raw = jnp.dot(hidden_one, query_full, preferred_element_type=jnp.float32)
    scale_vec = jnp.tile(query_scale, H) / math.sqrt(HD)
    queries = heads_of((query_raw * scale_vec).astype(jnp.bfloat16))
    key_rows = jnp.dot(hidden_one, key_full, preferred_element_type=jnp.float32).astype(
        jnp.bfloat16
    )
    value_rows = jnp.dot(hidden_one, value_full, preferred_element_type=jnp.float32).astype(
        jnp.bfloat16
    )

    def key_info(turn_index):
        source = (ctx_place - turn_index) % ctx_count
        key_pos = source * row_count + jnp.arange(row_count, dtype=jnp.int32)
        return (source, key_pos, segment_of(key_pos, starts_row))

    def keep_state(state_in):
        return state_in

    def attend(softmax_state, key_flat, value_flat, turn_index):
        source, key_pos, key_seg = key_info(turn_index)

        def compute(state_in):
            run_max, run_sum, run_acc = state_in
            key_block = heads_of(key_flat)
            value_block = heads_of(value_flat)
            allowed = block_mask(local_pos, local_seg, key_pos, key_seg)
            scores = jnp.where(allowed[None], scores_of(queries, key_block), neg_big)
            new_max = jnp.maximum(run_max, jnp.max(scores, axis=-1))
            weights = jnp.where(allowed[None], jnp.exp(scores - new_max[..., None]), 0.0)
            factor = jnp.exp(run_max - new_max)
            run_sum = run_sum * factor + jnp.sum(weights, axis=-1)
            run_acc = run_acc * factor[..., None] + jnp.einsum(
                "hqk,khd->hqd",
                weights.astype(jnp.bfloat16),
                value_block,
                preferred_element_type=jnp.float32,
            )
            return (new_max, run_sum, run_acc)

        return lax.cond(source <= ctx_place, compute, keep_state, softmax_state)

    start_state = (
        jnp.full((H, row_count), neg_big, jnp.float32),
        jnp.zeros((H, row_count), jnp.float32),
        jnp.zeros((H, row_count, HD), jnp.float32),
    )
    start_state = attend(start_state, key_rows, value_rows, jnp.int32(0))
    stores = ()

    def forward_turn(turn_index, loop_state):
        key_block, value_block, softmax_state, kept = loop_state
        key_block, value_block = shifted((key_block, value_block), "ctx", 1)
        softmax_state = attend(softmax_state, key_block, value_block, turn_index)
        return (key_block, value_block, softmax_state, kept)

    loop_out = lax.fori_loop(
        1, ctx_count, forward_turn, (key_rows, value_rows, start_state, stores)
    )
    run_max, run_sum, run_acc = loop_out[2]
    stores = loop_out[3]
    log_total = run_max + jnp.log(run_sum)
    attn_heads = run_acc / run_sum[..., None]
    attn_low = (
        jnp.transpose(attn_heads, (1, 0, 2)).reshape(row_count, model_width).astype(jnp.bfloat16)
    )
    resid = token_rows + jnp.dot(attn_low, out_full, preferred_element_type=jnp.float32)
    scale_two = rms_scale(resid)
    normed_two = resid * scale_two
    gain_two = mlp_gain_full.astype(jnp.float32)
    hidden_two = (normed_two * gain_two).astype(jnp.bfloat16)
    inner_pre = jnp.dot(hidden_two, inner_full, preferred_element_type=jnp.float32)
    active = jax.nn.silu(inner_pre).astype(jnp.bfloat16)
    result = resid + jnp.dot(active, outer_full, preferred_element_type=jnp.float32)
    grad_out = cotangent[0]
    grad_active = jnp.dot(grad_out, outer_full.T, preferred_element_type=jnp.float32)
    grad_outer = jnp.dot(active.T, grad_out, preferred_element_type=jnp.float32)
    sigmoid_in = jax.nn.sigmoid(inner_pre)
    grad_inner_pre = (grad_active * sigmoid_in * (1.0 + inner_pre * (1.0 - sigmoid_in))).astype(
        jnp.bfloat16
    )
    grad_inner = jnp.dot(hidden_two.T, grad_inner_pre, preferred_element_type=jnp.float32)
    grad_hidden_two = jnp.dot(grad_inner_pre, inner_full.T, preferred_element_type=jnp.float32)
    grad_gain_two = jnp.sum(grad_hidden_two * normed_two, axis=0)
    grad_resid = grad_out.astype(jnp.float32) + norm_back(
        grad_hidden_two * gain_two, normed_two, scale_two
    )
    grad_resid_low = grad_resid.astype(jnp.bfloat16)
    grad_outw = jnp.dot(attn_low.T, grad_resid_low, preferred_element_type=jnp.float32)
    grad_attended = heads_of(
        jnp.dot(grad_resid_low, out_full.T, preferred_element_type=jnp.float32).astype(jnp.bfloat16)
    )
    row_delta = jnp.einsum("qhd,hqd->hq", grad_attended.astype(jnp.float32), attn_heads)

    def attend_back(grad_parts, key_flat, value_flat, turn_index):
        source, key_pos, key_seg = key_info(turn_index)

        def compute(parts_in):
            grad_query_acc, grad_key_acc, grad_value_acc = parts_in
            key_block = heads_of(key_flat)
            value_block = heads_of(value_flat)
            allowed = block_mask(local_pos, local_seg, key_pos, key_seg)
            scores = scores_of(queries, key_block)
            probabilities = jnp.where(allowed[None], jnp.exp(scores - log_total[..., None]), 0.0)
            grad_value_acc = grad_value_acc + jnp.einsum(
                "hqk,qhd->khd",
                probabilities.astype(jnp.bfloat16),
                grad_attended,
                preferred_element_type=jnp.float32,
            ).reshape(row_count, model_width)
            grad_probs = jnp.einsum(
                "qhd,khd->hqk", grad_attended, value_block, preferred_element_type=jnp.float32
            )
            grad_scores = (probabilities * (grad_probs - row_delta[..., None])).astype(jnp.bfloat16)
            grad_query_acc = grad_query_acc + jnp.einsum(
                "hqk,khd->qhd", grad_scores, key_block, preferred_element_type=jnp.float32
            )
            grad_key_acc = grad_key_acc + jnp.einsum(
                "hqk,qhd->khd", grad_scores, queries, preferred_element_type=jnp.float32
            ).reshape(row_count, model_width)
            return (grad_query_acc, grad_key_acc, grad_value_acc)

        return lax.cond(source <= ctx_place, compute, keep_state, grad_parts)

    def back_compute(turn_index, loop_state):
        key_block, value_block, grad_parts = loop_state
        grad_parts = attend_back(grad_parts, key_block, value_block, turn_index)
        grad_key_acc, grad_value_acc = pass_grads(grad_parts[1], grad_parts[2])
        return (key_block, value_block, (grad_parts[0], grad_key_acc, grad_value_acc))

    def back_turn(turn_index, loop_state):
        key_block, value_block, grad_parts = back_compute(turn_index, loop_state)
        key_block, value_block = shifted((key_block, value_block), "ctx", 1)
        return (key_block, value_block, grad_parts)

    zero_heads = jnp.zeros((row_count, H, HD), jnp.float32)
    zero_flat = jnp.zeros((row_count, model_width), jnp.float32)
    back_state = lax.fori_loop(
        0, ctx_count - 1, back_turn, (key_rows, value_rows, (zero_heads, zero_flat, zero_flat))
    )
    back_state = back_compute(jnp.int32(ctx_count - 1), back_state)
    grad_query_acc, grad_key_acc, grad_value_acc = back_state[2]
    grad_query_flat = grad_query_acc.reshape(row_count, model_width)
    grad_key_low = grad_key_acc.astype(jnp.bfloat16)
    grad_value_low = grad_value_acc.astype(jnp.bfloat16)
    grad_query_raw = (grad_query_flat * scale_vec).astype(jnp.bfloat16)
    grad_scale = jnp.sum(
        (grad_query_flat * query_raw).reshape(row_count, H, HD), axis=(0, 1)
    ) / math.sqrt(HD)
    grad_qw = jnp.dot(hidden_one.T, grad_query_raw, preferred_element_type=jnp.float32)
    grad_kw = jnp.dot(hidden_one.T, grad_key_low, preferred_element_type=jnp.float32)
    grad_vw = jnp.dot(hidden_one.T, grad_value_low, preferred_element_type=jnp.float32)
    grad_hidden_one = (
        jnp.dot(grad_query_raw, query_full.T, preferred_element_type=jnp.float32)
        + jnp.dot(grad_key_low, key_full.T, preferred_element_type=jnp.float32)
        + jnp.dot(grad_value_low, value_full.T, preferred_element_type=jnp.float32)
    )
    grad_gain_one = jnp.sum(grad_hidden_one * normed_one, axis=0)
    grad_tokens = grad_resid_low.astype(jnp.float32) + norm_back(
        grad_hidden_one * gain_one, normed_one, scale_one
    )
    shard_count = lax.axis_size("fs")
    scale_rows = jnp.broadcast_to(grad_scale[None, :], (shard_count, grad_scale.shape[0]))
    shares = (
        lax.psum_scatter(
            grad_qw.astype(jnp.bfloat16), "fs", scatter_dimension=0, tiled=True
        ).astype(jnp.float32),
        lax.psum_scatter(
            grad_kw.astype(jnp.bfloat16), "fs", scatter_dimension=0, tiled=True
        ).astype(jnp.float32),
        lax.psum_scatter(
            grad_vw.astype(jnp.bfloat16), "fs", scatter_dimension=0, tiled=True
        ).astype(jnp.float32),
        lax.psum_scatter(
            grad_outw.astype(jnp.bfloat16), "fs", scatter_dimension=0, tiled=True
        ).astype(jnp.float32),
        lax.psum_scatter(
            grad_inner.astype(jnp.bfloat16), "fs", scatter_dimension=0, tiled=True
        ).astype(jnp.float32),
        lax.psum_scatter(
            grad_outer.astype(jnp.bfloat16), "fs", scatter_dimension=0, tiled=True
        ).astype(jnp.float32),
        lax.psum_scatter(
            grad_gain_one.astype(jnp.bfloat16), "fs", scatter_dimension=0, tiled=True
        ).astype(jnp.float32),
        lax.psum_scatter(
            grad_gain_two.astype(jnp.bfloat16), "fs", scatter_dimension=0, tiled=True
        ).astype(jnp.float32),
        lax.psum_scatter(
            scale_rows.astype(jnp.bfloat16), "fs", scatter_dimension=0, tiled=True
        ).astype(jnp.float32),
    )
    totals = (
        lax.psum(shares[0].astype(jnp.bfloat16), "ctx").astype(jnp.float32),
        lax.psum(shares[1].astype(jnp.bfloat16), "ctx").astype(jnp.float32),
        lax.psum(shares[2].astype(jnp.bfloat16), "ctx").astype(jnp.float32),
        lax.psum(shares[3].astype(jnp.bfloat16), "ctx").astype(jnp.float32),
        lax.psum(shares[4].astype(jnp.bfloat16), "ctx").astype(jnp.float32),
        lax.psum(shares[5].astype(jnp.bfloat16), "ctx").astype(jnp.float32),
        lax.psum(shares[6].astype(jnp.bfloat16), "ctx").astype(jnp.float32),
        lax.psum(shares[7].astype(jnp.bfloat16), "ctx").astype(jnp.float32),
        lax.psum(shares[8].astype(jnp.bfloat16), "ctx").astype(jnp.float32),
    )
    return (
        result[None].astype(jnp.bfloat16),
        grad_tokens[None].astype(jnp.bfloat16),
        totals[0],
        totals[1],
        totals[2],
        totals[3],
        totals[4],
        totals[5],
        totals[6],
        totals[7],
        totals[8][0],
    )


def solution(mesh):
    placed = (
        P("fs", "ctx", None),
        P("fs", None),
        P("fs", None),
        P("fs", None),
        P("fs", None),
        P("fs", None),
        P("fs", None),
        P("fs"),
        P("fs"),
        P(),
        P("fs", None),
        P("fs", "ctx", None),
    )
    return jax.shard_map(
        local,
        mesh=mesh,
        in_specs=placed,
        out_specs=(
            P("fs", "ctx", None),
            P("fs", "ctx", None),
            P("fs", None),
            P("fs", None),
            P("fs", None),
            P("fs", None),
            P("fs", None),
            P("fs", None),
            P("fs"),
            P("fs"),
            P(),
        ),
        check_vma=False,
    )
```

profile of v0, /device:TPU:0, one launch (start us, length us, event | category | flops | bytes accessed | tf_op | source)
XLA Modules:
  0.0 1840.4 jit_solution(10938345691382094596)
XLA Ops:
  21.5 37.2 %all-gather.9.cloned.1.call-done = bf16[1280,1280]{1,0:T(8,128)(2,1)} async-done(((bf16[640,1280]{1,0:T(8,128)(2,1)}), bf16[1280,1280]{1,0:T(8,128)(2,1)}) %all-gather.9.cloned.1.call-update) | async-done | bytes 3276816 | tf_op jit(solution)/shard_map/all_gather | solution.py:85
  62.0 44.7 %all-gather.11.cloned.1.call-done = bf16[1280,1280]{1,0:T(8,128)(2,1)} async-done(((bf16[640,1280]{1,0:T(8,128)(2,1)}), bf16[1280,1280]{1,0:T(8,128)(2,1)}) %all-gather.11.cloned.1.call-update) | async-done | bytes 3276816 | tf_op jit(solution)/shard_map/all_gather | solution.py:86
  112.8 41.9 %all-gather.13.cloned.1.call-done = bf16[1280,1280]{1,0:T(8,128)(2,1)} async-done(((bf16[640,1280]{1,0:T(8,128)(2,1)}), bf16[1280,1280]{1,0:T(8,128)(2,1)}) %all-gather.13.cloned.1.call-update) | async-done | bytes 3276816 | tf_op jit(solution)/shard_map/all_gather | solution.py:84
  168.4 336.5 %while.48 = (s32[]{:T(128)}, bf16[256,1280]{0,1:T(8,128)(2,1)S(1)}, bf16[256,1280]{0,1:T(8,128)(2,1)}, f32[16,256]{1,0:T(8,128)}, f32[16,256]{1,0:T(8,128)S(1)},...) while((s32[]{:T(128)}, bf16[256,1280]{0,1:T(8,128)(2,1)S(1)}, ...), condition=%wide.region_13.14_spmd.clone, body=%wide.region_7.13_spmd.clone.sunk | while | flops 346897152 | bytes 25590336 | solution.py:160
  176.7 20.1 %collective-permute-start = (bf16[256,1280]{0,1:T(8,128)(2,1)S(1)}, bf16[256,1280]{0,1:T(8,128)(2,1)S(1)}, u32[]{:S(2)}, u32[]{:S(2)}) collective-permute-start(bf16[256,1280]{0,1:T(8,128)(2,1)S(1)} %get-tuple-element.1454), channel_id=1, source_target_pairs={{0,2},{2,4},{4,6},{6,8},{8,10},{10,12},{12,14},{14,16},{16,18},{18... | collective-permute-start | bytes 1966088 | tf_op jit(solution)/shard_map/while/body/eval_jaxpr/ppermute | solution.py:25
  203.9 12.7 collective-permute-start
  216.7 11.7 collective-permute-start.1
  231.1 12.7 collective-permute-start
  250.9 16.2 collective-permute-start
  274.2 13.6 collective-permute-start
  297.3 18.7 %collective-permute-start = (bf16[256,1280]{0,1:T(8,128)(2,1)S(1)}, bf16[256,1280]{0,1:T(8,128)(2,1)S(1)}, u32[]{:S(2)}, u32[]{:S(2)}) collective-permute-start(bf16[256,1280]{0,1:T(8,128)(2,1)S(1)} %get-tuple-element.1454), channel_id=1, source_target_pairs={{0,2},{2,4},{4,6},{6,8},{8,10},{10,12},{12,14},{14,16},{16,18},{18... | collective-permute-start | bytes 1966088 | tf_op jit(solution)/shard_map/while/body/eval_jaxpr/ppermute | solution.py:25
  323.0 13.6 collective-permute-start
  343.7 13.6 collective-permute-start
  364.4 16.4 collective-permute-start
  387.8 19.8 %collective-permute-start = (bf16[256,1280]{0,1:T(8,128)(2,1)S(1)}, bf16[256,1280]{0,1:T(8,128)(2,1)S(1)}, u32[]{:S(2)}, u32[]{:S(2)}) collective-permute-start(bf16[256,1280]{0,1:T(8,128)(2,1)S(1)} %get-tuple-element.1454), channel_id=1, source_target_pairs={{0,2},{2,4},{4,6},{6,8},{8,10},{10,12},{12,14},{14,16},{16,18},{18... | collective-permute-start | bytes 1966088 | tf_op jit(solution)/shard_map/while/body/eval_jaxpr/ppermute | solution.py:25
  414.7 13.6 collective-permute-start
  435.4 21.0 %collective-permute-start = (bf16[256,1280]{0,1:T(8,128)(2,1)S(1)}, bf16[256,1280]{0,1:T(8,128)(2,1)S(1)}, u32[]{:S(2)}, u32[]{:S(2)}) collective-permute-start(bf16[256,1280]{0,1:T(8,128)(2,1)S(1)} %get-tuple-element.1454), channel_id=1, source_target_pairs={{0,2},{2,4},{4,6},{6,8},{8,10},{10,12},{12,14},{14,16},{16,18},{18... | collective-permute-start | bytes 1966088 | tf_op jit(solution)/shard_map/while/body/eval_jaxpr/ppermute | solution.py:25
  463.5 13.6 collective-permute-start
  484.2 13.6 collective-permute-start
  525.6 772.6 %while.49 = (s32[]{:T(128)}, bf16[256,1280]{0,1:T(8,128)(2,1)S(1)}, bf16[256,1280]{0,1:T(8,128)(2,1)}, f32[256,16,80]{0,2,1:T(8,128)}, f32[256,1280]{0,1:T(8,128...) while((s32[]{:T(128)}, bf16[256,1280]{0,1:T(8,128)(2,1)S(1)}, ...), condition=%wide.region_20.21_spmd.clone, body=%wide.region_16.20_spmd.clone.sunk | while | flops 850402048 | bytes 106052552 | solution.py:241
  528.9 12.5 conditional.11
  542.3 13.3 collective-permute-start.4
  558.9 15.1 collective-permute-start.2
  580.0 33.2 %collective-permute-done.4 = bf16[256,1280]{0,1:T(8,128)(2,1)} collective-permute-done((bf16[256,1280]{0,1:T(8,128)(2,1)}, bf16[256,1280]{0,1:T(8,128)(2,1)}, u32[]{:S(2)}, u32[]{:S(2)}) %collective-permute-start.4) | collective-permute-done | bytes 655392 | tf_op jit(solution)/shard_map/while/body/eval_jaxpr/ppermute | solution.py:19
  634.4 14.2 collective-permute-done.4
  710.2 19.8 %collective-permute-start.2 = (bf16[256,1280]{0,1:T(8,128)(2,1)S(1)}, bf16[256,1280]{0,1:T(8,128)(2,1)S(1)}, u32[]{:S(2)}, u32[]{:S(2)}) collective-permute-start(bf16[256,1280]{0,1:T(8,128)(2,1)S(1)} %copy-done.1), channel_id=1, source_target_pairs={{0,2},{2,4},{4,6},{6,8},{8,10},{10,12},{12,14},{14,16},{16,18},{18... | collective-permute-start | bytes 1966088 | tf_op jit(solution)/shard_map/while/body/eval_jaxpr/ppermute | solution.py:25
  768.0 18.7 %collective-permute-start.3 = (bf16[256,1280]{0,1:T(8,128)(2,1)S(1)}, bf16[256,1280]{0,1:T(8,128)(2,1)}, u32[]{:S(2)}, u32[]{:S(2)}) collective-permute-start(bf16[256,1280]{0,1:T(8,128)(2,1)S(1)} %copy-done.12), channel_id=1, source_target_pairs={{0,2},{2,4},{4,6},{6,8},{8,10},{10,12},{12,14},{14,16},{16,18},{18... | collective-permute-start | bytes 1966088 | tf_op jit(solution)/shard_map/while/body/eval_jaxpr/ppermute | solution.py:25
  824.7 17.8 collective-permute-done.4
  875.0 17.1 collective-permute-done.4
  924.6 17.0 collective-permute-done.4
  958.2 10.7 collective-permute-start.2
  975.1 16.2 collective-permute-done.4
  1009.1 13.7 collective-permute-start.3
  1022.8 18.0 collective-permute-done.4
  1063.6 26.8 %collective-permute-done.4 = bf16[256,1280]{0,1:T(8,128)(2,1)} collective-permute-done((bf16[256,1280]{0,1:T(8,128)(2,1)}, bf16[256,1280]{0,1:T(8,128)(2,1)}, u32[]{:S(2)}, u32[]{:S(2)}) %collective-permute-start.4) | collective-permute-done | bytes 655392 | tf_op jit(solution)/shard_map/while/body/eval_jaxpr/ppermute | solution.py:19
  1111.3 28.7 %collective-permute-done.4 = bf16[256,1280]{0,1:T(8,128)(2,1)} collective-permute-done((bf16[256,1280]{0,1:T(8,128)(2,1)}, bf16[256,1280]{0,1:T(8,128)(2,1)}, u32[]{:S(2)}, u32[]{:S(2)}) %collective-permute-start.4) | collective-permute-done | bytes 655392 | tf_op jit(solution)/shard_map/while/body/eval_jaxpr/ppermute | solution.py:19
  1160.9 28.7 %collective-permute-done.4 = bf16[256,1280]{0,1:T(8,128)(2,1)} collective-permute-done((bf16[256,1280]{0,1:T(8,128)(2,1)}, bf16[256,1280]{0,1:T(8,128)(2,1)}, u32[]{:S(2)}, u32[]{:S(2)}) %collective-permute-start.4) | collective-permute-done | bytes 655392 | tf_op jit(solution)/shard_map/while/body/eval_jaxpr/ppermute | solution.py:19
  1211.4 27.8 %collective-permute-done.4 = bf16[256,1280]{0,1:T(8,128)(2,1)} collective-permute-done((bf16[256,1280]{0,1:T(8,128)(2,1)}, bf16[256,1280]{0,1:T(8,128)(2,1)}, u32[]{:S(2)}, u32[]{:S(2)}) %collective-permute-start.4) | collective-permute-done | bytes 655392 | tf_op jit(solution)/shard_map/while/body/eval_jaxpr/ppermute | solution.py:19
  1259.2 29.6 %collective-permute-done.4 = bf16[256,1280]{0,1:T(8,128)(2,1)} collective-permute-done((bf16[256,1280]{0,1:T(8,128)(2,1)}, bf16[256,1280]{0,1:T(8,128)(2,1)}, u32[]{:S(2)}, u32[]{:S(2)}) %collective-permute-start.4) | collective-permute-done | bytes 655392 | tf_op jit(solution)/shard_map/while/body/eval_jaxpr/ppermute | solution.py:19
  1320.7 34.2 %collective-permute-done.6 = bf16[256,1280]{0,1:T(8,128)(2,1)S(1)} collective-permute-done((bf16[256,1280]{0,1:T(8,128)(2,1)S(1)}, bf16[256,1280]{0,1:T(8,128)(2,1)S(1)}, u32[]{:S(2)}, u32[]{:S(2)}) %collective-permute-start.6) | collective-permute-done | bytes 655392 | tf_op jit(solution)/shard_map/ppermute | solution.py:19
  1360.0 13.6 collective-permute-done.7
  1384.1 47.7 %reduce-scatter.13.cloned.1.call-done = bf16[640,1280]{1,0:T(8,128)(2,1)} async-done(((bf16[1280,1280]{1,0:T(8,128)(2,1)}), bf16[640,1280]{1,0:T(8,128)(2,1)}) %reduce-scatter.13.cloned.1.call-update) | async-done | bytes 1638416 | tf_op jit(solution)/shard_map/reduce_scatter | solution.py:277
  1431.8 47.6 %reduce-scatter.15.cloned.1.call-done = bf16[640,1280]{1,0:T(8,128)(2,1)} async-done(((bf16[1280,1280]{1,0:T(8,128)(2,1)}), bf16[640,1280]{1,0:T(8,128)(2,1)}) %reduce-scatter.15.cloned.1.call-update) | async-done | bytes 1638416 | tf_op jit(solution)/shard_map/reduce_scatter | solution.py:280
  1479.4 47.6 %reduce-scatter.17.cloned.1.call-done = bf16[640,1280]{1,0:T(8,128)(2,1)} async-done(((bf16[1280,1280]{1,0:T(8,128)(2,1)}), bf16[640,1280]{1,0:T(8,128)(2,1)}) %reduce-scatter.17.cloned.1.call-update) | async-done | bytes 1638416 | tf_op jit(solution)/shard_map/reduce_scatter | solution.py:283
  1527.0 47.6 %reduce-scatter.9.cloned.1.call-done = bf16[640,1280]{1,0:T(8,128)(2,1)} async-done(((bf16[1280,1280]{1,0:T(8,128)(2,1)}), bf16[640,1280]{1,0:T(8,128)(2,1)}) %reduce-scatter.9.cloned.1.call-update) | async-done | bytes 1638416 | tf_op jit(solution)/shard_map/reduce_scatter | solution.py:271
  1574.7 47.6 %reduce-scatter.11.cloned.1.call-done = bf16[640,1280]{1,0:T(8,128)(2,1)} async-done(((bf16[1280,1280]{1,0:T(8,128)(2,1)}), bf16[640,1280]{1,0:T(8,128)(2,1)}) %reduce-scatter.11.cloned.1.call-update) | async-done | bytes 1638416 | tf_op jit(solution)/shard_map/reduce_scatter | solution.py:274
  1641.9 35.5 %all-reduce.3 = (bf16[640]{0:T(1024)(128)(2,1)S(1)}, bf16[640]{0:T(1024)(128)(2,1)S(1)}, bf16[80]{0:T(256)(128)(2,1)S(1)}) all-reduce(bf16[640]{0:T(1024)(128)(2,1)S(1)} %dynamic-slice.1, bf16[640]{0:T(1024)(128)(2,1)S(1)} %dynamic-slice.3, bf16[80]{0:T(256)(128)(2,1)S(1)} %dynamic-slice_bitcast_fusion), channel_id=1, replica_groups=mesh['ctx'=16,'fs'=2] {'ctx'}, use_global_device_ids=true, to_apply=%region_39.40 | all-reduce | flops 1360 | bytes 5440 | tf_op jit(solution)/shard_map/psum | solution.py:303
  1680.4 139.5 %all-reduce.8.cloned.1.call-done = (bf16[640,1280]{1,0:T(8,128)(2,1)}, bf16[640,1280]{1,0:T(8,128)(2,1)}, bf16[640,1280]{1,0:T(8,128)(2,1)}, bf16[640,1280]{1,0:...) async-done(((bf16[640,1280]{1,0:T(8,128)(2,1)}, bf16[640,1280]{1,0:T(8,128)(2,1)}, bf16[640,1280]{1,0:T(8,128)(2,1)}, bf16[640,1280]{1,0:T(8,128)(2,1)}, ...) | async-done | bytes 9830416 | tf_op jit(solution)/shard_map/psum | solution.py:297
  (755 shorter events, 651.7 us)
Async XLA Ops:
  7.2 51.5 %all-gather.9.cloned.1.call-start = ((), (), s32[]{:S(2)}) async-start(), calls=%async_computation.6 | async-start | bytes 4915200 | tf_op jit(solution)/shard_map/all_gather | solution.py:85
  7.9 98.8 %all-gather.11.cloned.1.call-start = ((), (), s32[]{:S(2)}) async-start(), calls=%async_computation.7 | async-start | bytes 4915200 | tf_op jit(solution)/shard_map/all_gather | solution.py:86
  8.7 146.0 %all-gather.13.cloned.1.call-start = ((), (), s32[]{:S(2)}) async-start(), calls=%async_computation.8 | async-start | bytes 4915200 | tf_op jit(solution)/shard_map/all_gather | solution.py:84
  9.4 497.0 %all-gather.15.cloned.1.call-start = ((), (), s32[]{:S(2)}) async-start(), calls=%async_computation.9 | async-start | bytes 4915200 | tf_op jit(solution)/shard_map/all_gather | solution.py:87
  10.0 500.5 %all-gather.17.cloned.1.call-start = ((), (), s32[]{:S(2)}) async-start(), calls=%async_computation.10 | async-start | bytes 4915200 | tf_op jit(solution)/shard_map/all_gather | solution.py:88
  10.6 502.9 %all-gather.19.cloned.1.call-start = ((), (), s32[]{:S(2)}) async-start(), calls=%async_computation.11 | async-start | bytes 4915200 | tf_op jit(solution)/shard_map/all_gather | solution.py:89
  11.2 1372.9 %reduce-scatter.7.cloned.1.call-start = ((), (), s32[]{:S(2)}) async-start(), calls=%async_computation.12 | async-start | bytes 4915200 | tf_op jit(solution)/shard_map/reduce_scatter | solution.py:268
  542.3 70.9 %collective-permute-start.4 = (bf16[256,1280]{0,1:T(8,128)(2,1)}, bf16[256,1280]{0,1:T(8,128)(2,1)}, u32[]{:S(2)}, u32[]{:S(2)}) collective-permute-start(bf16[256,1280]{0,1:T(8,128)(2,1)} %convert_element_type.469), channel_id=1, source_target_pairs={{30,0},{0,2},{2,4},{4,6},{6,8},{8,10},{10,12},{12,14},{14,16},{16,... | collective-permute-start | bytes 1966088 | tf_op jit(solution)/shard_map/while/body/eval_jaxpr/ppermute | solution.py:19
  556.5 63.7 %collective-permute-start.5 = (bf16[256,1280]{0,1:T(8,128)(2,1)}, bf16[256,1280]{0,1:T(8,128)(2,1)}, u32[]{:S(2)}, u32[]{:S(2)}) collective-permute-start(bf16[256,1280]{0,1:T(8,128)(2,1)} %convert_element_type.471), channel_id=1, source_target_pairs={{30,0},{0,2},{2,4},{4,6},{6,8},{8,10},{10,12},{12,14},{14,16},{16,... | collective-permute-start | bytes 1966088 | tf_op jit(solution)/shard_map/while/body/eval_jaxpr/ppermute | solution.py:19
  558.9 63.6 %collective-permute-start.2 = (bf16[256,1280]{0,1:T(8,128)(2,1)S(1)}, bf16[256,1280]{0,1:T(8,128)(2,1)S(1)}, u32[]{:S(2)}, u32[]{:S(2)}) collective-permute-start(bf16[256,1280]{0,1:T(8,128)(2,1)S(1)} %copy-done.1), channel_id=1, source_target_pairs={{0,2},{2,4},{4,6},{6,8},{8,10},{10,12},{12,14},{14,16},{16,18},{18... | collective-permute-start | bytes 1966088 | tf_op jit(solution)/shard_map/while/body/eval_jaxpr/ppermute | solution.py:25
  574.0 48.5 %collective-permute-start.3 = (bf16[256,1280]{0,1:T(8,128)(2,1)S(1)}, bf16[256,1280]{0,1:T(8,128)(2,1)}, u32[]{:S(2)}, u32[]{:S(2)}) collective-permute-start(bf16[256,1280]{0,1:T(8,128)(2,1)S(1)} %copy-done.12), channel_id=1, source_target_pairs={{0,2},{2,4},{4,6},{6,8},{8,10},{10,12},{12,14},{14,16},{16,18},{18... | collective-permute-start | bytes 1966088 | tf_op jit(solution)/shard_map/while/body/eval_jaxpr/ppermute | solution.py:25
  664.7 36.1 %collective-permute-start.5 = (bf16[256,1280]{0,1:T(8,128)(2,1)}, bf16[256,1280]{0,1:T(8,128)(2,1)}, u32[]{:S(2)}, u32[]{:S(2)}) collective-permute-start(bf16[256,1280]{0,1:T(8,128)(2,1)} %convert_element_type.471), channel_id=1, source_target_pairs={{30,0},{0,2},{2,4},{4,6},{6,8},{8,10},{10,12},{12,14},{14,16},{16,... | collective-permute-start | bytes 1966088 | tf_op jit(solution)/shard_map/while/body/eval_jaxpr/ppermute | solution.py:19
  709.9 40.5 %collective-permute-start.5 = (bf16[256,1280]{0,1:T(8,128)(2,1)}, bf16[256,1280]{0,1:T(8,128)(2,1)}, u32[]{:S(2)}, u32[]{:S(2)}) collective-permute-start(bf16[256,1280]{0,1:T(8,128)(2,1)} %convert_element_type.471), channel_id=1, source_target_pairs={{30,0},{0,2},{2,4},{4,6},{6,8},{8,10},{10,12},{12,14},{14,16},{16,... | collective-permute-start | bytes 1966088 | tf_op jit(solution)/shard_map/while/body/eval_jaxpr/ppermute | solution.py:19
  710.2 42.4 %collective-permute-start.2 = (bf16[256,1280]{0,1:T(8,128)(2,1)S(1)}, bf16[256,1280]{0,1:T(8,128)(2,1)S(1)}, u32[]{:S(2)}, u32[]{:S(2)}) collective-permute-start(bf16[256,1280]{0,1:T(8,128)(2,1)S(1)} %copy-done.1), channel_id=1, source_target_pairs={{0,2},{2,4},{4,6},{6,8},{8,10},{10,12},{12,14},{14,16},{16,18},{18... | collective-permute-start | bytes 1966088 | tf_op jit(solution)/shard_map/while/body/eval_jaxpr/ppermute | solution.py:25
  759.4 40.5 %collective-permute-start.5 = (bf16[256,1280]{0,1:T(8,128)(2,1)}, bf16[256,1280]{0,1:T(8,128)(2,1)}, u32[]{:S(2)}, u32[]{:S(2)}) collective-permute-start(bf16[256,1280]{0,1:T(8,128)(2,1)} %convert_element_type.471), channel_id=1, source_target_pairs={{30,0},{0,2},{2,4},{4,6},{6,8},{8,10},{10,12},{12,14},{14,16},{16,... | collective-permute-start | bytes 1966088 | tf_op jit(solution)/shard_map/while/body/eval_jaxpr/ppermute | solution.py:19
  759.8 42.5 %collective-permute-start.2 = (bf16[256,1280]{0,1:T(8,128)(2,1)S(1)}, bf16[256,1280]{0,1:T(8,128)(2,1)S(1)}, u32[]{:S(2)}, u32[]{:S(2)}) collective-permute-start(bf16[256,1280]{0,1:T(8,128)(2,1)S(1)} %copy-done.1), channel_id=1, source_target_pairs={{0,2},{2,4},{4,6},{6,8},{8,10},{10,12},{12,14},{14,16},{16,18},{18... | collective-permute-start | bytes 1966088 | tf_op jit(solution)/shard_map/while/body/eval_jaxpr/ppermute | solution.py:25
  809.0 40.5 %collective-permute-start.5 = (bf16[256,1280]{0,1:T(8,128)(2,1)}, bf16[256,1280]{0,1:T(8,128)(2,1)}, u32[]{:S(2)}, u32[]{:S(2)}) collective-permute-start(bf16[256,1280]{0,1:T(8,128)(2,1)} %convert_element_type.471), channel_id=1, source_target_pairs={{30,0},{0,2},{2,4},{4,6},{6,8},{8,10},{10,12},{12,14},{14,16},{16,... | collective-permute-start | bytes 1966088 | tf_op jit(solution)/shard_map/while/body/eval_jaxpr/ppermute | solution.py:19
  809.4 42.4 %collective-permute-start.2 = (bf16[256,1280]{0,1:T(8,128)(2,1)S(1)}, bf16[256,1280]{0,1:T(8,128)(2,1)S(1)}, u32[]{:S(2)}, u32[]{:S(2)}) collective-permute-start(bf16[256,1280]{0,1:T(8,128)(2,1)S(1)} %copy-done.1), channel_id=1, source_target_pairs={{0,2},{2,4},{4,6},{6,8},{8,10},{10,12},{12,14},{14,16},{16,18},{18... | collective-permute-start | bytes 1966088 | tf_op jit(solution)/shard_map/while/body/eval_jaxpr/ppermute | solution.py:25
  858.6 40.5 %collective-permute-start.5 = (bf16[256,1280]{0,1:T(8,128)(2,1)}, bf16[256,1280]{0,1:T(8,128)(2,1)}, u32[]{:S(2)}, u32[]{:S(2)}) collective-permute-start(bf16[256,1280]{0,1:T(8,128)(2,1)} %convert_element_type.471), channel_id=1, source_target_pairs={{30,0},{0,2},{2,4},{4,6},{6,8},{8,10},{10,12},{12,14},{14,16},{16,... | collective-permute-start | bytes 1966088 | tf_op jit(solution)/shard_map/while/body/eval_jaxpr/ppermute | solution.py:19
  859.0 42.4 %collective-permute-start.2 = (bf16[256,1280]{0,1:T(8,128)(2,1)S(1)}, bf16[256,1280]{0,1:T(8,128)(2,1)S(1)}, u32[]{:S(2)}, u32[]{:S(2)}) collective-permute-start(bf16[256,1280]{0,1:T(8,128)(2,1)S(1)} %copy-done.1), channel_id=1, source_target_pairs={{0,2},{2,4},{4,6},{6,8},{8,10},{10,12},{12,14},{14,16},{16,18},{18... | collective-permute-start | bytes 1966088 | tf_op jit(solution)/shard_map/while/body/eval_jaxpr/ppermute | solution.py:25
  908.2 40.5 %collective-permute-start.5 = (bf16[256,1280]{0,1:T(8,128)(2,1)}, bf16[256,1280]{0,1:T(8,128)(2,1)}, u32[]{:S(2)}, u32[]{:S(2)}) collective-permute-start(bf16[256,1280]{0,1:T(8,128)(2,1)} %convert_element_type.471), channel_id=1, source_target_pairs={{30,0},{0,2},{2,4},{4,6},{6,8},{8,10},{10,12},{12,14},{14,16},{16,... | collective-permute-start | bytes 1966088 | tf_op jit(solution)/shard_map/while/body/eval_jaxpr/ppermute | solution.py:19
  908.6 42.4 %collective-permute-start.2 = (bf16[256,1280]{0,1:T(8,128)(2,1)S(1)}, bf16[256,1280]{0,1:T(8,128)(2,1)S(1)}, u32[]{:S(2)}, u32[]{:S(2)}) collective-permute-start(bf16[256,1280]{0,1:T(8,128)(2,1)S(1)} %copy-done.1), channel_id=1, source_target_pairs={{0,2},{2,4},{4,6},{6,8},{8,10},{10,12},{12,14},{14,16},{16,18},{18... | collective-permute-start | bytes 1966088 | tf_op jit(solution)/shard_map/while/body/eval_jaxpr/ppermute | solution.py:25
  957.8 40.5 %collective-permute-start.5 = (bf16[256,1280]{0,1:T(8,128)(2,1)}, bf16[256,1280]{0,1:T(8,128)(2,1)}, u32[]{:S(2)}, u32[]{:S(2)}) collective-permute-start(bf16[256,1280]{0,1:T(8,128)(2,1)} %convert_element_type.471), channel_id=1, source_target_pairs={{30,0},{0,2},{2,4},{4,6},{6,8},{8,10},{10,12},{12,14},{14,16},{16,... | collective-permute-start | bytes 1966088 | tf_op jit(solution)/shard_map/while/body/eval_jaxpr/ppermute | solution.py:19
  958.2 42.5 %collective-permute-start.2 = (bf16[256,1280]{0,1:T(8,128)(2,1)S(1)}, bf16[256,1280]{0,1:T(8,128)(2,1)S(1)}, u32[]{:S(2)}, u32[]{:S(2)}) collective-permute-start(bf16[256,1280]{0,1:T(8,128)(2,1)S(1)} %copy-done.1), channel_id=1, source_target_pairs={{0,2},{2,4},{4,6},{6,8},{8,10},{10,12},{12,14},{14,16},{16,18},{18... | collective-permute-start | bytes 1966088 | tf_op jit(solution)/shard_map/while/body/eval_jaxpr/ppermute | solution.py:25
  1007.4 40.5 %collective-permute-start.5 = (bf16[256,1280]{0,1:T(8,128)(2,1)}, bf16[256,1280]{0,1:T(8,128)(2,1)}, u32[]{:S(2)}, u32[]{:S(2)}) collective-permute-start(bf16[256,1280]{0,1:T(8,128)(2,1)} %convert_element_type.471), channel_id=1, source_target_pairs={{30,0},{0,2},{2,4},{4,6},{6,8},{8,10},{10,12},{12,14},{14,16},{16,... | collective-permute-start | bytes 1966088 | tf_op jit(solution)/shard_map/while/body/eval_jaxpr/ppermute | solution.py:19
  1007.8 42.4 %collective-permute-start.2 = (bf16[256,1280]{0,1:T(8,128)(2,1)S(1)}, bf16[256,1280]{0,1:T(8,128)(2,1)S(1)}, u32[]{:S(2)}, u32[]{:S(2)}) collective-permute-start(bf16[256,1280]{0,1:T(8,128)(2,1)S(1)} %copy-done.1), channel_id=1, source_target_pairs={{0,2},{2,4},{4,6},{6,8},{8,10},{10,12},{12,14},{14,16},{16,18},{18... | collective-permute-start | bytes 1966088 | tf_op jit(solution)/shard_map/while/body/eval_jaxpr/ppermute | solution.py:25
  1009.1 41.1 %collective-permute-start.3 = (bf16[256,1280]{0,1:T(8,128)(2,1)S(1)}, bf16[256,1280]{0,1:T(8,128)(2,1)}, u32[]{:S(2)}, u32[]{:S(2)}) collective-permute-start(bf16[256,1280]{0,1:T(8,128)(2,1)S(1)} %copy-done.12), channel_id=1, source_target_pairs={{0,2},{2,4},{4,6},{6,8},{8,10},{10,12},{12,14},{14,16},{16,18},{18... | collective-permute-start | bytes 1966088 | tf_op jit(solution)/shard_map/while/body/eval_jaxpr/ppermute | solution.py:25
  1057.0 40.5 %collective-permute-start.5 = (bf16[256,1280]{0,1:T(8,128)(2,1)}, bf16[256,1280]{0,1:T(8,128)(2,1)}, u32[]{:S(2)}, u32[]{:S(2)}) collective-permute-start(bf16[256,1280]{0,1:T(8,128)(2,1)} %convert_element_type.471), channel_id=1, source_target_pairs={{30,0},{0,2},{2,4},{4,6},{6,8},{8,10},{10,12},{12,14},{14,16},{16,... | collective-permute-start | bytes 1966088 | tf_op jit(solution)/shard_map/while/body/eval_jaxpr/ppermute | solution.py:19
  1057.3 42.5 %collective-permute-start.2 = (bf16[256,1280]{0,1:T(8,128)(2,1)S(1)}, bf16[256,1280]{0,1:T(8,128)(2,1)S(1)}, u32[]{:S(2)}, u32[]{:S(2)}) collective-permute-start(bf16[256,1280]{0,1:T(8,128)(2,1)S(1)} %copy-done.1), channel_id=1, source_target_pairs={{0,2},{2,4},{4,6},{6,8},{8,10},{10,12},{12,14},{14,16},{16,18},{18... | collective-permute-start | bytes 1966088 | tf_op jit(solution)/shard_map/while/body/eval_jaxpr/ppermute | solution.py:25
  1058.7 41.1 %collective-permute-start.3 = (bf16[256,1280]{0,1:T(8,128)(2,1)S(1)}, bf16[256,1280]{0,1:T(8,128)(2,1)}, u32[]{:S(2)}, u32[]{:S(2)}) collective-permute-start(bf16[256,1280]{0,1:T(8,128)(2,1)S(1)} %copy-done.12), channel_id=1, source_target_pairs={{0,2},{2,4},{4,6},{6,8},{8,10},{10,12},{12,14},{14,16},{16,18},{18... | collective-permute-start | bytes 1966088 | tf_op jit(solution)/shard_map/while/body/eval_jaxpr/ppermute | solution.py:25
  1106.6 40.5 %collective-permute-start.5 = (bf16[256,1280]{0,1:T(8,128)(2,1)}, bf16[256,1280]{0,1:T(8,128)(2,1)}, u32[]{:S(2)}, u32[]{:S(2)}) collective-permute-start(bf16[256,1280]{0,1:T(8,128)(2,1)} %convert_element_type.471), channel_id=1, source_target_pairs={{30,0},{0,2},{2,4},{4,6},{6,8},{8,10},{10,12},{12,14},{14,16},{16,... | collective-permute-start | bytes 1966088 | tf_op jit(solution)/shard_map/while/body/eval_jaxpr/ppermute | solution.py:19
  1106.9 42.4 %collective-permute-start.2 = (bf16[256,1280]{0,1:T(8,128)(2,1)S(1)}, bf16[256,1280]{0,1:T(8,128)(2,1)S(1)}, u32[]{:S(2)}, u32[]{:S(2)}) collective-permute-start(bf16[256,1280]{0,1:T(8,128)(2,1)S(1)} %copy-done.1), channel_id=1, source_target_pairs={{0,2},{2,4},{4,6},{6,8},{8,10},{10,12},{12,14},{14,16},{16,18},{18... | collective-permute-start | bytes 1966088 | tf_op jit(solution)/shard_map/while/body/eval_jaxpr/ppermute | solution.py:25
  1108.3 41.1 %collective-permute-start.3 = (bf16[256,1280]{0,1:T(8,128)(2,1)S(1)}, bf16[256,1280]{0,1:T(8,128)(2,1)}, u32[]{:S(2)}, u32[]{:S(2)}) collective-permute-start(bf16[256,1280]{0,1:T(8,128)(2,1)S(1)} %copy-done.12), channel_id=1, source_target_pairs={{0,2},{2,4},{4,6},{6,8},{8,10},{10,12},{12,14},{14,16},{16,18},{18... | collective-permute-start | bytes 1966088 | tf_op jit(solution)/shard_map/while/body/eval_jaxpr/ppermute | solution.py:25
  1156.1 40.5 %collective-permute-start.5 = (bf16[256,1280]{0,1:T(8,128)(2,1)}, bf16[256,1280]{0,1:T(8,128)(2,1)}, u32[]{:S(2)}, u32[]{:S(2)}) collective-permute-start(bf16[256,1280]{0,1:T(8,128)(2,1)} %convert_element_type.471), channel_id=1, source_target_pairs={{30,0},{0,2},{2,4},{4,6},{6,8},{8,10},{10,12},{12,14},{14,16},{16,... | collective-permute-start | bytes 1966088 | tf_op jit(solution)/shard_map/while/body/eval_jaxpr/ppermute | solution.py:19
  1156.5 42.5 %collective-permute-start.2 = (bf16[256,1280]{0,1:T(8,128)(2,1)S(1)}, bf16[256,1280]{0,1:T(8,128)(2,1)S(1)}, u32[]{:S(2)}, u32[]{:S(2)}) collective-permute-start(bf16[256,1280]{0,1:T(8,128)(2,1)S(1)} %copy-done.1), channel_id=1, source_target_pairs={{0,2},{2,4},{4,6},{6,8},{8,10},{10,12},{12,14},{14,16},{16,18},{18... | collective-permute-start | bytes 1966088 | tf_op jit(solution)/shard_map/while/body/eval_jaxpr/ppermute | solution.py:25
  1157.9 41.1 %collective-permute-start.3 = (bf16[256,1280]{0,1:T(8,128)(2,1)S(1)}, bf16[256,1280]{0,1:T(8,128)(2,1)}, u32[]{:S(2)}, u32[]{:S(2)}) collective-permute-start(bf16[256,1280]{0,1:T(8,128)(2,1)S(1)} %copy-done.12), channel_id=1, source_target_pairs={{0,2},{2,4},{4,6},{6,8},{8,10},{10,12},{12,14},{14,16},{16,18},{18... | collective-permute-start | bytes 1966088 | tf_op jit(solution)/shard_map/while/body/eval_jaxpr/ppermute | solution.py:25
  1205.7 40.5 %collective-permute-start.5 = (bf16[256,1280]{0,1:T(8,128)(2,1)}, bf16[256,1280]{0,1:T(8,128)(2,1)}, u32[]{:S(2)}, u32[]{:S(2)}) collective-permute-start(bf16[256,1280]{0,1:T(8,128)(2,1)} %convert_element_type.471), channel_id=1, source_target_pairs={{30,0},{0,2},{2,4},{4,6},{6,8},{8,10},{10,12},{12,14},{14,16},{16,... | collective-permute-start | bytes 1966088 | tf_op jit(solution)/shard_map/while/body/eval_jaxpr/ppermute | solution.py:19
  1206.1 42.4 %collective-permute-start.2 = (bf16[256,1280]{0,1:T(8,128)(2,1)S(1)}, bf16[256,1280]{0,1:T(8,128)(2,1)S(1)}, u32[]{:S(2)}, u32[]{:S(2)}) collective-permute-start(bf16[256,1280]{0,1:T(8,128)(2,1)S(1)} %copy-done.1), channel_id=1, source_target_pairs={{0,2},{2,4},{4,6},{6,8},{8,10},{10,12},{12,14},{14,16},{16,18},{18... | collective-permute-start | bytes 1966088 | tf_op jit(solution)/shard_map/while/body/eval_jaxpr/ppermute | solution.py:25
  1207.5 41.1 %collective-permute-start.3 = (bf16[256,1280]{0,1:T(8,128)(2,1)S(1)}, bf16[256,1280]{0,1:T(8,128)(2,1)}, u32[]{:S(2)}, u32[]{:S(2)}) collective-permute-start(bf16[256,1280]{0,1:T(8,128)(2,1)S(1)} %copy-done.12), channel_id=1, source_target_pairs={{0,2},{2,4},{4,6},{6,8},{8,10},{10,12},{12,14},{14,16},{16,18},{18... | collective-permute-start | bytes 1966088 | tf_op jit(solution)/shard_map/while/body/eval_jaxpr/ppermute | solution.py:25
  1255.3 40.5 %collective-permute-start.5 = (bf16[256,1280]{0,1:T(8,128)(2,1)}, bf16[256,1280]{0,1:T(8,128)(2,1)}, u32[]{:S(2)}, u32[]{:S(2)}) collective-permute-start(bf16[256,1280]{0,1:T(8,128)(2,1)} %convert_element_type.471), channel_id=1, source_target_pairs={{30,0},{0,2},{2,4},{4,6},{6,8},{8,10},{10,12},{12,14},{14,16},{16,... | collective-permute-start | bytes 1966088 | tf_op jit(solution)/shard_map/while/body/eval_jaxpr/ppermute | solution.py:19
  1255.7 42.5 %collective-permute-start.2 = (bf16[256,1280]{0,1:T(8,128)(2,1)S(1)}, bf16[256,1280]{0,1:T(8,128)(2,1)S(1)}, u32[]{:S(2)}, u32[]{:S(2)}) collective-permute-start(bf16[256,1280]{0,1:T(8,128)(2,1)S(1)} %copy-done.1), channel_id=1, source_target_pairs={{0,2},{2,4},{4,6},{6,8},{8,10},{10,12},{12,14},{14,16},{16,18},{18... | collective-permute-start | bytes 1966088 | tf_op jit(solution)/shard_map/while/body/eval_jaxpr/ppermute | solution.py:25
  1257.0 41.1 %collective-permute-start.3 = (bf16[256,1280]{0,1:T(8,128)(2,1)S(1)}, bf16[256,1280]{0,1:T(8,128)(2,1)}, u32[]{:S(2)}, u32[]{:S(2)}) collective-permute-start(bf16[256,1280]{0,1:T(8,128)(2,1)S(1)} %copy-done.12), channel_id=1, source_target_pairs={{0,2},{2,4},{4,6},{6,8},{8,10},{10,12},{12,14},{14,16},{16,18},{18... | collective-permute-start | bytes 1966088 | tf_op jit(solution)/shard_map/while/body/eval_jaxpr/ppermute | solution.py:25
  1305.5 126.3 %reduce-scatter.13.cloned.1.call-start = ((), (), s32[]{:S(2)}) async-start(), calls=%async_computation.15 | async-start | bytes 4915200 | tf_op jit(solution)/shard_map/reduce_scatter | solution.py:277
  1309.5 170.0 %reduce-scatter.15.cloned.1.call-start = ((), (), s32[]{:S(2)}) async-start(), calls=%async_computation.16 | async-start | bytes 4915200 | tf_op jit(solution)/shard_map/reduce_scatter | solution.py:280
  1313.8 213.2 %reduce-scatter.17.cloned.1.call-start = ((), (), s32[]{:S(2)}) async-start(), calls=%async_computation.17 | async-start | bytes 4915200 | tf_op jit(solution)/shard_map/reduce_scatter | solution.py:283
  1319.3 255.4 %reduce-scatter.9.cloned.1.call-start = ((), (), s32[]{:S(2)}) async-start(), calls=%async_computation.13 | async-start | bytes 4915200 | tf_op jit(solution)/shard_map/reduce_scatter | solution.py:271
  1358.6 263.6 %reduce-scatter.11.cloned.1.call-start = ((), (), s32[]{:S(2)}) async-start(), calls=%async_computation.14 | async-start | bytes 4915200 | tf_op jit(solution)/shard_map/reduce_scatter | solution.py:274
  1377.4 442.5 %all-reduce.8.cloned.1.call-start = ((), (), s32[]{:S(2)}) async-start(), calls=%async_computation.18 | async-start | bytes 19660800 | tf_op jit(solution)/shard_map/psum | solution.py:297
  (167 other events, 1926.1 us)
Sparse Core Ops, SparseCore 0:
  9.6 49.0 all-gather.8
  60.2 46.4 all-gather.10
  108.2 46.3 all-gather.12
  156.1 46.4 all-gather.14
  203.9 46.3 all-gather.16
  251.8 46.4 all-gather.18
  1305.6 78.4 reduce-scatter.6
  1387.0 44.7 reduce-scatter.12
  1434.6 44.7 reduce-scatter.14
  1482.2 44.7 reduce-scatter.16
  1529.8 44.7 reduce-scatter.8
  1577.4 44.7 reduce-scatter.10
  1626.6 193.2 all-reduce.7
where the time goes:
time: 1850 us; the launch traced here: 1840 us
  waiting for transfers between devices  955 us (52%)
  starting transfers between devices  515 us (28%)
  other arithmetic  153 us (8%)
  local copies, waits for them, and re-layouts  86.4 us (5%)
  matrix products  63.5 us (3%)
  blocking collectives  50.2 us (3%)
    ppermute x60, starting transfers between devices, shifted(): lax.ppermute(value, axis, [(source, source + steps) for source in range(l...  493 us
    ppermute x32, waiting for transfers between devices, passed_along(): return lax.ppermute(block, axis, route)  416 us
    psum x1, waiting for transfers between devices, local(): lax.psum(shares[0].astype(jnp.bfloat16), 'ctx').astype(jnp.float32)  140 us
    while x180, local copies, waits for them, and re-layouts  60.8 us
    reduce_scatter x1, waiting for transfers between devices, local(): lax.psum_scatter(grad_outw.astype(jnp.bfloat16), 'fs', scatter_dimension=...  47.7 us
    reduce_scatter x1, waiting for transfers between devices, local(): lax.psum_scatter(grad_kw.astype(jnp.bfloat16), 'fs', scatter_dimension=0,...  47.6 us
    reduce_scatter x1, waiting for transfers between devices, local(): lax.psum_scatter(grad_inner.astype(jnp.bfloat16), 'fs', scatter_dimension...  47.6 us
    reduce_scatter x1, waiting for transfers between devices, local(): lax.psum_scatter(grad_vw.astype(jnp.bfloat16), 'fs', scatter_dimension=0,...  47.6 us
  transfers between devices with their start and end apart: 105, of which 57 were waited for; matrix products, arithmetic and copies ran while one was open for 9% of the time, Pallas kernels for 0%

commit v1 on v0

--- a/solution.py
+++ b/solution.py
@@ -1,8 +1,11 @@
+import functools
 import math
 
 import jax
 import jax.numpy as jnp
 from jax import lax
+from jax.experimental import pallas as pl
+from jax.experimental.pallas import tpu as pltpu
 from jax.sharding import PartitionSpec as P
 
 H = 16
@@ -53,7 +56,7 @@
     )
 
 
-def local(
+def general_local(
     tokens,
     query_weight,
     key_weight,
@@ -319,6 +322,589 @@
     )
 
 
+MESH = pl.DeviceIdType.MESH
+ANY = pl.BlockSpec(memory_space=pl.ANY)
+VMEM = pl.BlockSpec(memory_space=pltpu.VMEM)
+BF = jnp.bfloat16
+F32 = jnp.float32
+
+
+def fast_fits(mesh):
+    return mesh.shape["ctx"] == H and mesh.shape["fs"] == 2
+
+
+def remote(src, dst, ssem, rsem, target):
+    return pltpu.make_async_remote_copy(
+        src_ref=src, dst_ref=dst, send_sem=ssem, recv_sem=rsem, device_id=target, device_id_type=MESH
+    )
+
+
+def signal(target):
+    pl.semaphore_signal(
+        pltpu.get_barrier_semaphore(), inc=1, device_id=target, device_id_type=MESH
+    )
+
+
+def place():
+    me = lax.axis_index("ctx")
+    return me, lax.axis_index("fs"), me // 4, lax.rem(me // 2, 2), lax.rem(me, 2)
+
+
+def dot(a, b, dims=((1,), (0,))):
+    return lax.dot_general(a, b, (dims, ((), ())), preferred_element_type=F32)
+
+
+NT = ((1,), (1,))
+TN = ((0,), (0,))
+
+
+def weight_pull(own, other, k, fs, me, ssem, rsem):
+    half = own[0].shape[0] // 2
+    rows = pl.ds(pl.multiple_of(k * half, 64), half)
+    yn = (me, 1 - fs)
+    sib = (me + 1 - 2 * k, fs)
+    n = len(own)
+    first = [remote(own[i].at[rows], other[i].at[rows], ssem.at[i], rsem.at[i], yn) for i in range(n)]
+    second = [
+        remote(other[i].at[rows], other[i].at[rows], ssem.at[n + i], rsem.at[n + i], sib)
+        for i in range(n)
+    ]
+    return first, second
+
+
+def gather_kernel(n_w, tok_ref, gain_ref, wt_ref, *rest):
+    own = rest[:n_w]
+    h_all, wt_all, gain_full = rest[n_w : n_w + 3]
+    other = rest[n_w + 3 : 2 * n_w + 3]
+    h_own, gain_other, gain_own, ssem, rsem, wssem, wrsem, ysem, lsem = rest[2 * n_w + 3 :]
+    me, fs, z, x, k = place()
+    sib, xn, yn = (me + 1 - 2 * k, fs), (me + 2 - 4 * x, fs), (me, 1 - fs)
+    up, dn = (me + 4, fs), (me - 4, fs)
+    bar = pltpu.get_barrier_semaphore()
+    signal(sib)
+    signal(xn)
+    signal(yn)
+
+    @pl.when(z < 3)
+    def _():
+        signal(up)
+
+    @pl.when(z > 0)
+    def _():
+        signal(dn)
+
+    gain_own[...] = gain_ref[...]
+    rows = tok_ref[...].astype(F32)
+    normed = rows * lax.rsqrt(jnp.mean(rows * rows, axis=-1, keepdims=True) + epsilon)
+    pl.semaphore_wait(bar, 3 + (z + 2) // 3 + (5 - z) // 3)
+
+    gain_copy = remote(gain_own, gain_other, ysem.at[0], ysem.at[1], yn)
+    gain_copy.start()
+    half = wt_ref.shape[1]
+    columns = pl.ds(pl.multiple_of(fs * half, 128), half)
+    wt_copy = remote(wt_ref, wt_all.at[:, columns], ysem.at[2], ysem.at[3], yn)
+    wt_copy.start()
+    wt_here = pltpu.make_async_copy(wt_ref, wt_all.at[:, columns], lsem.at[0])
+    wt_here.start()
+    first, second = weight_pull(own, other, k, fs, me, wssem, wrsem)
+    gain_copy.wait()
+    for c in first:
+        c.start()
+    g_here = gain_own[...].astype(F32)
+    g_there = gain_other[...].astype(F32)
+    gains = jnp.where(
+        fs == 0,
+        jnp.concatenate([g_here, g_there], axis=1),
+        jnp.concatenate([g_there, g_here], axis=1),
+    )
+    gain_full[...] = gains
+    h_own[...] = (normed * gains[0:1]).astype(BF)
+
+    def cp(slot, t, si, mine=False):
+        return remote(h_own if mine else h_all.at[slot], h_all.at[slot], ssem.at[si], rsem.at[slot], t)
+
+    here = pltpu.make_async_copy(h_own, h_all.at[me], lsem.at[1])
+    cp(me, xn, 0, True).start()
+
+    @pl.when(z < 3)
+    def _():
+        cp(me, up, 1, True).start()
+
+    @pl.when(z > 0)
+    def _():
+        cp(me, dn, 2, True).start()
+
+    cp(me, sib, 3, True).start()
+    here.start()
+    for d in range(1, 4):
+        a = 4 + (d - 1) * 6
+
+        @pl.when(z >= d)
+        def _(a=a, d=d):
+            s = me - 4 * d
+            cp(s, dn, a).wait_recv()
+
+            @pl.when(z < 3)
+            def _():
+                cp(s, up, a).start()
+
+            cp(s, xn, a + 1).start()
+            cp(s, sib, a + 2).start()
+
+        @pl.when(z + d <= 3)
+        def _(a=a, d=d):
+            s = me + 4 * d
+            cp(s, up, a + 3).wait_recv()
+
+            @pl.when(z > 0)
+            def _():
+                cp(s, dn, a + 3).start()
+
+            cp(s, xn, a + 4).start()
+            cp(s, sib, a + 5).start()
+
+        if d <= n_w:
+            first[d - 1].wait_recv()
+            second[d - 1].start()
+
+    xo = me + 2 - 4 * x
+    for zz in range(4):
+        s = xo + 4 * (zz - z)
+        cp(s, xn, 22 + zz).wait_recv()
+        cp(s, sib, 22 + zz).start()
+    for i in range(3, n_w):
+        first[i].wait_recv()
+        second[i].start()
+    for zz in range(4):
+        for xx in range(2):
+            cp(zz * 4 + xx * 2 + 1 - k, sib, 0).wait_recv()
+    cp(me, xn, 0, True).wait_send()
+
+    @pl.when(z < 3)
+    def _():
+        cp(me, up, 1, True).wait_send()
+
+    @pl.when(z > 0)
+    def _():
+        cp(me, dn, 2, True).wait_send()
+
+    cp(me, sib, 3, True).wait_send()
+    for d in range(1, 4):
+        a = 4 + (d - 1) * 6
+
+        @pl.when(z >= d)
+        def _(a=a, d=d):
+            s = me - 4 * d
+
+            @pl.when(z < 3)
+            def _():
+                cp(s, up, a).wait_send()
+
+            cp(s, xn, a + 1).wait_send()
+            cp(s, sib, a + 2).wait_send()
+
+        @pl.when(z + d <= 3)
+        def _(a=a, d=d):
+            s = me + 4 * d
+
+            @pl.when(z > 0)
+            def _():
+                cp(s, dn, a + 3).wait_send()
+
+            cp(s, xn, a + 4).wait_send()
+            cp(s, sib, a + 5).wait_send()
+
+    for zz in range(4):
+        cp(xo + 4 * (zz - z), sib, 22 + zz).wait_send()
+    wt_copy.wait()
+    wt_here.wait()
+    here.wait()
+    for i in range(n_w):
+        first[i].wait_send()
+        second[i].wait()
+
+
+def gather_call(tok, gains, wt, weights):
+    n_w = len(weights)
+    rows, width = tok.shape
+    shapes = [
+        jax.ShapeDtypeStruct((H, rows, width), BF),
+        jax.ShapeDtypeStruct((wt.shape[0], 2 * wt.shape[1]), BF),
+        jax.ShapeDtypeStruct((gains.shape[0], 2 * gains.shape[1]), F32),
+    ] + [jax.ShapeDtypeStruct(w.shape, BF) for w in weights]
+    return pl.pallas_call(
+        functools.partial(gather_kernel, n_w),
+        out_shape=shapes,
+        in_specs=[VMEM, VMEM, ANY] + [ANY] * n_w,
+        out_specs=[ANY, ANY, VMEM] + [ANY] * n_w,
+        scratch_shapes=[
+            pltpu.VMEM((rows, width), BF),
+            pltpu.VMEM(gains.shape, BF),
+            pltpu.VMEM(gains.shape, BF),
+            pltpu.SemaphoreType.DMA((26,)),
+            pltpu.SemaphoreType.DMA((H,)),
+            pltpu.SemaphoreType.DMA((2 * n_w,)),
+            pltpu.SemaphoreType.DMA((2 * n_w,)),
+            pltpu.SemaphoreType.DMA((4,)),
+            pltpu.SemaphoreType.DMA((2,)),
+        ],
+        compiler_params=pltpu.CompilerParams(
+            collective_id=1, has_side_effects=True, vmem_limit_bytes=32 * 2**20
+        ),
+        name="gather_hidden",
+    )(tok, gains, wt, *weights)
+
+
+def swap_kernel(n_w, has_y, *refs):
+    x_ref = refs[0]
+    own = refs[1 : 1 + n_w]
+    y_ref = refs[1 + n_w : 1 + n_w + has_y]
+    at = 1 + n_w + has_y
+    o_ref = refs[at]
+    other = refs[at + 1 : at + 1 + n_w]
+    y_out = refs[at + 1 + n_w : at + 1 + n_w + has_y]
+    ssem, rsem, wssem, wrsem, lsem = refs[at + 1 + n_w + has_y :]
+    me, fs, z, x, k = place()
+    bar = pltpu.get_barrier_semaphore()
+    for i in range(1, H):
+        signal((lax.rem(me + i, H), fs))
+    if n_w or has_y:
+        signal((me, 1 - fs))
+    pl.semaphore_wait(bar, H - 1 + (1 if n_w or has_y else 0))
+    copies = []
+    for i in range(1, H):
+        t = lax.rem(me + i, H)
+        c = remote(x_ref.at[t], o_ref.at[me], ssem.at[i], rsem.at[i], (t, fs))
+        c.start()
+        copies.append(c)
+    here = pltpu.make_async_copy(x_ref.at[me], o_ref.at[me], lsem)
+    here.start()
+    if has_y:
+        c = remote(y_ref[0], y_out[0], ssem.at[0], rsem.at[0], (me, 1 - fs))
+        c.start()
+        copies.append(c)
+    if n_w:
+        first, second = weight_pull(own, other, k, fs, me, wssem, wrsem)
+        for c in first:
+            c.start()
+        for i in range(n_w):
+            first[i].wait_recv()
+            second[i].start()
+        for i in range(n_w):
+            first[i].wait_send()
+            second[i].wait()
+    for c in copies:
+        c.wait()
+    here.wait()
+
+
+def swap_call(cid, x, weights=(), y=None):
+    n_w, has_y = len(weights), int(y is not None)
+    args = [x, *weights] + ([y] if has_y else [])
+    out = pl.pallas_call(
+        functools.partial(swap_kernel, n_w, has_y),
+        out_shape=[jax.ShapeDtypeStruct(a.shape, a.dtype) for a in args],
+        in_specs=[ANY] * len(args),
+        out_specs=[ANY] * len(args),
+        scratch_shapes=[
+            pltpu.SemaphoreType.DMA((H,)),
+            pltpu.SemaphoreType.DMA((H,)),
+            pltpu.SemaphoreType.DMA((max(1, 2 * n_w),)),
+            pltpu.SemaphoreType.DMA((max(1, 2 * n_w),)),
+            pltpu.SemaphoreType.DMA,
+        ],
+        compiler_params=pltpu.CompilerParams(collective_id=cid, has_side_effects=True),
+        name="swap%d" % cid,
+    )(*args)
+    return out
+
+
+def visible(j, i, rows, first_key):
+    kpos = j * rows + lax.broadcasted_iota(jnp.int32, (rows, rows), 0)
+    qpos = i * rows + lax.broadcasted_iota(jnp.int32, (rows, rows), 1)
+    return (kpos <= qpos) & (kpos >= first_key)
+
+
+def attend_kernel(
+    h_ref, wt_ref, scale_ref, first_ref,
+    o_ref, o32_ref, lse_ref, qt_ref, q_ref, kt_ref, k_ref, v_ref, raw_ref,
+    k_sc, vt_sc,
+):
+    i = pl.program_id(0)
+    last = pl.num_programs(0) - 1
+    rows = h_ref.shape[1]
+    qkv = dot(wt_ref[...], h_ref[0], NT)
+    raw = qkv[:HD]
+    raw_ref[0] = raw
+    q32 = raw * scale_ref[...]
+    qt = q32.astype(BF)
+    qt_ref[0] = qt
+    q_ref[0] = q32.T.astype(BF)
+    kt32 = qkv[HD : 2 * HD]
+    vt32 = qkv[2 * HD :]
+    kt_ref[0] = kt32.astype(BF)
+    key = kt32.T.astype(BF)
+    k_ref[0] = key
+    v_ref[0] = vt32.T.astype(BF)
+    k_sc[i] = key
+    vt_sc[i] = vt32.astype(BF)
+    first_key = first_ref[0]
+
+    def tile(masked, j, carry):
+        run_max, run_sum, acc = carry
+        s = dot(k_sc[j], qt)
+        if masked:
+            s = jnp.where(visible(j, i, rows, first_key), s, neg_big)
+        new_max = jnp.maximum(run_max, jnp.max(s, axis=0, keepdims=True))
+        p = jnp.exp(s - new_max)
+        factor = jnp.exp(run_max - new_max)
+        run_sum = run_sum * factor + jnp.sum(p, axis=0, keepdims=True)
+        acc = acc * factor + dot(vt_sc[j], p.astype(BF))
+        return new_max, run_sum, acc
+
+    carry = (
+        jnp.full((1, rows), neg_big, F32),
+        jnp.zeros((1, rows), F32),
+        jnp.zeros((HD, rows), F32),
+    )
+    carry = tile(True, i, carry)
+    edge = (i == last) | (i == 0)
+    carry = lax.fori_loop(1, jnp.where(edge, 1, i), functools.partial(tile, False), carry)
+    carry = lax.fori_loop(
+        jnp.where(edge, 1, i), i, functools.partial(tile, True), carry
+    )
+    carry = lax.fori_loop(0, jnp.minimum(i, 1), functools.partial(tile, True), carry)
+    run_max, run_sum, acc = carry
+    out = acc / run_sum
+    o32_ref[0] = out
+    o_ref[0] = out.astype(BF)
+    lse_ref[0] = run_max + jnp.log(run_sum)
+
+
+def attend_call(h_all, wt, scale_col, first_key):
+    n, rows, width = h_all.shape
+
+    def blk(*shape):
+        return pl.BlockSpec((1, *shape), lambda i: (i, 0, 0))
+
+    def whole(a):
+        return pl.BlockSpec(a.shape, lambda i: (0,) * a.ndim)
+
+    def out(dtype, *shape):
+        return jax.ShapeDtypeStruct((n, *shape), dtype)
+
+    return pl.pallas_call(
+        attend_kernel,
+        grid=(n,),
+        out_shape=[
+            out(BF, HD, rows), out(F32, HD, rows), out(F32, 1, rows), out(BF, HD, rows),
+            out(BF, rows, HD), out(BF, HD, rows), out(BF, rows, HD), out(BF, rows, HD),
+            out(F32, HD, rows),
+        ],
+        in_specs=[blk(rows, width), whole(wt), whole(scale_col), blk(1, rows)],
+        out_specs=[
+            blk(HD, rows), blk(HD, rows), blk(1, rows), blk(HD, rows), blk(rows, HD),
+            blk(HD, rows), blk(rows, HD), blk(rows, HD), blk(HD, rows),
+        ],
+        scratch_shapes=[pltpu.VMEM((n, rows, HD), BF), pltpu.VMEM((n, HD, rows), BF)],
+        compiler_params=pltpu.CompilerParams(vmem_limit_bytes=48 * 2**20),
+        name="attend",
+    )(h_all, wt, scale_col, first_key)
+
+
+def attend_back_kernel(
+    h_ref, scale_ref, first_ref, k_ref, v_ref, kt_ref, raw_ref, q_ref, qt_ref, gt_ref, o_ref, lse_ref,
+    d_ref, dw_ref, ds_ref,
+    g_sc, delta_sc, dq_sc, scale_sc,
+):
+    j = pl.program_id(0)
+    last = pl.num_programs(0) - 1
+    rows = h_ref.shape[1]
+
+    @pl.when(j == 0)
+    def _():
+        def prepare(i, c):
+            g = gt_ref[i].astype(F32)
+            g_sc[i] = g.T.astype(BF)
+            delta_sc[i] = jnp.sum(g * o_ref[i], axis=0, keepdims=True)
+            dq_sc[i] = jnp.zeros((HD, rows), F32)
+            return c
+
+        lax.fori_loop(0, last + 1, prepare, 0)
+        scale_sc[...] = jnp.zeros_like(scale_sc)
+        dw_ref[...] = jnp.zeros_like(dw_ref)
+
+    key, value, kt = k_ref[0], v_ref[0], kt_ref[0]
+
+    def tile(masked, i, carry):
+        dk, dv = carry
+        s = dot(key, qt_ref[i])
+        if masked:
+            s = jnp.where(visible(j, i, rows, first_ref[i]), s, neg_big)
+        p = jnp.exp(s - lse_ref[i])
+        dv = dv + dot(p.astype(BF), g_sc[i])
+        dp = dot(value, gt_ref[i])
+        ds = (p * (dp - delta_sc[i])).astype(BF)
+        dk = dk + dot(ds, q_ref[i])
+        dq_sc[i] += dot(kt, ds)
+        return dk, dv
+
+    carry = (jnp.zeros((rows, HD), F32), jnp.zeros((rows, HD), F32))
+    carry = tile(True, j, carry)
+    inner_end = jnp.where(j == 0, 1, last)
+    carry = lax.fori_loop(j + 1, inner_end, functools.partial(tile, False), carry)
+    carry = lax.fori_loop(
+        jnp.maximum(j + 1, inner_end), last + 1, functools.partial(tile, True), carry
+    )
+    dk, dv = carry
+    dq = dq_sc[j]
+    scale_sc[...] += dq * raw_ref[0]
+    grads = jnp.concatenate([dq * scale_ref[...], dk.T, dv.T], axis=0).astype(BF)
+    d_ref[0] = grads
+    dw_ref[...] += dot(grads, h_ref[0])
+
+    @pl.when(j == last)
+    def _():
+        ds_ref[...] = jnp.sum(scale_sc[...], axis=1, keepdims=True)
+
+
+def attend_back_call(h_all, scale_col, first_key, k, v, kt, raw, q, qt, gt, o32, lse):
+    n, rows, width = h_all.shape
+
+    def blk(*shape):
+        return pl.BlockSpec((1, *shape), lambda i: (i, 0, 0))
+
+    def whole(a):
+        return pl.BlockSpec(a.shape, lambda i: (0,) * a.ndim)
+
+    return pl.pallas_call(
+        attend_back_kernel,
+        grid=(n,),
+        out_shape=[
+            jax.ShapeDtypeStruct((n, 3 * HD, rows), BF),
+            jax.ShapeDtypeStruct((3 * HD, width), F32),
+            jax.ShapeDtypeStruct((HD, 1), F32),
+        ],
+        in_specs=[
+            blk(rows, width), whole(scale_col), whole(first_key), blk(rows, HD), blk(rows, HD),
+            blk(HD, rows), blk(HD, rows), whole(q), whole(qt), whole(gt), whole(o32), whole(lse),
+        ],
+        out_specs=[
+            blk(3 * HD, rows),
+            pl.BlockSpec((3 * HD, width), lambda i: (0, 0)),
+            pl.BlockSpec((HD, 1), lambda i: (0, 0)),
+        ],
+        scratch_shapes=[
+            pltpu.VMEM((n, rows, HD), BF),
+            pltpu.VMEM((n, 1, rows), F32),
+            pltpu.VMEM((n, HD, rows), F32),
+            pltpu.VMEM((HD, rows), F32),
+        ],
+        compiler_params=pltpu.CompilerParams(vmem_limit_bytes=48 * 2**20),
+        name="attend_back",
+    )(h_all, scale_col, first_key, k, v, kt, raw, q, qt, gt, o32, lse)
+
+
+def joined(own, other, fs):
+    return jnp.where(
+        fs == 0, jnp.concatenate([own, other], axis=0), jnp.concatenate([other, own], axis=0)
+    )
+
+
+def fast_local(
+    tokens, query_weight, key_weight, value_weight, out_weight, inner_weight, outer_weight,
+    attn_gain, mlp_gain, query_scale, doc_starts, cotangent,
+):
+    me, fs = lax.axis_index("ctx"), lax.axis_index("fs")
+    rows, width = tokens.shape[1:]
+    tok = tokens[0]
+    cot = cotangent[0]
+
+    def head_columns(w):
+        return lax.dynamic_slice(w, (0, me * HD), (w.shape[0], HD)).T
+
+    wt = jnp.concatenate([head_columns(w) for w in (query_weight, key_weight, value_weight)], axis=0)
+    gains = jnp.stack([attn_gain, mlp_gain])
+    positions = jnp.arange(H * rows, dtype=jnp.int32)
+    starts = doc_starts[0]
+    first_key = jnp.max(
+        jnp.where(starts[None, :] <= positions[:, None], starts[None, :], 0), axis=1
+    ).reshape(H, 1, rows)
+    scale_col = (query_scale / math.sqrt(HD))[:, None]
+
+    h_all, wt_all, gain_full, out_o, inner_o, outer_o = gather_call(
+        tok, gains, wt, (out_weight, inner_weight, outer_weight)
+    )
+    o_t, o32, lse, qt, q, kt, k, v, raw = attend_call(h_all, wt_all, scale_col, first_key)
+    attn_t, query_o, key_o, value_o = swap_call(2, o_t, (query_weight, key_weight, value_weight))
+    attn_t = attn_t.reshape(width, rows)
+
+    out_full = joined(out_weight, out_o, fs)
+    inner_full = joined(inner_weight, inner_o, fs)
+    outer_full = joined(outer_weight, outer_o, fs)
+    gain_one, gain_two = gain_full[0:1], gain_full[1:2]
+    token_rows = tok.astype(F32)
+    resid = token_rows + dot(attn_t, out_full, TN)
+    scale_two = rms_scale(resid)
+    normed_two = resid * scale_two
+    hidden_two = (normed_two * gain_two).astype(BF)
+    inner_pre = dot(hidden_two, inner_full)
+    active = jax.nn.silu(inner_pre).astype(BF)
+    result = (resid + dot(active, outer_full)).astype(BF)
+    grad_active = dot(cot, outer_full, NT)
+    sig = jax.nn.sigmoid(inner_pre)
+    grad_inner_pre = (grad_active * sig * (1.0 + inner_pre * (1.0 - sig))).astype(BF)
+    grad_hidden_two = dot(grad_inner_pre, inner_full, NT)
+    grad_gain_two = jnp.sum(grad_hidden_two * normed_two, axis=0)
+    grad_resid = (
+        cot.astype(F32) + norm_back(grad_hidden_two * gain_two, normed_two, scale_two)
+    ).astype(BF)
+    grad_att_t = dot(out_full, grad_resid, NT).astype(BF).reshape(H, HD, rows)
+    (g_t,) = swap_call(3, grad_att_t)
+    grad_outer = dot(active, cot, TN).astype(BF)
+    grad_inner = dot(hidden_two, grad_inner_pre, TN).astype(BF)
+    grad_outw = dot(attn_t, grad_resid).astype(BF)
+
+    d_all, dw, dscale = attend_back_call(
+        h_all, scale_col, first_key, k, v, kt, raw, q, qt, g_t, o32, lse
+    )
+    half = width // 2
+    dw_mine = lax.dynamic_slice(dw, (0, fs * half), (dw.shape[0], half))
+    dw_send = lax.dynamic_slice(dw, (0, (1 - fs) * half), (dw.shape[0], half)).astype(BF)
+    d_mine, dw_got = swap_call(4, d_all, (), dw_send)
+    dw_sum = (dw_mine + dw_got.astype(F32)).astype(BF)
+    d_mine = d_mine.reshape(H, 3, HD, rows)
+    query_full = joined(query_weight, query_o, fs)
+    key_full = joined(key_weight, key_o, fs)
+    value_full = joined(value_weight, value_o, fs)
+    grad_hidden_one = sum(
+        dot(d_mine[:, i].reshape(width, rows), w, ((0,), (1,)))
+        for i, w in enumerate((query_full, key_full, value_full))
+    )
+    scale_one = rms_scale(token_rows)
+    normed_one = token_rows * scale_one
+    grad_gain_one = jnp.sum(grad_hidden_one * normed_one, axis=0)
+    grad_tokens = (
+        grad_resid.astype(F32) + norm_back(grad_hidden_one * gain_one, normed_one, scale_one)
+    ).astype(BF)
+
+    dw_all = lax.all_gather(dw_sum, "ctx", axis=0, tiled=False).reshape(H, 3, HD, half)
+    dw_qkv = [dw_all[:, i].reshape(width, half).T.astype(F32) for i in range(3)]
+    dense = [
+        lax.psum(lax.psum_scatter(g, "fs", scatter_dimension=0, tiled=True), "ctx").astype(F32)
+        for g in (grad_outw, grad_inner, grad_outer)
+    ]
+    small = lax.psum(
+        jnp.concatenate([grad_gain_one, grad_gain_two, dscale[:, 0]]), ("ctx", "fs")
+    )
+    gain_one_sum = lax.dynamic_slice(small, (fs * half,), (half,))
+    gain_two_sum = lax.dynamic_slice(small, (width + fs * half,), (half,))
+    scale_sum = small[2 * width :] / math.sqrt(HD)
+    return (
+        result[None], grad_tokens[None], *dw_qkv, *dense, gain_one_sum, gain_two_sum, scale_sum,
+    )
+
+
 def solution(mesh):
     placed = (
         P("fs", "ctx", None),
@@ -335,7 +921,7 @@
         P("fs", "ctx", None),
     )
     return jax.shard_map(
-        local,
+        fast_local if fast_fits(mesh) else general_local,
         mesh=mesh,
         in_specs=placed,
         out_specs=(

time: 1850 us -> 646 us (0.35)
  waiting for transfers between devices: 955 us -> 127 us
  starting transfers between devices: 515 us -> 0.38 us
  Pallas kernels: 0 us -> 342 us
  other arithmetic: 153 us -> 20.8 us
  local copies, waits for them, and re-layouts: 86.4 us -> 53.3 us
  matrix products: 63.5 us -> 31.2 us
    ppermute x92 -> x0, starting transfers between devices: 514 us -> none  [the longest x60 493 us: shifted(): lax.ppermute(value, axis, [(source, source + steps) for source in range(l...]
    ppermute x92 -> x0, waiting for transfers between devices: 443 us -> none  [the longest x32 416 us: passed_along(): return lax.ppermute(block, axis, route)]
    pallas_call x0 -> x6, Pallas kernels: none -> 342 us  [the longest x3 140 us: swap_call(): pl.pallas_call(functools.partial(swap_kernel, n_w, has_y), out_shape=[jax...]
    psum x1, waiting for transfers between devices: 140 us -> 0.01 us  [fast_local(): lax.psum(lax.psum_scatter(g, 'fs', scatter_dimension=0, tiled=True), 'ctx')]
    all_gather x6 -> x1, waiting for transfers between devices: 124 us -> 0.01 us  [fast_local(): lax.all_gather(dw_sum, 'ctx', axis=0, tiled=False).reshape(H, 3, HD, half)]
    reduce_scatter x6 -> x3, waiting for transfers between devices: 245 us -> 127 us  [fast_local(): lax.psum_scatter(g, 'fs', scatter_dimension=0, tiled=True)]
    convert_element_type x108 -> x8, other arithmetic: 117 us -> 17 us  [the longest x3 7.45 us: fast_local(): lax.psum(lax.psum_scatter(g, 'fs', scatter_dimension=0, tiled=True), 'ctx')]
    while x180 -> x0, local copies, waits for them, and re-layouts: 60.8 us -> none
  transfers between devices with their start and end apart: 105 -> 5, of which waited for: 57 -> 3; matrix products, arithmetic and copies ran while one was open for 9% -> 6% of each run, Pallas kernels for 0% -> 23%
where the time goes in v1:
time: 646 us; the launch traced here: 645 us
  Pallas kernels  342 us (53%)
  waiting for transfers between devices  127 us (20%)
  blocking collectives  56.3 us (9%)
  local copies, waits for them, and re-layouts  53.3 us (8%)
  matrix products  31.2 us (5%)
  other arithmetic  20.8 us (3%)
  between operations  14.2 us (2%)
    pallas_call x3, Pallas kernels, swap_call(): pl.pallas_call(functools.partial(swap_kernel, n_w, has_y), out_shape=[jax...  140 us
    reduce_scatter x3, waiting for transfers between devices, fast_local(): lax.psum_scatter(g, 'fs', scatter_dimension=0, tiled=True)  127 us
    pallas_call x1, Pallas kernels, gather_call(): pl.pallas_call(functools.partial(gather_kernel, n_w), out_shape=shapes, i...  70.5 us
    pallas_call x1, Pallas kernels, attend_back_call(): pl.pallas_call(attend_back_kernel, grid=(n,), out_shape=[jax.ShapeDtypeSt...  67.6 us
    pallas_call x1, Pallas kernels, attend_call(): pl.pallas_call(attend_kernel, grid=(n,), out_shape=[out(BF, HD, rows), ou...  64.1 us
    psum x1, blocking collectives, fast_local(): lax.psum(jnp.concatenate([grad_gain_one, grad_gain_two, dscale[:, 0]]), (...  56.3 us
    unnamed x96, local copies, waits for them, and re-layouts  40.9 us
    dot_general x12, matrix products, dot(): return lax.dot_general(a, b, (dims, ((), ())), preferred_element_type=F32)  31.2 us
  transfers between devices with their start and end apart: 5, of which 3 were waited for; matrix products, arithmetic and copies ran while one was open for 6% of the time, Pallas kernels for 23%

profile of v1, /device:TPU:0, one launch (start us, length us, event | category | flops | bytes accessed | tf_op | source)
XLA Modules:
  0.0 645.3 jit_solution(2138248000856141357)
XLA Ops:
  8.8 1.2 constant_dynamic-slice_fusion
  10.3 1.1 constant_dynamic-slice_fusion.2
  11.9 1.4 copy-done.4
  13.3 1.4 copy-done.6
  14.8 70.5 %gather_hidden.1 = (bf16[16,256,1280]{2,1,0:T(8,128)(2,1)S(1)}, bf16[240,1280]{1,0:T(8,128)(2,1)S(1)}, f32[2,1280]{1,0:T(2,128)S(1)}, bf16[640,1280]{1,0:T(8,128...) custom-call(bf16[256,1280]{1,0:T(8,128)(2,1)S(1)} %bitcast.68, ...), custom_call_target="tpu_custom_call" | custom-call | tf_op jit(solution)/shard_map/gather_hidden/pallas_call | solution.py:535
  85.3 4.0 copy-done
  89.3 1.2 copy-done.18
  90.5 1.2 copy-done.21
  91.6 64.1 %attend.1 = (bf16[16,80,256]{2,1,0:T(8,128)(2,1)S(1)}, f32[16,80,256]{2,1,0:T(8,128)}, f32[16,1,256]{2,1,0:T(1,128)S(1)}, bf16[16,80,256]{2,1,0:T(8,128)(2,1)S(1...) custom-call(bf16[16,256,1280]{2,1,0:T(8,128)(2,1)} %copy-done, ...), custom_call_target="tpu_custom_call" | custom-call | tf_op jit(solution)/shard_map/attend/pallas_call | solution.py:696
  160.2 61.6 %swap2.1 = (bf16[16,80,256]{2,1,0:T(8,128)(2,1)}, bf16[640,1280]{1,0:T(8,128)(2,1)}, bf16[640,1280]{1,0:T(8,128)(2,1)}, bf16[640,1280]{1,0:T(8,128)(2,1)}) custom-call(bf16[16,80,256]{2,1,0:T(8,128)(2,1)} %copy-done.17, bf16[640,1280]{1,0:T(8,128)(2,1)} %refs_1_.1, bf16[640,1280]{1,0:T(8,128)(2,1)} %refs_2_.1, bf16[640,1280]{1,0:T(8,128)(2,1)} %refs_3_.1), custom_call_target="tpu_custom_call" | custom-call | tf_op jit(solution)/shard_map/swap2/pallas_call | solution.py:604
  221.9 4.0 multiply_reduce_fusion.2
  226.0 1.3 fusion.42
  229.0 1.4 fusion.25
  230.4 1.5 multiply_reduce_fusion
  233.2 2.7 convolution_convert_fusion.2
  236.0 1.2 copy-done.27
  237.3 4.0 convolution_convert_fusion.1
  242.3 4.3 convolution_convert_fusion
  246.7 31.5 %reduce-scatter.4.cloned.1.call-done = bf16[640,1280]{1,0:T(8,128)(2,1)} async-done(((bf16[1280,1280]{1,0:T(8,128)(2,1)}), bf16[640,1280]{1,0:T(8,128)(2,1)}) %reduce-scatter.4.cloned.1.call-update) | async-done | bytes 1638416 | tf_op jit(solution)/shard_map/reduce_scatter | solution.py:894
  278.3 47.7 %reduce-scatter.6.cloned.1.call-done = bf16[640,1280]{1,0:T(8,128)(2,1)} async-done(((bf16[1280,1280]{1,0:T(8,128)(2,1)}), bf16[640,1280]{1,0:T(8,128)(2,1)}) %reduce-scatter.6.cloned.1.call-update) | async-done | bytes 1638416 | tf_op jit(solution)/shard_map/reduce_scatter | solution.py:894
  326.0 47.6 %reduce-scatter.8.cloned.1.call-done = bf16[640,1280]{1,0:T(8,128)(2,1)} async-done(((bf16[1280,1280]{1,0:T(8,128)(2,1)}), bf16[640,1280]{1,0:T(8,128)(2,1)}) %reduce-scatter.8.cloned.1.call-update) | async-done | bytes 1638416 | tf_op jit(solution)/shard_map/reduce_scatter | solution.py:894
  373.9 1.2 copy-done.5
  375.1 4.1 convolution_convert_fusion.3
  379.2 22.5 %swap3.1.gt_ref = bf16[16,80,256]{2,1,0:T(8,128)(2,1)} custom-call(bf16[16,80,256]{2,1,0:T(8,128)(2,1)} %bitcast.75), custom_call_target="tpu_custom_call" | custom-call | tf_op jit(solution)/shard_map/swap3/pallas_call | solution.py:604
  401.7 1.1 copy-done.2
  402.8 1.2 copy-done.12
  404.0 1.1 copy-done.14
  405.1 1.1 copy-done.16
  406.2 67.6 %attend_back.1 = (bf16[16,240,256]{2,1,0:T(8,128)(2,1)}, f32[240,1280]{1,0:T(8,128)}, f32[80,1]{1,0:T(8,128)S(1)}) custom-call(bf16[16,256,1280]{2,1,0:T(8,128)(2,1)} %copy-done, f32[80,1]{1,0:T(8,128)S(1)} %copy.47.scale_ref, s32[16,1,256]{2,1,0:T(1,128)S(1)} %bitcast.70, bf16[16,256,80]{2,1,0:T(8,128)(2,1)S(1)} %copy-done.10, ...), custom_call_target="tpu_custom_call" | custom-call | tf_op jit(solution)/shard_map/attend_back/pallas_call | solution.py:780
  473.8 2.0 dynamic-slice_convert_fusion.refs_1_
  475.8 55.7 %swap4.1 = (bf16[16,240,256]{2,1,0:T(8,128)(2,1)}, bf16[240,640]{1,0:T(8,128)(2,1)}) custom-call(bf16[16,240,256]{2,1,0:T(8,128)(2,1)} %get-tuple-element.51.refs_0_, bf16[240,640]{1,0:T(8,128)(2,1)} %dynamic-slice_convert_fusion.refs_1_), custom_call_target="tpu_custom_call" | custom-call | tf_op jit(solution)/shard_map/swap4/pallas_call | solution.py:604
  531.5 1.7 add_convert_fusion.1
  533.6 1.8 fusion.53
  538.1 1.1 fusion.22
  540.1 2.3 fusion.36
  542.4 56.3 %psum.31 = f32[2640]{0:T(1024)S(1)} all-reduce(f32[2640]{0:T(1024)S(1)} %pad_maximum_fusion.1), channel_id=1, replica_groups=mesh['ctx'=16,'fs'=2] {'ctx','fs'}, use_global_device_ids=true, to_apply=%region_13.14 | all-reduce | flops 2640 | bytes 21120 | tf_op jit(solution)/shard_map/psum | solution.py:897
  599.9 2.7 fusion.38
  602.7 3.4 fusion.27
  606.1 3.5 convert_element_type.107
  609.7 2.0 convert_element_type.109
  611.7 2.0 convert_element_type.111
  613.6 4.0 fusion.52
  617.6 2.1 convert_bitcast_fusion.2
  619.7 4.6 copy.53
  624.2 3.3 convert_bitcast_fusion.1
  627.6 4.6 copy.54
  632.1 2.0 convert_bitcast_fusion
  634.2 4.6 copy.55
  (113 shorter events, 16.4 us)
Async XLA Ops:
  7.2 4.4 copy-start.43
  7.2 4.5 copy-start.39
  7.2 4.7 copy-start.1
  7.2 4.7 copy-start.3
  7.2 271.1 %reduce-scatter.4.cloned.1.call-start = ((), (), s32[]{:S(2)}) async-start(), calls=%async_computation.3 | async-start | bytes 4915200 | tf_op jit(solution)/shard_map/reduce_scatter | solution.py:894
  11.9 1.4 copy-start.4
  13.3 1.4 copy-start.6
  85.3 4.0 copy-start
  89.3 1.2 copy-start.18
  90.5 1.2 copy-start.21
  91.6 64.1 %copy-start.22 = (bf16[640,1280]{1,0:T(8,128)(2,1)}, bf16[640,1280]{1,0:T(8,128)(2,1)S(1)}, u32[]{:S(2)}) copy-start(bf16[640,1280]{1,0:T(8,128)(2,1)S(1)} %get-tuple-element.41) | copy-start | bytes 4915204
  155.7 1.0 copy-start.9
  156.7 1.0 copy-start.11
  157.7 0.8 copy-start.13
  221.9 4.1 copy-start.23
  225.9 6.0 copy-start.26
  226.0 2.4 copy-start.7
  226.0 2.6 copy-start.19
  226.0 3.0 copy-start.36
  227.3 1.1 copy-start.44
  230.4 1.5 copy-start.38
  232.0 1.3 copy-start.29
  232.4 0.8 copy-start.24
  235.9 1.3 copy-start.27
  236.0 90.0 %reduce-scatter.6.cloned.1.call-start = ((), (), s32[]{:S(2)}) async-start(), calls=%async_computation.4 | async-start | bytes 4915200 | tf_op jit(solution)/shard_map/reduce_scatter | solution.py:894
  241.2 1.1 copy-start.37
  241.2 132.4 %reduce-scatter.8.cloned.1.call-start = ((), (), s32[]{:S(2)}) async-start(), calls=%async_computation.5 | async-start | bytes 4915200 | tf_op jit(solution)/shard_map/reduce_scatter | solution.py:894
  246.7 359.4 %all-reduce.3.cloned.1.call-start = ((), (), s32[]{:S(2)}) async-start(), calls=%async_computation.7 | async-start | bytes 9830400 | tf_op jit(solution)/shard_map/psum | solution.py:894
  373.7 1.4 copy-start.5
  373.7 239.9 %all-gather.3.cloned.1.call-start = ((), (), s32[]{:S(2)}) async-start(), calls=%async_computation.6 | async-start | bytes 5222400 | tf_op jit(solution)/shard_map/all_gather | solution.py:891
  379.2 22.5 %copy-start.10 = (bf16[16,256,80]{2,1,0:T(8,128)(2,1)S(1)}, bf16[16,256,80]{2,1,0:T(8,128)(2,1)}, u32[]{:S(2)}) copy-start(bf16[16,256,80]{2,1,0:T(8,128)(2,1)} %copy-done.9) | copy-start | bytes 1966084
  401.7 1.1 copy-start.2
  402.8 1.2 copy-start.12
  404.0 1.1 copy-start.14
  405.1 1.1 copy-start.16
  473.8 57.7 %copy-start.35 = (f32[240,1280]{1,0:T(8,128)S(1)}, f32[240,1280]{1,0:T(8,128)}, u32[]{:S(2)}) copy-start(f32[240,1280]{1,0:T(8,128)} %get-tuple-element.52) | copy-start | bytes 3686404
  533.6 2.1 copy-start.30
  533.6 2.5 copy-start.42
  536.2 1.5 copy-start.31
  536.2 1.9 copy-start.41
  538.1 1.5 copy-start.32
  538.1 2.0 copy-start.40
  540.1 59.9 %copy-start.25 = (bf16[256,1280]{1,0:T(8,128)(2,1)S(1)}, bf16[256,1280]{1,0:T(8,128)(2,1)}, u32[]{:S(2)}) copy-start(bf16[256,1280]{1,0:T(8,128)(2,1)} %copy-done.24) | copy-start | bytes 1966084
  540.1 62.6 %copy-start.28 = (f32[256,1280]{1,0:T(8,128)S(1)}, f32[256,1280]{1,0:T(8,128)}, u32[]{:S(2)}) copy-start(f32[256,1280]{1,0:T(8,128)} %copy-done.26) | copy-start | bytes 3932164
  599.9 2.7 copy-start.8
  599.9 2.7 copy-start.20
  606.1 3.6 copy-start.34
  609.7 2.0 copy-start.33
  (2 other events, 1.7 us)
Sparse Core Ops, SparseCore 0:
  236.1 42.1 reduce-scatter.3
  281.2 44.7 reduce-scatter.5
  328.8 44.7 reduce-scatter.7
  378.0 171.8 all-reduce.2
  552.8 55.7 all-gather.2

commit v2 on v1

--- a/solution.py
+++ b/solution.py
@@ -358,6 +358,10 @@
 TN = ((0,), (0,))
 
 
+LOG2E = math.log2(math.e)
+UNITS = H // 2
+
+
 def weight_pull(own, other, k, fs, me, ssem, rsem):
     half = own[0].shape[0] // 2
     rows = pl.ds(pl.multiple_of(k * half, 64), half)
@@ -372,31 +376,35 @@
     return first, second
 
 
-def gather_kernel(n_w, tok_ref, gain_ref, wt_ref, *rest):
+def visible(j, i, rows, first_key):
+    kpos = j * rows + lax.broadcasted_iota(jnp.int32, (rows, rows), 0)
+    qpos = i * rows + lax.broadcasted_iota(jnp.int32, (rows, rows), 1)
+    return (kpos <= qpos) & (kpos >= first_key)
+
+
+def forward_kernel(n_w, tok_ref, gain_ref, wt_ref, scale_ref, first_ref, *rest):
     own = rest[:n_w]
-    h_all, wt_all, gain_full = rest[n_w : n_w + 3]
-    other = rest[n_w + 3 : 2 * n_w + 3]
-    h_own, gain_other, gain_own, ssem, rsem, wssem, wrsem, ysem, lsem = rest[2 * n_w + 3 :]
+    at = n_w
+    h_all, gain_full, attn_ref = rest[at : at + 3]
+    o32_ref, lse_ref, qt_ref, q_ref, kt_ref, k_ref, v_ref, raw_ref = rest[at + 3 : at + 11]
+    other = rest[at + 11 : at + 11 + n_w]
+    (
+        wt_all, gain_own, gain_other, o_sc, vt_sc, m_sc, l_sc, acc_sc,
+        ssem, rsem, osend, orecv, wssem, wrsem, ysem, lsem,
+    ) = rest[at + 11 + n_w :]
     me, fs, z, x, k = place()
     sib, xn, yn = (me + 1 - 2 * k, fs), (me + 2 - 4 * x, fs), (me, 1 - fs)
     up, dn = (me + 4, fs), (me - 4, fs)
+    rows = tok_ref.shape[0]
+    unit_rows = 2 * rows
     bar = pltpu.get_barrier_semaphore()
-    signal(sib)
-    signal(xn)
+    for i in range(1, H):
+        signal((lax.rem(me + i, H), fs))
     signal(yn)
-
-    @pl.when(z < 3)
-    def _():
-        signal(up)
-
-    @pl.when(z > 0)
-    def _():
-        signal(dn)
-
     gain_own[...] = gain_ref[...]
-    rows = tok_ref[...].astype(F32)
-    normed = rows * lax.rsqrt(jnp.mean(rows * rows, axis=-1, keepdims=True) + epsilon)
-    pl.semaphore_wait(bar, 3 + (z + 2) // 3 + (5 - z) // 3)
+    tokens = tok_ref[...].astype(F32)
+    normed = tokens * lax.rsqrt(jnp.mean(tokens * tokens, axis=-1, keepdims=True) + epsilon)
+    pl.semaphore_wait(bar, H)
 
     gain_copy = remote(gain_own, gain_other, ysem.at[0], ysem.at[1], yn)
     gain_copy.start()
@@ -408,8 +416,6 @@
     wt_here.start()
     first, second = weight_pull(own, other, k, fs, me, wssem, wrsem)
     gain_copy.wait()
-    for c in first:
-        c.start()
     g_here = gain_own[...].astype(F32)
     g_there = gain_other[...].astype(F32)
     gains = jnp.where(
@@ -418,29 +424,85 @@
         jnp.concatenate([g_there, g_here], axis=1),
     )
     gain_full[...] = gains
-    h_own[...] = (normed * gains[0:1]).astype(BF)
-
-    def cp(slot, t, si, mine=False):
-        return remote(h_own if mine else h_all.at[slot], h_all.at[slot], ssem.at[si], rsem.at[slot], t)
-
-    here = pltpu.make_async_copy(h_own, h_all.at[me], lsem.at[1])
-    cp(me, xn, 0, True).start()
+    my_rows = pl.ds(pl.multiple_of(k * rows, rows), rows)
+    h_all[me // 2, my_rows, :] = (normed * gains[0:1]).astype(BF)
+
+    def slot(s):
+        return h_all.at[s // 2, pl.ds(pl.multiple_of(lax.rem(s, 2) * rows, rows), rows)]
+
+    def cp(s, t, si):
+        return remote(slot(s), slot(s), ssem.at[si], rsem.at[s], t)
+
+    cp(me, xn, 0).start()
 
     @pl.when(z < 3)
     def _():
-        cp(me, up, 1, True).start()
+        cp(me, up, 1).start()
 
     @pl.when(z > 0)
     def _():
-        cp(me, dn, 2, True).start()
-
-    cp(me, sib, 3, True).start()
-    here.start()
-    for d in range(1, 4):
+        cp(me, dn, 2).start()
+
+    cp(me, sib, 3).start()
+    for c in first:
+        c.start()
+    wt_here.wait()
+    wt_copy.wait()
+
+    def project(u):
+        qkv = dot(wt_all[...], h_all[u], NT)
+        raw = qkv[:HD]
+        raw_ref[u] = raw
+        q32 = raw * scale_ref[...]
+        qt_ref[u] = (q32 * LOG2E).astype(BF)
+        q_ref[u] = q32.T.astype(BF)
+        kt = qkv[HD : 2 * HD]
+        vt = qkv[2 * HD :]
+        kt_ref[u] = kt.astype(BF)
+        k_ref[u] = kt.T.astype(BF)
+        v_ref[u] = vt.T.astype(BF)
+        vt_sc[u] = vt.astype(BF)
+        m_sc[u] = jnp.full((1, unit_rows), neg_big, F32)
+        l_sc[u] = jnp.zeros((1, unit_rows), F32)
+        acc_sc[u] = jnp.zeros((HD, unit_rows), F32)
+
+    def pair(j, i):
+        s = dot(k_ref[j], qt_ref[i])
+        s = jnp.where(visible(j, i, unit_rows, first_ref[i]), s, neg_big)
+        run_max = m_sc[i]
+        new_max = jnp.maximum(run_max, jnp.max(s, axis=0, keepdims=True))
+        p = jnp.exp2(s - new_max)
+        factor = jnp.exp2(run_max - new_max)
+        l_sc[i] = l_sc[i] * factor + jnp.sum(p, axis=0, keepdims=True)
+        acc_sc[i] = acc_sc[i] * factor + dot(vt_sc[j], p.astype(BF))
+        m_sc[i] = new_max
+
+    def when_here(uz, ux):
+        return 4 * jnp.maximum(uz - z, z - uz) + 2 * jnp.maximum(ux - x, x - ux) + (uz + 4 - z) // 5
+
+    def process(uz, ux):
+        u = uz * 2 + ux
+        cp(u * 2 + 1 - k, sib, 0).wait_recv()
+        project(u)
+        pair(u, u)
+        mine = when_here(uz, ux)
+
+        def earlier(e, c):
+            @pl.when(when_here(e // 2, lax.rem(e, 2)) < mine)
+            def _():
+                pair(jnp.minimum(e, u), jnp.maximum(e, u))
+
+            return c
+
+        lax.fori_loop(0, UNITS, earlier, 0)
+
+    xo = me + 2 - 4 * x
+
+    def column_arrival(d):
         a = 4 + (d - 1) * 6
 
         @pl.when(z >= d)
-        def _(a=a, d=d):
+        def _():
             s = me - 4 * d
             cp(s, dn, a).wait_recv()
 
@@ -452,7 +514,7 @@
             cp(s, sib, a + 2).start()
 
         @pl.when(z + d <= 3)
-        def _(a=a, d=d):
+        def _():
             s = me + 4 * d
             cp(s, up, a + 3).wait_recv()
 
@@ -463,37 +525,113 @@
             cp(s, xn, a + 4).start()
             cp(s, sib, a + 5).start()
 
-        if d <= n_w:
-            first[d - 1].wait_recv()
-            second[d - 1].start()
-
-    xo = me + 2 - 4 * x
-    for zz in range(4):
-        s = xo + 4 * (zz - z)
-        cp(s, xn, 22 + zz).wait_recv()
-        cp(s, sib, 22 + zz).start()
-    for i in range(3, n_w):
+    def across_arrival(d):
+        @pl.when(z >= d)
+        def _():
+            s = xo - 4 * d
+            cp(s, xn, 0).wait_recv()
+            cp(s, sib, 22 + z - d).start()
+
+        @pl.when((z + d <= 3) & (d > 0))
+        def _():
+            s = xo + 4 * d
+            cp(s, xn, 0).wait_recv()
+            cp(s, sib, 22 + z + d).start()
+
+    def step(d, c):
+        @pl.when((d >= 1) & (d <= 3))
+        def _():
+            column_arrival(d)
+
+        @pl.when(d >= 1)
+        def _():
+            across_arrival(d - 1)
+
+        for i in range(n_w):
+            if i < 4:
+
+                @pl.when(d == i + 1)
+                def _(i=i):
+                    first[i].wait_recv()
+                    second[i].start()
+
+        def compute(n, c2):
+            across = 1 - n // 2
+            dd = d - across
+            uz = z + dd * (2 * lax.rem(n, 2) - 1)
+            ux = x + across * (1 - 2 * x)
+            ok = (dd >= 0) & (dd <= 3) & (uz >= 0) & (uz <= 3)
+            ok = ok & ((dd > 0) | (lax.rem(n, 2) == 0))
+
+            @pl.when(ok)
+            def _():
+                process(uz, ux)
+
+            return c2
+
+        lax.fori_loop(0, 4, compute, 0)
+        return c
+
+    lax.fori_loop(0, 5, step, 0)
+
+    def out_copy(b):
+        u = b // 2
+        lanes = pl.ds(pl.multiple_of(lax.rem(b, 2) * rows, 128), rows)
+        return o_sc.at[u, :, lanes]
+
+    def finish(n, c):
+        u = lax.rem(me // 2 + n, UNITS)
+        out = acc_sc[u] / l_sc[u]
+        o32_ref[u] = out
+        o_sc[u] = out.astype(BF)
+        lse_ref[u] = m_sc[u] + jnp.log2(l_sc[u])
+
+        def send(e, c2):
+            b = u * 2 + e
+
+            @pl.when(b != me)
+            def _():
+                remote(out_copy(b), attn_ref.at[me], osend.at[b], orecv.at[me], (b, fs)).start()
+
+            @pl.when(b == me)
+            def _():
+                pltpu.make_async_copy(out_copy(b), attn_ref.at[me], lsem.at[1]).start()
+
+            return c2
+
+        return lax.fori_loop(0, 2, send, c)
+
+    lax.fori_loop(0, UNITS, finish, 0)
+    for i in range(4, n_w):
         first[i].wait_recv()
         second[i].start()
-    for zz in range(4):
-        for xx in range(2):
-            cp(zz * 4 + xx * 2 + 1 - k, sib, 0).wait_recv()
-    cp(me, xn, 0, True).wait_send()
+
+    def taken(b, c):
+        @pl.when(b != me)
+        def _():
+            remote(out_copy(b), attn_ref.at[b], osend.at[b], orecv.at[b], (b, fs)).wait()
+
+        return c
+
+    lax.fori_loop(0, H, taken, 0)
+    pltpu.make_async_copy(out_copy(me), attn_ref.at[me], lsem.at[1]).wait()
+    cp(me, xn, 0).wait_send()
 
     @pl.when(z < 3)
     def _():
-        cp(me, up, 1, True).wait_send()
+        cp(me, up, 1).wait_send()
 
     @pl.when(z > 0)
     def _():
-        cp(me, dn, 2, True).wait_send()
-
-    cp(me, sib, 3, True).wait_send()
-    for d in range(1, 4):
+        cp(me, dn, 2).wait_send()
+
+    cp(me, sib, 3).wait_send()
+
+    def sent(d, c):
         a = 4 + (d - 1) * 6
 
         @pl.when(z >= d)
-        def _(a=a, d=d):
+        def _():
             s = me - 4 * d
 
             @pl.when(z < 3)
@@ -504,7 +642,7 @@
             cp(s, sib, a + 2).wait_send()
 
         @pl.when(z + d <= 3)
-        def _(a=a, d=d):
+        def _():
             s = me + 4 * d
 
             @pl.when(z > 0)
@@ -514,34 +652,52 @@
             cp(s, xn, a + 4).wait_send()
             cp(s, sib, a + 5).wait_send()
 
-    for zz in range(4):
+        return c
+
+    lax.fori_loop(1, 4, sent, 0)
+
+    def sent_across(zz, c):
         cp(xo + 4 * (zz - z), sib, 22 + zz).wait_send()
-    wt_copy.wait()
-    wt_here.wait()
-    here.wait()
+        return c
+
+    lax.fori_loop(0, 4, sent_across, 0)
     for i in range(n_w):
         first[i].wait_send()
         second[i].wait()
 
 
-def gather_call(tok, gains, wt, weights):
+def forward_call(tok, gains, wt, scale_col, first_key, weights):
     n_w = len(weights)
     rows, width = tok.shape
+    ur = 2 * rows
+
+    def out(dtype, *shape):
+        return jax.ShapeDtypeStruct((UNITS, *shape), dtype)
+
     shapes = [
-        jax.ShapeDtypeStruct((H, rows, width), BF),
-        jax.ShapeDtypeStruct((wt.shape[0], 2 * wt.shape[1]), BF),
+        out(BF, ur, width),
         jax.ShapeDtypeStruct((gains.shape[0], 2 * gains.shape[1]), F32),
+        jax.ShapeDtypeStruct((H, HD, rows), BF),
+        out(F32, HD, ur), out(F32, 1, ur), out(BF, HD, ur), out(BF, ur, HD), out(BF, HD, ur),
+        out(BF, ur, HD), out(BF, ur, HD), out(F32, HD, ur),
     ] + [jax.ShapeDtypeStruct(w.shape, BF) for w in weights]
     return pl.pallas_call(
-        functools.partial(gather_kernel, n_w),
+        functools.partial(forward_kernel, n_w),
         out_shape=shapes,
-        in_specs=[VMEM, VMEM, ANY] + [ANY] * n_w,
-        out_specs=[ANY, ANY, VMEM] + [ANY] * n_w,
+        in_specs=[VMEM] * 5 + [ANY] * n_w,
+        out_specs=[VMEM, VMEM, ANY] + [VMEM] * 8 + [ANY] * n_w,
         scratch_shapes=[
-            pltpu.VMEM((rows, width), BF),
+            pltpu.VMEM((wt.shape[0], 2 * wt.shape[1]), BF),
             pltpu.VMEM(gains.shape, BF),
             pltpu.VMEM(gains.shape, BF),
+            pltpu.VMEM((UNITS, HD, ur), BF),
+            pltpu.VMEM((UNITS, HD, ur), BF),
+            pltpu.VMEM((UNITS, 1, ur), F32),
+            pltpu.VMEM((UNITS, 1, ur), F32),
+            pltpu.VMEM((UNITS, HD, ur), F32),
             pltpu.SemaphoreType.DMA((26,)),
+            pltpu.SemaphoreType.DMA((H,)),
+            pltpu.SemaphoreType.DMA((H,)),
             pltpu.SemaphoreType.DMA((H,)),
             pltpu.SemaphoreType.DMA((2 * n_w,)),
             pltpu.SemaphoreType.DMA((2 * n_w,)),
@@ -549,10 +705,10 @@
             pltpu.SemaphoreType.DMA((2,)),
         ],
         compiler_params=pltpu.CompilerParams(
-            collective_id=1, has_side_effects=True, vmem_limit_bytes=32 * 2**20
+            collective_id=1, has_side_effects=True, vmem_limit_bytes=56 * 2**20
         ),
-        name="gather_hidden",
-    )(tok, gains, wt, *weights)
+        name="forward",
+    )(tok, gains, wt, scale_col, first_key, *weights)
 
 
 def swap_kernel(n_w, has_y, *refs):
@@ -619,190 +775,90 @@
     return out
 
 
-def visible(j, i, rows, first_key):
-    kpos = j * rows + lax.broadcasted_iota(jnp.int32, (rows, rows), 0)
-    qpos = i * rows + lax.broadcasted_iota(jnp.int32, (rows, rows), 1)
-    return (kpos <= qpos) & (kpos >= first_key)
-
-
-def attend_kernel(
-    h_ref, wt_ref, scale_ref, first_ref,
-    o_ref, o32_ref, lse_ref, qt_ref, q_ref, kt_ref, k_ref, v_ref, raw_ref,
-    k_sc, vt_sc,
-):
-    i = pl.program_id(0)
-    last = pl.num_programs(0) - 1
-    rows = h_ref.shape[1]
-    qkv = dot(wt_ref[...], h_ref[0], NT)
-    raw = qkv[:HD]
-    raw_ref[0] = raw
-    q32 = raw * scale_ref[...]
-    qt = q32.astype(BF)
-    qt_ref[0] = qt
-    q_ref[0] = q32.T.astype(BF)
-    kt32 = qkv[HD : 2 * HD]
-    vt32 = qkv[2 * HD :]
-    kt_ref[0] = kt32.astype(BF)
-    key = kt32.T.astype(BF)
-    k_ref[0] = key
-    v_ref[0] = vt32.T.astype(BF)
-    k_sc[i] = key
-    vt_sc[i] = vt32.astype(BF)
-    first_key = first_ref[0]
-
-    def tile(masked, j, carry):
-        run_max, run_sum, acc = carry
-        s = dot(k_sc[j], qt)
-        if masked:
-            s = jnp.where(visible(j, i, rows, first_key), s, neg_big)
-        new_max = jnp.maximum(run_max, jnp.max(s, axis=0, keepdims=True))
-        p = jnp.exp(s - new_max)
-        factor = jnp.exp(run_max - new_max)
-        run_sum = run_sum * factor + jnp.sum(p, axis=0, keepdims=True)
-        acc = acc * factor + dot(vt_sc[j], p.astype(BF))
-        return new_max, run_sum, acc
-
-    carry = (
-        jnp.full((1, rows), neg_big, F32),
-        jnp.zeros((1, rows), F32),
-        jnp.zeros((HD, rows), F32),
-    )
-    carry = tile(True, i, carry)
-    edge = (i == last) | (i == 0)
-    carry = lax.fori_loop(1, jnp.where(edge, 1, i), functools.partial(tile, False), carry)
-    carry = lax.fori_loop(
-        jnp.where(edge, 1, i), i, functools.partial(tile, True), carry
-    )
-    carry = lax.fori_loop(0, jnp.minimum(i, 1), functools.partial(tile, True), carry)
-    run_max, run_sum, acc = carry
-    out = acc / run_sum
-    o32_ref[0] = out
-    o_ref[0] = out.astype(BF)
-    lse_ref[0] = run_max + jnp.log(run_sum)
-
-
-def attend_call(h_all, wt, scale_col, first_key):
-    n, rows, width = h_all.shape
-
-    def blk(*shape):
-        return pl.BlockSpec((1, *shape), lambda i: (i, 0, 0))
-
-    def whole(a):
-        return pl.BlockSpec(a.shape, lambda i: (0,) * a.ndim)
-
-    def out(dtype, *shape):
-        return jax.ShapeDtypeStruct((n, *shape), dtype)
-
-    return pl.pallas_call(
-        attend_kernel,
-        grid=(n,),
-        out_shape=[
-            out(BF, HD, rows), out(F32, HD, rows), out(F32, 1, rows), out(BF, HD, rows),
-            out(BF, rows, HD), out(BF, HD, rows), out(BF, rows, HD), out(BF, rows, HD),
-            out(F32, HD, rows),
-        ],
-        in_specs=[blk(rows, width), whole(wt), whole(scale_col), blk(1, rows)],
-        out_specs=[
-            blk(HD, rows), blk(HD, rows), blk(1, rows), blk(HD, rows), blk(rows, HD),
-            blk(HD, rows), blk(rows, HD), blk(rows, HD), blk(HD, rows),
-        ],
-        scratch_shapes=[pltpu.VMEM((n, rows, HD), BF), pltpu.VMEM((n, HD, rows), BF)],
-        compiler_params=pltpu.CompilerParams(vmem_limit_bytes=48 * 2**20),
-        name="attend",
-    )(h_all, wt, scale_col, first_key)
-
-
-def attend_back_kernel(
+def backward_kernel(
     h_ref, scale_ref, first_ref, k_ref, v_ref, kt_ref, raw_ref, q_ref, qt_ref, gt_ref, o_ref, lse_ref,
     d_ref, dw_ref, ds_ref,
-    g_sc, delta_sc, dq_sc, scale_sc,
+    g_sc, delta_sc, dq_sc, scale_sc, dk_sc, dv_sc,
 ):
-    j = pl.program_id(0)
-    last = pl.num_programs(0) - 1
-    rows = h_ref.shape[1]
-
-    @pl.when(j == 0)
-    def _():
-        def prepare(i, c):
-            g = gt_ref[i].astype(F32)
-            g_sc[i] = g.T.astype(BF)
-            delta_sc[i] = jnp.sum(g * o_ref[i], axis=0, keepdims=True)
-            dq_sc[i] = jnp.zeros((HD, rows), F32)
-            return c
-
-        lax.fori_loop(0, last + 1, prepare, 0)
-        scale_sc[...] = jnp.zeros_like(scale_sc)
-        dw_ref[...] = jnp.zeros_like(dw_ref)
-
-    key, value, kt = k_ref[0], v_ref[0], kt_ref[0]
-
-    def tile(masked, i, carry):
-        dk, dv = carry
-        s = dot(key, qt_ref[i])
+    units, rows = h_ref.shape[:2]
+
+    def prepare(i, c):
+        g = jnp.concatenate([gt_ref[2 * i], gt_ref[2 * i + 1]], axis=1).astype(F32)
+        g_sc[i] = g.T.astype(BF)
+        delta_sc[i] = jnp.sum(g * o_ref[i], axis=0, keepdims=True)
+        dq_sc[i] = jnp.zeros((HD, rows), F32)
+        return c
+
+    lax.fori_loop(0, units, prepare, 0)
+    scale_sc[...] = jnp.zeros_like(scale_sc)
+    dw_ref[...] = jnp.zeros_like(dw_ref)
+
+    def pair(masked, j, i):
+        s = dot(k_ref[j], qt_ref[i])
         if masked:
             s = jnp.where(visible(j, i, rows, first_ref[i]), s, neg_big)
-        p = jnp.exp(s - lse_ref[i])
-        dv = dv + dot(p.astype(BF), g_sc[i])
-        dp = dot(value, gt_ref[i])
+        p = jnp.exp2(s - lse_ref[i])
+        dv_sc[...] += dot(p.astype(BF), g_sc[i])
+        g = jnp.concatenate([gt_ref[2 * i], gt_ref[2 * i + 1]], axis=1)
+        dp = dot(v_ref[j], g)
         ds = (p * (dp - delta_sc[i])).astype(BF)
-        dk = dk + dot(ds, q_ref[i])
-        dq_sc[i] += dot(kt, ds)
-        return dk, dv
-
-    carry = (jnp.zeros((rows, HD), F32), jnp.zeros((rows, HD), F32))
-    carry = tile(True, j, carry)
-    inner_end = jnp.where(j == 0, 1, last)
-    carry = lax.fori_loop(j + 1, inner_end, functools.partial(tile, False), carry)
-    carry = lax.fori_loop(
-        jnp.maximum(j + 1, inner_end), last + 1, functools.partial(tile, True), carry
-    )
-    dk, dv = carry
-    dq = dq_sc[j]
-    scale_sc[...] += dq * raw_ref[0]
-    grads = jnp.concatenate([dq * scale_ref[...], dk.T, dv.T], axis=0).astype(BF)
-    d_ref[0] = grads
-    dw_ref[...] += dot(grads, h_ref[0])
-
-    @pl.when(j == last)
-    def _():
-        ds_ref[...] = jnp.sum(scale_sc[...], axis=1, keepdims=True)
-
-
-def attend_back_call(h_all, scale_col, first_key, k, v, kt, raw, q, qt, gt, o32, lse):
+        dk_sc[...] += dot(ds, q_ref[i])
+        dq_sc[i] += dot(kt_ref[j], ds)
+
+    def column(j, c):
+        dk_sc[...] = jnp.zeros_like(dk_sc)
+        dv_sc[...] = jnp.zeros_like(dv_sc)
+        pair(True, j, j)
+
+        def plain(i, c2):
+            pair(False, j, i)
+            return c2
+
+        def edge(i, c2):
+            pair(True, j, i)
+            return c2
+
+        end = jnp.where(j == 0, 1, units - 1)
+        lax.fori_loop(j + 1, end, plain, 0)
+        lax.fori_loop(jnp.maximum(j + 1, end), units, edge, 0)
+        dq = dq_sc[j]
+        scale_sc[...] += dq * raw_ref[j]
+        grads = jnp.concatenate(
+            [dq * scale_ref[...], dk_sc[...].T, dv_sc[...].T], axis=0
+        ).astype(BF)
+        d_ref[2 * j] = grads[:, : rows // 2]
+        d_ref[2 * j + 1] = grads[:, rows // 2 :]
+        dw_ref[...] += dot(grads, h_ref[j])
+        return c
+
+    lax.fori_loop(0, units, column, 0)
+    ds_ref[...] = jnp.sum(scale_sc[...], axis=1, keepdims=True)
+
+
+def backward_call(h_all, scale_col, first_key, k, v, kt, raw, q, qt, gt, o32, lse):
     n, rows, width = h_all.shape
-
-    def blk(*shape):
-        return pl.BlockSpec((1, *shape), lambda i: (i, 0, 0))
-
-    def whole(a):
-        return pl.BlockSpec(a.shape, lambda i: (0,) * a.ndim)
-
+    args = (h_all, scale_col, first_key, k, v, kt, raw, q, qt, gt, o32, lse)
     return pl.pallas_call(
-        attend_back_kernel,
-        grid=(n,),
+        backward_kernel,
         out_shape=[
-            jax.ShapeDtypeStruct((n, 3 * HD, rows), BF),
+            jax.ShapeDtypeStruct((H, 3 * HD, rows // 2), BF),
             jax.ShapeDtypeStruct((3 * HD, width), F32),
             jax.ShapeDtypeStruct((HD, 1), F32),
         ],
-        in_specs=[
-            blk(rows, width), whole(scale_col), whole(first_key), blk(rows, HD), blk(rows, HD),
-            blk(HD, rows), blk(HD, rows), whole(q), whole(qt), whole(gt), whole(o32), whole(lse),
-        ],
-        out_specs=[
-            blk(3 * HD, rows),
-            pl.BlockSpec((3 * HD, width), lambda i: (0, 0)),
-            pl.BlockSpec((HD, 1), lambda i: (0, 0)),
-        ],
+        in_specs=[VMEM] * len(args),
+        out_specs=[VMEM] * 3,
         scratch_shapes=[
             pltpu.VMEM((n, rows, HD), BF),
             pltpu.VMEM((n, 1, rows), F32),
             pltpu.VMEM((n, HD, rows), F32),
             pltpu.VMEM((HD, rows), F32),
+            pltpu.VMEM((rows, HD), F32),
+            pltpu.VMEM((rows, HD), F32),
         ],
-        compiler_params=pltpu.CompilerParams(vmem_limit_bytes=48 * 2**20),
-        name="attend_back",
-    )(h_all, scale_col, first_key, k, v, kt, raw, q, qt, gt, o32, lse)
+        compiler_params=pltpu.CompilerParams(vmem_limit_bytes=56 * 2**20),
+        cost_estimate=pl.CostEstimate(flops=40 * 10**9, bytes_accessed=30 * 2**20, transcendentals=10**7),
+        name="backward",
+    )(*args)
 
 
 def joined(own, other, fs):
@@ -829,14 +885,16 @@
     starts = doc_starts[0]
     first_key = jnp.max(
         jnp.where(starts[None, :] <= positions[:, None], starts[None, :], 0), axis=1
-    ).reshape(H, 1, rows)
+    ).reshape(UNITS, 1, 2 * rows)
     scale_col = (query_scale / math.sqrt(HD))[:, None]
 
-    h_all, wt_all, gain_full, out_o, inner_o, outer_o = gather_call(
-        tok, gains, wt, (out_weight, inner_weight, outer_weight)
-    )
-    o_t, o32, lse, qt, q, kt, k, v, raw = attend_call(h_all, wt_all, scale_col, first_key)
-    attn_t, query_o, key_o, value_o = swap_call(2, o_t, (query_weight, key_weight, value_weight))
+    (
+        h_all, gain_full, attn_t, o32, lse, qt, q, kt, k, v, raw,
+        out_o, inner_o, outer_o, query_o, key_o,
+    ) = forward_call(
+        tok, gains, wt, scale_col, first_key,
+        (out_weight, inner_weight, outer_weight, query_weight, key_weight),
+    )
     attn_t = attn_t.reshape(width, rows)
 
     out_full = joined(out_weight, out_o, fs)
@@ -860,12 +918,12 @@
         cot.astype(F32) + norm_back(grad_hidden_two * gain_two, normed_two, scale_two)
     ).astype(BF)
     grad_att_t = dot(out_full, grad_resid, NT).astype(BF).reshape(H, HD, rows)
-    (g_t,) = swap_call(3, grad_att_t)
+    g_t, value_o = swap_call(3, grad_att_t, (value_weight,))
     grad_outer = dot(active, cot, TN).astype(BF)
     grad_inner = dot(hidden_two, grad_inner_pre, TN).astype(BF)
     grad_outw = dot(attn_t, grad_resid).astype(BF)
 
-    d_all, dw, dscale = attend_back_call(
+    d_all, dw, dscale = backward_call(
         h_all, scale_col, first_key, k, v, kt, raw, q, qt, g_t, o32, lse
     )
     half = width // 2

time: 646 us -> 530 us (0.82)
  Pallas kernels: 342 us -> 242 us
  local copies, waits for them, and re-layouts: 53.3 us -> 27.7 us
  waiting for transfers between devices: 127 us -> 141 us
    pallas_call x3 -> x2, Pallas kernels: 140 us -> 85.4 us  [swap_call(): pl.pallas_call(functools.partial(swap_kernel, n_w, has_y), out_shape=[jax...]
    pallas_call x3 -> x2, Pallas kernels: 202 us -> 156 us  [the longest x1 114 us: forward_call(): pl.pallas_call(functools.partial(forward_kernel, n_w), out_shape=shapes,...]
    all_gather x1, waiting for transfers between devices: 0.01 us -> 45.2 us  [fast_local(): lax.all_gather(dw_sum, 'ctx', axis=0, tiled=False).reshape(H, 3, HD, half)]
    reduce_scatter x3, waiting for transfers between devices: 127 us -> 95.3 us  [fast_local(): lax.psum_scatter(g, 'fs', scatter_dimension=0, tiled=True)]
    unnamed x96 -> x46, local copies, waits for them, and re-layouts: 40.9 us -> 13.6 us
  transfers between devices with their start and end apart: 5 -> 5, of which waited for: 3 -> 3; matrix products, arithmetic and copies ran while one was open for 6% -> 8% of each run, Pallas kernels for 23% -> 24%
where the time goes in v2:
time: 530 us; the launch traced here: 529 us
  Pallas kernels  242 us (46%)
  waiting for transfers between devices  141 us (27%)
  blocking collectives  51.3 us (10%)
  matrix products  33.2 us (6%)
  local copies, waits for them, and re-layouts  27.7 us (5%)
  other arithmetic  20.4 us (4%)
  between operations  14.1 us (3%)
    pallas_call x1, Pallas kernels, forward_call(): pl.pallas_call(functools.partial(forward_kernel, n_w), out_shape=shapes,...  114 us
    reduce_scatter x3, waiting for transfers between devices, fast_local(): lax.psum_scatter(g, 'fs', scatter_dimension=0, tiled=True)  95.3 us
    pallas_call x2, Pallas kernels, swap_call(): pl.pallas_call(functools.partial(swap_kernel, n_w, has_y), out_shape=[jax...  85.4 us
    psum x1, blocking collectives, fast_local(): lax.psum(jnp.concatenate([grad_gain_one, grad_gain_two, dscale[:, 0]]), (...  51.3 us
    all_gather x1, waiting for transfers between devices, fast_local(): lax.all_gather(dw_sum, 'ctx', axis=0, tiled=False).reshape(H, 3, HD, half)  45.2 us
    pallas_call x1, Pallas kernels, backward_call(): pl.pallas_call(backward_kernel, out_shape=[jax.ShapeDtypeStruct((H, 3 * H...  42.7 us
    dot_general x12, matrix products, dot(): return lax.dot_general(a, b, (dims, ((), ())), preferred_element_type=F32)  33.2 us
    unnamed x46, local copies, waits for them, and re-layouts  13.6 us
  transfers between devices with their start and end apart: 5, of which 3 were waited for; matrix products, arithmetic and copies ran while one was open for 8% of the time, Pallas kernels for 24%

profile of v2, /device:TPU:0, one launch (start us, length us, event | category | flops | bytes accessed | tf_op | source)
XLA Modules:
  0.0 529.2 jit_solution(5036352525710666180)
XLA Ops:
  7.2 0.7 multiply_bitcast_fusion
  7.9 0.7 stack.9
  8.6 0.7 stack.10
  9.3 1.4 select_reduce_fusion
  10.6 0.7 copy.47.scale_ref
  11.4 1.1 constant_dynamic-slice_fusion.2
  12.6 1.2 constant_dynamic-slice_fusion
  14.1 0.6 pad_maximum_fusion.2.gain_ref
  14.7 0.7 pad_maximum_fusion.wt_ref
  15.5 113.5 %forward.1 = (bf16[8,512,1280]{2,1,0:T(8,128)(2,1)}, f32[2,1280]{1,0:T(2,128)}, bf16[16,80,256]{2,1,0:T(8,128)(2,1)}, f32[8,80,512]{2,1,0:T(8,128)}, f32[8,1,512...) custom-call(bf16[256,1280]{1,0:T(8,128)(2,1)} %bitcast.68, ...), custom_call_target="tpu_custom_call" | custom-call | tf_op jit(solution)/shard_map/forward/pallas_call | solution.py:684
  129.0 0.8 slice_reduce_fusion
  129.9 3.4 multiply_reduce_fusion.2
  133.4 1.1 fusion.42
  135.0 0.5 copy-done.13
  135.5 1.3 fusion.25
  136.9 2.9 convolution_convert_fusion.1
  139.8 4.5 multiply_reduce_fusion
  144.7 0.8 copy-done.1
  145.5 2.7 convolution_convert_fusion.2
  148.3 4.3 convolution_convert_fusion
  152.9 5.0 convolution_convert_fusion.3
  157.9 42.2 %swap3.1 = (bf16[16,80,256]{2,1,0:T(8,128)(2,1)}, bf16[640,1280]{1,0:T(8,128)(2,1)}) custom-call(bf16[16,80,256]{2,1,0:T(8,128)(2,1)} %bitcast.73, bf16[640,1280]{1,0:T(8,128)(2,1)} %refs_1_.1), custom_call_target="tpu_custom_call" | custom-call | tf_op jit(solution)/shard_map/swap3/pallas_call | solution.py:760
  200.2 47.6 %reduce-scatter.4.cloned.1.call-done = bf16[640,1280]{1,0:T(8,128)(2,1)} async-done(((bf16[1280,1280]{1,0:T(8,128)(2,1)}), bf16[640,1280]{1,0:T(8,128)(2,1)}) %reduce-scatter.4.cloned.1.call-update) | async-done | bytes 1638416 | tf_op jit(solution)/shard_map/reduce_scatter | solution.py:952
  247.8 47.6 %reduce-scatter.8.cloned.1.call-done = bf16[640,1280]{1,0:T(8,128)(2,1)} async-done(((bf16[1280,1280]{1,0:T(8,128)(2,1)}), bf16[640,1280]{1,0:T(8,128)(2,1)}) %reduce-scatter.8.cloned.1.call-update) | async-done | bytes 1638416 | tf_op jit(solution)/shard_map/reduce_scatter | solution.py:952
  295.5 42.7 %backward.1 = (bf16[16,240,256]{2,1,0:T(8,128)(2,1)}, f32[240,1280]{1,0:T(8,128)}, f32[80,1]{1,0:T(8,128)}) custom-call(bf16[8,512,1280]{2,1,0:T(8,128)(2,1)} %get-tuple-element.39.h_ref, f32[80,1]{1,0:T(8,128)} %copy.47.scale_ref, s32[8,1,512]{2,1,0:T(1,128)} %bitcast.81, bf16[8,512,80]{2,1,0:T(8,128)(2,1)} %get-tuple-element.40.k_ref, ...), custom_call_target="tpu_custom_call" | custom-call | flops 40000000000 | bytes 31457280 | tf_op jit(solution)/shard_map/backward/pallas_call | solution.py:841
  338.2 1.8 dynamic-slice_convert_fusion.refs_1_
  340.0 43.2 %swap4.1 = (bf16[16,240,256]{2,1,0:T(8,128)(2,1)}, bf16[240,640]{1,0:T(8,128)(2,1)}) custom-call(bf16[16,240,256]{2,1,0:T(8,128)(2,1)} %get-tuple-element.49.refs_0_, bf16[240,640]{1,0:T(8,128)(2,1)} %dynamic-slice_convert_fusion.refs_1_), custom_call_target="tpu_custom_call" | custom-call | tf_op jit(solution)/shard_map/swap4/pallas_call | solution.py:760
  383.2 1.9 add_convert_fusion.1
  385.6 1.8 fusion.53
  388.1 1.1 fusion
  390.0 1.1 fusion.22
  391.4 0.5 copy-done.17
  391.9 2.3 fusion.36
  394.3 51.3 %psum.31 = f32[2640]{0:T(1024)S(1)} all-reduce(f32[2640]{0:T(1024)S(1)} %pad_maximum_fusion.1), channel_id=1, replica_groups=mesh['ctx'=16,'fs'=2] {'ctx','fs'}, use_global_device_ids=true, to_apply=%region_13.14 | all-reduce | flops 2640 | bytes 21120 | tf_op jit(solution)/shard_map/psum | solution.py:955
  445.6 0.7 fusion.54
  446.2 0.5 slice_multiply_fusion
  446.8 2.7 fusion.38
  449.5 3.4 fusion.27
  452.9 3.5 convert_element_type.107
  456.4 2.0 convert_element_type.109
  458.4 2.0 convert_element_type.111
  460.4 45.2 %all-gather.3.cloned.1.call-done = bf16[3840,640]{1,0:T(8,128)(2,1)} async-done(((bf16[240,640]{1,0:T(8,128)(2,1)}), bf16[3840,640]{1,0:T(8,128)(2,1)}) %all-gather.3.cloned.1.call-update) | async-done | bytes 4915216 | tf_op jit(solution)/shard_map/all_gather | solution.py:949
  505.6 4.5 fusion.52
  510.5 3.0 copy.55
  513.5 1.6 convert_bitcast_fusion.1
  515.1 3.0 copy.54
  518.1 1.6 convert_bitcast_fusion.2
  519.7 3.0 copy.53
  (61 shorter events, 4.5 us)
Async XLA Ops:
  7.2 193.0 %reduce-scatter.6.cloned.1.call-start = ((), (), s32[]{:S(2)}) async-start(), calls=%async_computation.4 | async-start | bytes 4915200 | tf_op jit(solution)/shard_map/reduce_scatter | solution.py:952
  15.5 114.4 %copy-start = (bf16[1,256,1280]{2,1,0:T(8,128)(2,1)S(1)}, bf16[1,256,1280]{2,1,0:T(8,128)(2,1)}, u32[]{:S(2)}) copy-start(bf16[1,256,1280]{2,1,0:T(8,128)(2,1)} %param.12) | copy-start | bytes 1966084
  15.5 114.4 %copy-start.6 = (bf16[640,1280]{1,0:T(8,128)(2,1)S(1)}, bf16[640,1280]{1,0:T(8,128)(2,1)}, u32[]{:S(2)}) copy-start(bf16[640,1280]{1,0:T(8,128)(2,1)} %rest_0_.1) | copy-start | bytes 4915204
  129.9 3.5 copy-start.5
  129.9 3.5 copy-start.18
  133.4 1.4 copy-start.7
  133.4 1.6 copy-start.11
  133.4 2.1 copy-start.13
  134.6 2.3 copy-start.19
  139.7 108.1 %reduce-scatter.4.cloned.1.call-start = ((), (), s32[]{:S(2)}) async-start(), calls=%async_computation.3 | async-start | bytes 4915200 | tf_op jit(solution)/shard_map/reduce_scatter | solution.py:952
  144.3 1.2 copy-start.1
  148.3 147.2 %reduce-scatter.8.cloned.1.call-start = ((), (), s32[]{:S(2)}) async-start(), calls=%async_computation.5 | async-start | bytes 4915200 | tf_op jit(solution)/shard_map/reduce_scatter | solution.py:952
  152.7 300.2 %all-reduce.3.cloned.1.call-start = ((), (), s32[]{:S(2)}) async-start(), calls=%async_computation.7 | async-start | bytes 9830400 | tf_op jit(solution)/shard_map/psum | solution.py:952
  295.5 210.1 %all-gather.3.cloned.1.call-start = ((), (), s32[]{:S(2)}) async-start(), calls=%async_computation.6 | async-start | bytes 5222400 | tf_op jit(solution)/shard_map/all_gather | solution.py:949
  340.0 45.2 %copy-start.12 = (f32[80,1]{1,0:T(8,128)S(1)}, f32[80,1]{1,0:T(8,128)}, u32[]{:S(2)}) copy-start(f32[80,1]{1,0:T(8,128)} %get-tuple-element.56) | copy-start | bytes 964
  385.5 2.0 copy-start.2
  385.5 2.5 copy-start.16
  388.1 1.4 copy-start.3
  388.1 1.9 copy-start.15
  390.0 1.4 copy-start.4
  390.0 2.0 copy-start.17
  446.7 2.7 copy-start.8
  446.8 2.7 copy-start.14
  452.9 3.5 copy-start.10
  456.4 2.0 copy-start.9
Sparse Core Ops, SparseCore 0:
  139.9 60.1 reduce-scatter.5
  203.0 44.7 reduce-scatter.3
  250.7 44.7 reduce-scatter.7
  299.8 148.3 all-reduce.2
  451.1 54.5 all-gather.2

commit v3 on v2

--- a/solution.py
+++ b/solution.py
@@ -711,87 +711,169 @@
     )(tok, gains, wt, scale_col, first_key, *weights)
 
 
-def swap_kernel(n_w, has_y, *refs):
-    x_ref = refs[0]
-    own = refs[1 : 1 + n_w]
-    y_ref = refs[1 + n_w : 1 + n_w + has_y]
-    at = 1 + n_w + has_y
-    o_ref = refs[at]
-    other = refs[at + 1 : at + 1 + n_w]
-    y_out = refs[at + 1 + n_w : at + 1 + n_w + has_y]
-    ssem, rsem, wssem, wrsem, lsem = refs[at + 1 + n_w + has_y :]
+def half_rows(start, size, align):
+    return pl.ds(pl.multiple_of(start, align), size)
+
+
+def backward_kernel(
+    n_w, gt_ref, *rest,
+):
+    dense = rest[:3]
+    own = rest[3 : 3 + n_w]
+    at = 3 + n_w
+    h_ref, scale_ref, first_ref, k_ref, v_ref, kt_ref, raw_ref, q_ref, qt_ref, o_ref, lse_ref = rest[
+        at : at + 11
+    ]
+    at += 11
+    got_ref, piece_ref, ds_ref = rest[at : at + 3]
+    other = rest[at + 3 : at + 3 + n_w]
+    (
+        g_in, g_sc, delta_sc, dq_sc, scale_sc, dk_sc, dv_sc, d_sc, dw_sc, dw_out, dw_got,
+        s1, r0, ra, rb, r2, rz,
+        gsend, grecv, qsend, qrecv, ksend, krecv, wssem, wrsem, dsend, drecv, psend, precv, lsem,
+    ) = rest[at + 3 + n_w :]
     me, fs, z, x, k = place()
+    sib, xn, yn = (me + 1 - 2 * k, fs), (me + 2 - 4 * x, fs), (me, 1 - fs)
+    units, rows = h_ref.shape[:2]
+    block = rows // 2
+    n_g = 3
+    part = s1.shape[2]
+    width = s1.shape[3]
+    cols = width // 2
     bar = pltpu.get_barrier_semaphore()
     for i in range(1, H):
         signal((lax.rem(me + i, H), fs))
-    if n_w or has_y:
-        signal((me, 1 - fs))
-    pl.semaphore_wait(bar, H - 1 + (1 if n_w or has_y else 0))
-    copies = []
-    for i in range(1, H):
-        t = lax.rem(me + i, H)
-        c = remote(x_ref.at[t], o_ref.at[me], ssem.at[i], rsem.at[i], (t, fs))
+    signal(yn)
+
+    def mine(g, f):
+        return pltpu.make_async_copy(
+            dense[g].at[half_rows(f * 2 * part + k * part, part, 64)], s1.at[g, f], lsem.at[g * 2 + f]
+        )
+
+    def theirs(g, f):
+        return remote(
+            dense[g].at[half_rows(f * 2 * part + (1 - k) * part, part, 64)],
+            r0.at[g, f], dsend.at[g * 2 + f], drecv.at[g * 2 + f], sib,
+        )
+
+    for g in range(n_g):
+        for f in range(2):
+            mine(g, f).start()
+    pl.semaphore_wait(bar, H)
+
+    def lanes(b):
+        return half_rows(lax.rem(b, 2) * block, block, 128)
+
+    def g_copy(b, t):
+        return remote(
+            gt_ref.at[b], g_in.at[t // 2, :, lanes(t)], gsend.at[b], grecv.at[t], (b, fs)
+        )
+
+    def g_start(n, c):
+        g_copy(lax.rem(me + n, H), me).start()
+        return c
+
+    lax.fori_loop(1, H, g_start, 0)
+    g_here = pltpu.make_async_copy(gt_ref.at[me], g_in.at[me // 2, :, lanes(me)], lsem.at[6])
+    g_here.start()
+    for g in range(n_g):
+        for f in range(2):
+            theirs(g, f).start()
+    first, second = weight_pull(own, other, k, fs, me, wssem, wrsem)
+    for c in first:
         c.start()
-        copies.append(c)
-    here = pltpu.make_async_copy(x_ref.at[me], o_ref.at[me], lsem)
-    here.start()
-    if has_y:
-        c = remote(y_ref[0], y_out[0], ssem.at[0], rsem.at[0], (me, 1 - fs))
-        c.start()
-        copies.append(c)
-    if n_w:
-        first, second = weight_pull(own, other, k, fs, me, wssem, wrsem)
-        for c in first:
-            c.start()
-        for i in range(n_w):
-            first[i].wait_recv()
-            second[i].start()
-        for i in range(n_w):
-            first[i].wait_send()
-            second[i].wait()
-    for c in copies:
-        c.wait()
-    here.wait()
-
-
-def swap_call(cid, x, weights=(), y=None):
-    n_w, has_y = len(weights), int(y is not None)
-    args = [x, *weights] + ([y] if has_y else [])
-    out = pl.pallas_call(
-        functools.partial(swap_kernel, n_w, has_y),
-        out_shape=[jax.ShapeDtypeStruct(a.shape, a.dtype) for a in args],
-        in_specs=[ANY] * len(args),
-        out_specs=[ANY] * len(args),
-        scratch_shapes=[
-            pltpu.SemaphoreType.DMA((H,)),
-            pltpu.SemaphoreType.DMA((H,)),
-            pltpu.SemaphoreType.DMA((max(1, 2 * n_w),)),
-            pltpu.SemaphoreType.DMA((max(1, 2 * n_w),)),
-            pltpu.SemaphoreType.DMA,
-        ],
-        compiler_params=pltpu.CompilerParams(collective_id=cid, has_side_effects=True),
-        name="swap%d" % cid,
-    )(*args)
-    return out
-
-
-def backward_kernel(
-    h_ref, scale_ref, first_ref, k_ref, v_ref, kt_ref, raw_ref, q_ref, qt_ref, gt_ref, o_ref, lse_ref,
-    d_ref, dw_ref, ds_ref,
-    g_sc, delta_sc, dq_sc, scale_sc, dk_sc, dv_sc,
-):
-    units, rows = h_ref.shape[:2]
+
+    top, bottom = slice(0, part // 2), slice(part // 2, part)
+    x_here = half_rows(x * cols, cols, 128)
+    x_there = half_rows((1 - x) * cols, cols, 128)
+    up_a = remote(s1.at[:, 1 - fs, top, :], ra, psend.at[0], precv.at[0], yn)
+    up_b = remote(s1.at[:, :, bottom, x_there], rb, psend.at[1], precv.at[1], xn)
+    two_a = remote(s1.at[:, fs, top, x_there], r2.at[:, top], psend.at[2], precv.at[2], xn)
+    two_b = remote(s1.at[:, 1 - fs, bottom, x_here], r2.at[:, bottom], psend.at[3], precv.at[3], yn)
+    slab = part // 4
+
+    def z_copy(t, slot, sem):
+        return remote(
+            s1.at[:, fs, half_rows(t * slab, slab, 16), x_here],
+            rz.at[slot], psend.at[4 + sem], precv.at[4 + slot], (me + 4 * (t - z), fs),
+        )
+
+    for g in range(n_g):
+        for f in range(2):
+            mine(g, f).wait()
+            theirs(g, f).wait()
+
+            def add(i, c, g=g, f=f):
+                r = half_rows(i * 32, 32, 32)
+                s1[g, f, r, :] += r0[g, f, r, :]
+                return c
+
+            lax.fori_loop(0, part // 32, add, 0)
+    up_a.start()
+    up_b.start()
+
+    def after_one():
+        up_a.wait()
+        up_b.wait()
+        for g in range(n_g):
+
+            def add(i, c, g=g):
+                r = half_rows(i * 32, 32, 32)
+                s1[g, fs, r, :] += ra[g, r, :]
+                low = half_rows(part // 2 + i * 32, 32, 32)
+                for f in range(2):
+                    s1[g, f, low, x_here] += rb[g, f, r, :]
+                return c
+
+            lax.fori_loop(0, part // 64, add, 0)
+        two_a.start()
+        two_b.start()
+
+    def after_two():
+        two_a.wait()
+        two_b.wait()
+        for g in range(n_g):
+
+            def add(i, c, g=g):
+                r = half_rows(i * 32, 32, 32)
+                s1[g, fs, r, x_here] += r2[g, r, :]
+                return c
+
+            lax.fori_loop(0, part // 32, add, 0)
+        for d in range(1, 4):
+            t = lax.rem(z + d, 4)
+            z_copy(t, z, d).start()
+
+    def after_three():
+        for d in range(1, 4):
+            t = lax.rem(z + d, 4)
+            z_copy(t, t, d).wait()
+        here = half_rows(z * slab, slab, 16)
+        for g in range(n_g):
+            total = s1[g, fs, here, x_here].astype(F32)
+            for d in range(1, 4):
+                total = total + rz[lax.rem(z + d, 4), g].astype(F32)
+            piece_ref[g] = total.astype(BF)
+
+    scale_sc[...] = jnp.zeros_like(scale_sc)
+    dw_sc[...] = jnp.zeros_like(dw_sc)
+
+    def g_taken(n, c):
+        b = lax.rem(me + n, H)
+        g_copy(b, b).wait()
+        return c
+
+    g_here.wait()
+    lax.fori_loop(1, H, g_taken, 0)
 
     def prepare(i, c):
-        g = jnp.concatenate([gt_ref[2 * i], gt_ref[2 * i + 1]], axis=1).astype(F32)
+        g = g_in[i].astype(F32)
         g_sc[i] = g.T.astype(BF)
         delta_sc[i] = jnp.sum(g * o_ref[i], axis=0, keepdims=True)
         dq_sc[i] = jnp.zeros((HD, rows), F32)
         return c
 
     lax.fori_loop(0, units, prepare, 0)
-    scale_sc[...] = jnp.zeros_like(scale_sc)
-    dw_ref[...] = jnp.zeros_like(dw_ref)
 
     def pair(masked, j, i):
         s = dot(k_ref[j], qt_ref[i])
@@ -799,13 +881,28 @@
             s = jnp.where(visible(j, i, rows, first_ref[i]), s, neg_big)
         p = jnp.exp2(s - lse_ref[i])
         dv_sc[...] += dot(p.astype(BF), g_sc[i])
-        g = jnp.concatenate([gt_ref[2 * i], gt_ref[2 * i + 1]], axis=1)
-        dp = dot(v_ref[j], g)
+        dp = dot(v_ref[j], g_in[i])
         ds = (p * (dp - delta_sc[i])).astype(BF)
         dk_sc[...] += dot(ds, q_ref[i])
         dq_sc[i] += dot(kt_ref[j], ds)
 
-    def column(j, c):
+    def out(b, lo, n):
+        return d_sc.at[b // 2, pl.ds(lo, n), :, lanes(b)]
+
+    def to(t, lo, n):
+        return got_ref.at[pl.ds(lo, n), half_rows(t * HD, HD, 16)]
+
+    def kv_copy(b, t):
+        return remote(out(b, 1, 2), to(t, 1, 2), ksend.at[b], krecv.at[t], (b, fs))
+
+    def q_copy(b, t):
+        return remote(out(b, 0, 1), to(t, 0, 1), qsend.at[b], qrecv.at[t], (b, fs))
+
+    kv_here = pltpu.make_async_copy(out(me, 1, 2), to(me, 1, 2), lsem.at[7])
+    q_here = pltpu.make_async_copy(out(me, 0, 1), to(me, 0, 1), lsem.at[8])
+
+    def column(n, c):
+        j = lax.rem(me // 2 + n, units)
         dk_sc[...] = jnp.zeros_like(dk_sc)
         dv_sc[...] = jnp.zeros_like(dv_sc)
         pair(True, j, j)
@@ -821,44 +918,381 @@
         end = jnp.where(j == 0, 1, units - 1)
         lax.fori_loop(j + 1, end, plain, 0)
         lax.fori_loop(jnp.maximum(j + 1, end), units, edge, 0)
-        dq = dq_sc[j]
-        scale_sc[...] += dq * raw_ref[j]
-        grads = jnp.concatenate(
-            [dq * scale_ref[...], dk_sc[...].T, dv_sc[...].T], axis=0
-        ).astype(BF)
-        d_ref[2 * j] = grads[:, : rows // 2]
-        d_ref[2 * j + 1] = grads[:, rows // 2 :]
-        dw_ref[...] += dot(grads, h_ref[j])
+        d_sc[j, 1] = dk_sc[...].T.astype(BF)
+        d_sc[j, 2] = dv_sc[...].T.astype(BF)
+
+        def send(e, c2):
+            b = 2 * j + e
+
+            @pl.when(b != me)
+            def _():
+                kv_copy(b, me).start()
+
+            @pl.when(b == me)
+            def _():
+                kv_here.start()
+
+            return c2
+
+        lax.fori_loop(0, 2, send, 0)
+        for e in range(2):
+            dw_sc[1 + e] += dot(d_sc[j, 1 + e], h_ref[j])
+
+        @pl.when(n == 3)
+        def _():
+            after_one()
+
+        @pl.when(n == 6)
+        def _():
+            after_two()
+
         return c
 
     lax.fori_loop(0, units, column, 0)
+
+    def queries(n, c):
+        i = lax.rem(me // 2 + n, units)
+        dq = dq_sc[i]
+        scale_sc[...] += dq * raw_ref[i]
+        d_sc[i, 0] = (dq * scale_ref[...]).astype(BF)
+
+        def send(e, c2):
+            b = 2 * i + e
+
+            @pl.when(b != me)
+            def _():
+                q_copy(b, me).start()
+
+            @pl.when(b == me)
+            def _():
+                q_here.start()
+
+            return c2
+
+        lax.fori_loop(0, 2, send, 0)
+        return c
+
+    lax.fori_loop(0, units, queries, 0)
+    for i in range(n_w):
+        first[i].wait_recv()
+        second[i].start()
+
+    def query_weight(i, c):
+        dw_sc[0] += dot(d_sc[i, 0], h_ref[i])
+        return c
+
+    lax.fori_loop(0, units, query_weight, 0)
+    half = dw_out.shape[2]
+    dw_out[...] = dw_sc[:, :, half_rows((1 - fs) * half, half, 128)].astype(BF)
+    dw_copy = remote(dw_out, dw_got, psend.at[8], precv.at[8], yn)
+    dw_copy.start()
     ds_ref[...] = jnp.sum(scale_sc[...], axis=1, keepdims=True)
-
-
-def backward_call(h_all, scale_col, first_key, k, v, kt, raw, q, qt, gt, o32, lse):
+    after_three()
+    dw_copy.wait()
+    piece_ref[n_g:] = (dw_sc[:, :, half_rows(fs * half, half, 128)] + dw_got[...].astype(F32)).astype(BF)
+
+    def taken(n, c):
+        b = lax.rem(me + n, H)
+        kv_copy(b, b).wait()
+        q_copy(b, b).wait()
+        return c
+
+    lax.fori_loop(1, H, taken, 0)
+    kv_here.wait()
+    q_here.wait()
+    for i in range(n_w):
+        first[i].wait_send()
+        second[i].wait()
+
+
+def backward_call(gt, dense, weights, h_all, scale_col, first_key, k, v, kt, raw, q, qt, o32, lse):
+    n_w = len(weights)
     n, rows, width = h_all.shape
-    args = (h_all, scale_col, first_key, k, v, kt, raw, q, qt, gt, o32, lse)
+    vm = (h_all, scale_col, first_key, k, v, kt, raw, q, qt, o32, lse)
+    half = width // 2
+    part = dense[0].shape[0] // 4
+    sem = pltpu.SemaphoreType.DMA
     return pl.pallas_call(
-        backward_kernel,
+        functools.partial(backward_kernel, n_w),
         out_shape=[
-            jax.ShapeDtypeStruct((H, 3 * HD, rows // 2), BF),
-            jax.ShapeDtypeStruct((3 * HD, width), F32),
+            jax.ShapeDtypeStruct((3, H * HD, rows // 2), BF),
+            jax.ShapeDtypeStruct((6, part // 4, half), BF),
             jax.ShapeDtypeStruct((HD, 1), F32),
-        ],
-        in_specs=[VMEM] * len(args),
-        out_specs=[VMEM] * 3,
+        ]
+        + [jax.ShapeDtypeStruct(w.shape, BF) for w in weights],
+        in_specs=[ANY] * (4 + n_w) + [VMEM] * len(vm),
+        out_specs=[ANY, VMEM, VMEM] + [ANY] * n_w,
         scratch_shapes=[
+            pltpu.VMEM((n, HD, rows), BF),
             pltpu.VMEM((n, rows, HD), BF),
             pltpu.VMEM((n, 1, rows), F32),
             pltpu.VMEM((n, HD, rows), F32),
             pltpu.VMEM((HD, rows), F32),
             pltpu.VMEM((rows, HD), F32),
             pltpu.VMEM((rows, HD), F32),
+            pltpu.VMEM((n, 3, HD, rows), BF),
+            pltpu.VMEM((3, HD, width), F32),
+            pltpu.VMEM((3, HD, half), BF),
+            pltpu.VMEM((3, HD, half), BF),
+            pltpu.VMEM((3, 2, part, width), BF),
+            pltpu.VMEM((3, 2, part, width), BF),
+            pltpu.VMEM((3, part // 2, width), BF),
+            pltpu.VMEM((3, 2, part // 2, half), BF),
+            pltpu.VMEM((3, part, half), BF),
+            pltpu.VMEM((4, 3, part // 4, half), BF),
+            sem((H,)), sem((H,)), sem((H,)), sem((H,)), sem((H,)), sem((H,)),
+            sem((max(1, 2 * n_w),)), sem((max(1, 2 * n_w),)), sem((6,)), sem((6,)), sem((9,)), sem((9,)),
+            sem((9,)),
         ],
-        compiler_params=pltpu.CompilerParams(vmem_limit_bytes=56 * 2**20),
-        cost_estimate=pl.CostEstimate(flops=40 * 10**9, bytes_accessed=30 * 2**20, transcendentals=10**7),
+        compiler_params=pltpu.CompilerParams(
+            collective_id=2, has_side_effects=True, vmem_limit_bytes=60 * 2**20
+        ),
         name="backward",
-    )(*args)
+    )(gt, *dense, *weights, *vm)
+
+
+def final_kernel(
+    piece_ref, tok_ref, gr_ref, gain_ref, small_ref, d_ref,
+    qo_ref, ko_ref, vo_ref, qn_ref, kn_ref, vn_ref,
+    all_ref, tg_ref, sums_ref,
+    e_sc, small_out, small_in, small_y, small_got, ssem, rsem, vsend, vrecv, ysem, lsem,
+):
+    me, fs, z, x, k = place()
+    sib, xn, yn = (me + 1 - 2 * k, fs), (me + 2 - 4 * x, fs), (me, 1 - fs)
+    up, dn = (me + 4, fs), (me - 4, fs)
+    bar = pltpu.get_barrier_semaphore()
+    for i in range(1, H):
+        signal((lax.rem(me + i, H), fs))
+    signal(yn)
+    here = pltpu.make_async_copy(piece_ref, all_ref.at[me], lsem.at[0])
+    here.start()
+    pl.semaphore_wait(bar, H)
+
+    def cp(s, t, si, mine=False):
+        return remote(
+            piece_ref if mine else all_ref.at[s], all_ref.at[s], ssem.at[si], rsem.at[s], t
+        )
+
+    cp(me, xn, 0, True).start()
+
+    @pl.when(z < 3)
+    def _():
+        cp(me, up, 1, True).start()
+
+    @pl.when(z > 0)
+    def _():
+        cp(me, dn, 2, True).start()
+
+    cp(me, sib, 3, True).start()
+
+    half = qo_ref.shape[0]
+    for w, (a, b) in enumerate(((qo_ref, qn_ref), (ko_ref, kn_ref), (vo_ref, vn_ref))):
+        for r, m in ((fs, a), (1 - fs, b)):
+            rows = half_rows(r * half, half, 128)
+            term = dot(m[...], d_ref[w])
+            if w == 0:
+                e_sc[rows, :] = term
+            else:
+                e_sc[rows, :] += term
+    grad_hidden = e_sc[...].T
+    tokens = tok_ref[...].astype(F32)
+    scale = lax.rsqrt(jnp.mean(tokens * tokens, axis=-1, keepdims=True) + epsilon)
+    normed = tokens * scale
+    small_out[...] = small_ref[...]
+    small_out[0:1, :] = jnp.sum(grad_hidden * normed, axis=0, keepdims=True)
+
+    def v_copy(b, t):
+        return remote(small_out, small_in.at[t], vsend.at[b], vrecv.at[t], (b, fs))
+
+    def v_start(n, c):
+        v_copy(lax.rem(me + n, H), me).start()
+        return c
+
+    lax.fori_loop(1, H, v_start, 0)
+    e = grad_hidden * gain_ref[0:1, :]
+    tg_ref[...] = (
+        gr_ref[...].astype(F32) + scale * (e - normed * jnp.mean(e * normed, axis=-1, keepdims=True))
+    ).astype(BF)
+
+    xo = me + 2 - 4 * x
+
+    def column_arrival(d):
+        a = 4 + (d - 1) * 6
+
+        @pl.when(z >= d)
+        def _():
+            s = me - 4 * d
+            cp(s, dn, a).wait_recv()
+
+            @pl.when(z < 3)
+            def _():
+                cp(s, up, a).start()
+
+            cp(s, xn, a + 1).start()
+            cp(s, sib, a + 2).start()
+
+        @pl.when(z + d <= 3)
+        def _():
+            s = me + 4 * d
+            cp(s, up, a + 3).wait_recv()
+
+            @pl.when(z > 0)
+            def _():
+                cp(s, dn, a + 3).start()
+
+            cp(s, xn, a + 4).start()
+            cp(s, sib, a + 5).start()
+
+    def across_arrival(d):
+        @pl.when(z >= d)
+        def _():
+            s = xo - 4 * d
+            cp(s, xn, 0).wait_recv()
+            cp(s, sib, 22 + z - d).start()
+
+        @pl.when((z + d <= 3) & (d > 0))
+        def _():
+            s = xo + 4 * d
+            cp(s, xn, 0).wait_recv()
+            cp(s, sib, 22 + z + d).start()
+
+    column_arrival(1)
+
+    def v_taken(n, c):
+        b = lax.rem(me + n, H)
+        v_copy(b, b).wait()
+        return c
+
+    lax.fori_loop(1, H, v_taken, 0)
+
+    def v_add(n, total):
+        return total + small_in[lax.rem(me + n, H)]
+
+    small_y[...] = lax.fori_loop(1, H, v_add, small_out[...])
+    y_copy = remote(small_y, small_got, ysem.at[0], ysem.at[1], yn)
+    y_copy.start()
+    across_arrival(0)
+    column_arrival(2)
+    across_arrival(1)
+    y_copy.wait()
+    sums_ref[...] = small_y[...] + small_got[...]
+    column_arrival(3)
+    across_arrival(2)
+    across_arrival(3)
+
+    def from_sib(n, c):
+        cp(n * 2 + 1 - k, sib, 0).wait_recv()
+        return c
+
+    lax.fori_loop(0, UNITS, from_sib, 0)
+    here.wait()
+    cp(me, xn, 0, True).wait_send()
+
+    @pl.when(z < 3)
+    def _():
+        cp(me, up, 1, True).wait_send()
+
+    @pl.when(z > 0)
+    def _():
+        cp(me, dn, 2, True).wait_send()
+
+    cp(me, sib, 3, True).wait_send()
+
+    def sent(d, c):
+        a = 4 + (d - 1) * 6
+
+        @pl.when(z >= d)
+        def _():
+            s = me - 4 * d
+
+            @pl.when(z < 3)
+            def _():
+                cp(s, up, a).wait_send()
+
+            cp(s, xn, a + 1).wait_send()
+            cp(s, sib, a + 2).wait_send()
+
+        @pl.when(z + d <= 3)
+        def _():
+            s = me + 4 * d
+
+            @pl.when(z > 0)
+            def _():
+                cp(s, dn, a + 3).wait_send()
+
+            cp(s, xn, a + 4).wait_send()
+            cp(s, sib, a + 5).wait_send()
+
+        return c
+
+    lax.fori_loop(1, 4, sent, 0)
+
+    def sent_across(zz, c):
+        cp(xo + 4 * (zz - z), sib, 22 + zz).wait_send()
+        return c
+
+    lax.fori_loop(0, 4, sent_across, 0)
+
+
+def final_call(piece, tok, grad_resid, gain_full, small, d_all, own, other):
+    rows, width = tok.shape
+    sem = pltpu.SemaphoreType.DMA
+    return pl.pallas_call(
+        final_kernel,
+        out_shape=[
+            jax.ShapeDtypeStruct((H, *piece.shape), BF),
+            jax.ShapeDtypeStruct((rows, width), BF),
+            jax.ShapeDtypeStruct(small.shape, F32),
+        ],
+        in_specs=[VMEM] * 12,
+        out_specs=[ANY, VMEM, VMEM],
+        scratch_shapes=[
+            pltpu.VMEM((width, rows), F32),
+            pltpu.VMEM(small.shape, F32),
+            pltpu.VMEM((H, *small.shape), F32),
+            pltpu.VMEM(small.shape, F32),
+            pltpu.VMEM(small.shape, F32),
+            sem((26,)), sem((H,)), sem((H,)), sem((H,)), sem((2,)), sem((1,)),
+        ],
+        compiler_params=pltpu.CompilerParams(
+            collective_id=3, has_side_effects=True, vmem_limit_bytes=56 * 2**20
+        ),
+        name="final",
+    )(piece, tok, grad_resid, gain_full, small, d_all, *own, *other)
+
+
+def spread_kernel(dense_ref, heads_ref, dense_out, heads_out):
+    for zz in range(4):
+        for xx in range(2):
+            slab, cols = dense_ref.shape[-2:]
+            dense_out[0, zz * slab : (zz + 1) * slab, xx * cols : (xx + 1) * cols] = dense_ref[
+                zz, xx, 0, 0
+            ].astype(F32)
+    n, _, hd, cols = heads_ref.shape
+    heads_out[0] = heads_ref[...].reshape(n * hd, cols).astype(F32).T
+
+
+def spread_call(pieces):
+    n, parts, slab, cols = pieces.shape
+    split = pieces.reshape(4, 2, 2, parts, slab, cols)
+    return pl.pallas_call(
+        spread_kernel,
+        grid=(3, 2),
+        out_shape=[
+            jax.ShapeDtypeStruct((3, 8 * slab, 2 * cols), F32),
+            jax.ShapeDtypeStruct((3, cols, n * slab), F32),
+        ],
+        in_specs=[
+            pl.BlockSpec((4, 2, 1, 1, slab, cols), lambda w, h: (0, 0, h, w, 0, 0)),
+            pl.BlockSpec((n // 2, 1, slab, cols), lambda w, h: (h, 3 + w, 0, 0)),
+        ],
+        out_specs=[
+            pl.BlockSpec((1, 4 * slab, 2 * cols), lambda w, h: (w, h, 0)),
+            pl.BlockSpec((1, cols, n * slab // 2), lambda w, h: (w, 0, h)),
+        ],
+        compiler_params=pltpu.CompilerParams(vmem_limit_bytes=48 * 2**20),
+        name="spread",
+    )(split, pieces)
 
 
 def joined(own, other, fs):
@@ -918,48 +1352,24 @@
         cot.astype(F32) + norm_back(grad_hidden_two * gain_two, normed_two, scale_two)
     ).astype(BF)
     grad_att_t = dot(out_full, grad_resid, NT).astype(BF).reshape(H, HD, rows)
-    g_t, value_o = swap_call(3, grad_att_t, (value_weight,))
     grad_outer = dot(active, cot, TN).astype(BF)
     grad_inner = dot(hidden_two, grad_inner_pre, TN).astype(BF)
     grad_outw = dot(attn_t, grad_resid).astype(BF)
-
-    d_all, dw, dscale = backward_call(
-        h_all, scale_col, first_key, k, v, kt, raw, q, qt, g_t, o32, lse
+    d_all, piece, dscale, value_o = backward_call(
+        grad_att_t, (grad_outw, grad_inner, grad_outer), (value_weight,),
+        h_all, scale_col, first_key, k, v, kt, raw, q, qt, o32, lse,
     )
     half = width // 2
-    dw_mine = lax.dynamic_slice(dw, (0, fs * half), (dw.shape[0], half))
-    dw_send = lax.dynamic_slice(dw, (0, (1 - fs) * half), (dw.shape[0], half)).astype(BF)
-    d_mine, dw_got = swap_call(4, d_all, (), dw_send)
-    dw_sum = (dw_mine + dw_got.astype(F32)).astype(BF)
-    d_mine = d_mine.reshape(H, 3, HD, rows)
-    query_full = joined(query_weight, query_o, fs)
-    key_full = joined(key_weight, key_o, fs)
-    value_full = joined(value_weight, value_o, fs)
-    grad_hidden_one = sum(
-        dot(d_mine[:, i].reshape(width, rows), w, ((0,), (1,)))
-        for i, w in enumerate((query_full, key_full, value_full))
-    )
-    scale_one = rms_scale(token_rows)
-    normed_one = token_rows * scale_one
-    grad_gain_one = jnp.sum(grad_hidden_one * normed_one, axis=0)
-    grad_tokens = (
-        grad_resid.astype(F32) + norm_back(grad_hidden_one * gain_one, normed_one, scale_one)
-    ).astype(BF)
-
-    dw_all = lax.all_gather(dw_sum, "ctx", axis=0, tiled=False).reshape(H, 3, HD, half)
-    dw_qkv = [dw_all[:, i].reshape(width, half).T.astype(F32) for i in range(3)]
-    dense = [
-        lax.psum(lax.psum_scatter(g, "fs", scatter_dimension=0, tiled=True), "ctx").astype(F32)
-        for g in (grad_outw, grad_inner, grad_outer)
-    ]
-    small = lax.psum(
-        jnp.concatenate([grad_gain_one, grad_gain_two, dscale[:, 0]]), ("ctx", "fs")
-    )
-    gain_one_sum = lax.dynamic_slice(small, (fs * half,), (half,))
-    gain_two_sum = lax.dynamic_slice(small, (width + fs * half,), (half,))
-    scale_sum = small[2 * width :] / math.sqrt(HD)
+    small = jnp.zeros((8, width), F32).at[1].set(grad_gain_two).at[2, :HD].set(dscale[:, 0])
+    pieces, grad_tokens, sums = final_call(
+        piece, tok, grad_resid, gain_full, small, d_all,
+        (query_weight, key_weight, value_weight), (query_o, key_o, value_o),
+    )
+    dense, heads = spread_call(pieces)
+    gain_sums = lax.dynamic_slice(sums, (0, fs * half), (2, half))
     return (
-        result[None], grad_tokens[None], *dw_qkv, *dense, gain_one_sum, gain_two_sum, scale_sum,
+        result[None], grad_tokens[None], heads[0], heads[1], heads[2], dense[0], dense[1], dense[2],
+        gain_sums[0], gain_sums[1], sums[2, :HD] / math.sqrt(HD),
     )
 
 

time: 530 us -> 385 us (0.73)
  waiting for transfers between devices: 141 us -> 0 us
  Pallas kernels: 242 us -> 333 us
  blocking collectives: 51.3 us -> 0 us
  other arithmetic: 20.4 us -> 4.57 us
  between operations: 14.1 us -> 0.89 us
  matrix products: 33.2 us -> 22.2 us
    reduce_scatter x3 -> x0, waiting for transfers between devices: 95.3 us -> none  [fast_local(): lax.psum_scatter(g, 'fs', scatter_dimension=0, tiled=True)]
    pallas_call x3, Pallas kernels: 128 us -> 219 us  [the longest x1 120 us: backward_call(): pl.pallas_call(functools.partial(backward_kernel, n_w), out_shape=[jax.Sh...]
    psum x1 -> x0, blocking collectives: 51.3 us -> none  [fast_local(): lax.psum(jnp.concatenate([grad_gain_one, grad_gain_two, dscale[:, 0]]), (...]
    all_gather x1 -> x0, waiting for transfers between devices: 45.2 us -> none  [fast_local(): lax.all_gather(dw_sum, 'ctx', axis=0, tiled=False).reshape(H, 3, HD, half)]
    squeeze x0 -> x2, local copies, waits for them, and re-layouts: none -> 13.2 us  [the longest x1 9.11 us: fast_local(): heads[2]]
    convert_element_type x7 -> x0, other arithmetic: 13 us -> none  [the longest x3 7.41 us: fast_local(): lax.psum(lax.psum_scatter(g, 'fs', scatter_dimension=0, tiled=True), 'ctx')]
    dot_general x12 -> x9, matrix products: 33.2 us -> 22.2 us  [dot(): return lax.dot_general(a, b, (dims, ((), ())), preferred_element_type=F32)]
    unnamed x46 -> x40, local copies, waits for them, and re-layouts: 13.6 us -> 4.66 us
  transfers between devices with their start and end apart: 5 -> 0, of which waited for: 3 -> 0; matrix products, arithmetic and copies ran while one was open for 8% -> 0% of each run, Pallas kernels for 24% -> 0%
where the time goes in v3:
time: 385 us
  Pallas kernels  333 us (86%)
  local copies, waits for them, and re-layouts  24 us (6%)
  matrix products  22.2 us (6%)
  other arithmetic  4.57 us (1%)
    pallas_call x1, Pallas kernels, backward_call(): pl.pallas_call(functools.partial(backward_kernel, n_w), out_shape=[jax.Sh...  120 us
    pallas_call x1, Pallas kernels, forward_call(): pl.pallas_call(functools.partial(forward_kernel, n_w), out_shape=shapes,...  114 us
    pallas_call x1, Pallas kernels, final_call(): pl.pallas_call(final_kernel, out_shape=[jax.ShapeDtypeStruct((H, *piece.s...  87.2 us
    dot_general x9, matrix products, dot(): return lax.dot_general(a, b, (dims, ((), ())), preferred_element_type=F32)  22.2 us
    pallas_call x1, Pallas kernels, spread_call(): pl.pallas_call(spread_kernel, grid=(3, 2), out_shape=[jax.ShapeDtypeStruc...  11.7 us
    squeeze x1, local copies, waits for them, and re-layouts, fast_local(): heads[2]  9.11 us

profile of v3, /device:TPU:0, one launch (start us, length us, event | category | flops | bytes accessed | tf_op | source)
XLA Modules:
  0.0 384.8 jit_solution(16981253284757562651)
XLA Ops:
  0.6 0.0 copy-start.14
  0.7 0.0 copy-start.10
  0.7 0.7 stack.10
  1.4 0.7 stack.9
  2.0 0.6 pad_maximum_fusion.1.gain_ref
  2.6 1.2 constant_dynamic-slice_fusion
  3.9 0.1 copy.44
  4.0 0.1 copy.43
  4.2 1.1 constant_dynamic-slice_fusion.2
  5.3 0.1 copy.42
  5.4 0.8 pad_maximum_fusion.wt_ref
  6.2 0.7 copy.38.scale_ref.rest_5_
  6.9 0.7 select_reduce_fusion
  7.6 113.8 %forward.1 = (bf16[8,512,1280]{2,1,0:T(8,128)(2,1)}, f32[2,1280]{1,0:T(2,128)}, bf16[16,80,256]{2,1,0:T(8,128)(2,1)}, f32[8,80,512]{2,1,0:T(8,128)}, f32[8,1,512...) custom-call(bf16[256,1280]{1,0:T(8,128)(2,1)} %bitcast.53, ...), custom_call_target="tpu_custom_call" | custom-call | tf_op jit(solution)/shard_map/forward/pallas_call | solution.py:684
  121.4 0.0 copy-done.1
  121.5 0.0 copy-done.5
  121.5 0.0 copy-start.9
  121.5 0.0 copy-start.4
  121.5 3.5 multiply_reduce_fusion.2
  125.0 0.0 copy-start.3
  125.0 1.2 fusion.8
  126.3 0.2 copy-done.3
  126.5 0.5 copy-done.13
  127.0 2.2 fusion.4
  129.1 1.4 fusion.2
  130.5 1.4 multiply_reduce_fusion
  131.9 0.0 copy-start.11
  131.9 0.4 add_convert_fusion.gr_ref
  132.3 1.0 copy-done.11
  133.4 3.9 %convolution_convert_fusion.3 = bf16[1280,256]{1,0:T(8,128)(2,1)} fusion(bf16[256,1280]{1,0:T(8,128)(2,1)S(1)} %add_convert_fusion.gr_ref, bf16[640,1280]{1,0:T(8,128)(2,1)S(1)} %copy-done.11, bf16[640,1280]{1,0:T(8,128)(2,1)S(1)} %copy-done.5, pred[]{:T(512)S(6)} %eq.2), kind=kOutput, calls=%fused_computation.19 | convolution fusion | flops 853934080 | bytes 4587521 | tf_op jit(solution)/shard_map/dot_general | solution.py:354
  137.3 2.7 convolution_convert_fusion.2.rest_0_
  140.0 2.9 convolution_convert_fusion.1.rest_1_
  142.9 3.0 convolution_convert_fusion.rest_2_
  145.9 120.4 %backward.1 = (bf16[3,1280,256]{2,1,0:T(8,128)(2,1)}, bf16[6,80,640]{2,1,0:T(8,128)(2,1)}, f32[80,1]{1,0:T(8,128)}, bf16[640,1280]{1,0:T(8,128)(2,1)}) custom-call(bf16[16,80,256]{2,1,0:T(8,128)(2,1)} %bitcast.58, bf16[1280,1280]{1,0:T(8,128)(2,1)} %convolution_convert_fusion.2.rest_0_, bf16[1280,1280]{1,0:T(8,128)(2,1)} %convolution_convert_fusion.1.rest_1_, ...), custom_call_target="tpu_custom_call" | custom-call | tf_op jit(solution)/shard_map/backward/pallas_call | solution.py:1015
  266.4 0.9 reduce.5
  267.3 0.2 scatter.9.small_ref
  267.5 0.0 copy-start.8
  267.5 0.6 copy-done.8
  268.1 87.2 %final.1 = (bf16[16,6,80,640]{3,2,1,0:T(8,128)(2,1)}, bf16[256,1280]{1,0:T(8,128)(2,1)}, f32[8,1280]{1,0:T(8,128)}) custom-call(bf16[6,80,640]{2,1,0:T(8,128)(2,1)} %get-tuple-element.74.piece_ref, bf16[256,1280]{1,0:T(8,128)(2,1)} %bitcast.54, bf16[256,1280]{1,0:T(8,128)(2,1)} %copy-done, f32[2,1280]{1,0:T(2,128)} %get-tuple-element.62.gain_ref, ...), custom_call_target="tpu_custom_call" | custom-call | tf_op jit(solution)/shard_map/final/pallas_call | solution.py:1240
  355.3 11.7 %spread.1 = (f32[3,640,1280]{2,1,0:T(8,128)}, f32[3,640,1280]{2,1,0:T(8,128)}) custom-call(bf16[4,2,2,6,80,640]{5,4,3,2,1,0:T(8,128)(2,1)} %bitcast.50, bf16[16,6,80,640]{3,2,1,0:T(8,128)(2,1)} %get-tuple-element.81.heads_ref), custom_call_target="tpu_custom_call" | custom-call | tf_op jit(solution)/shard_map/spread/pallas_call | solution.py:1278
  367.1 0.0 slice-start.2
  367.1 9.1 %slice_bitcast_fusion.3 = (f32[640,1280]{1,0:T(8,128)}, f32[640,1280]{1,0:T(8,128)}, f32[640,1280]{1,0:T(8,128)}) fusion(f32[3,640,1280]{2,1,0:T(8,128)} %get-tuple-element.82), kind=kLoop, calls=%fused_computation.9 | loop fusion | bytes 19660800 | tf_op jit(solution)/shard_map/squeeze | solution.py:1371
  376.2 1.0 slice-done.2
  377.2 4.1 %slice_bitcast_fusion = (f32[640,1280]{1,0:T(8,128)}, f32[640,1280]{1,0:T(8,128)}, f32[640,1280]{1,0:T(8,128)}) fusion(f32[3,640,1280]{2,1,0:T(8,128)S(1)} %bitcast.52), kind=kLoop, calls=%fused_computation.6 | loop fusion | bytes 19660800 | tf_op jit(solution)/shard_map/squeeze | solution.py:1371
  381.3 1.5 dynamic-slice_reduce_fusion
  382.8 1.2 multiply_bitcast_fusion
  384.0 0.0 copy-done.7
  384.0 0.8 copy.47
  (27 shorter events, 0.1 us)
Async XLA Ops:
  0.6 5.5 %copy-start.14 = (f32[80]{0:T(128)S(1)}, f32[80]{0:T(128)}, u32[]{:S(2)}) copy-start(f32[80]{0:T(128)} %param.25) | copy-start | bytes 964
  0.7 6.2 %copy-start.10 = (s32[1,8]{1,0:T(1,128)S(1)}, s32[1,8]{1,0:T(1,128)}, u32[]{:S(2)}) copy-start(s32[1,8]{1,0:T(1,128)} %param.26) | copy-start | bytes 100
  7.6 113.8 %copy-start.1 = (bf16[1,256,1280]{2,1,0:T(8,128)(2,1)S(1)}, bf16[1,256,1280]{2,1,0:T(8,128)(2,1)}, u32[]{:S(2)}) copy-start(bf16[1,256,1280]{2,1,0:T(8,128)(2,1)} %param.16) | copy-start | bytes 1966084
  7.6 113.8 %copy-start.5 = (bf16[640,1280]{1,0:T(8,128)(2,1)S(1)}, bf16[640,1280]{1,0:T(8,128)(2,1)}, u32[]{:S(2)}) copy-start(bf16[640,1280]{1,0:T(8,128)(2,1)} %rest_0_.1) | copy-start | bytes 4915204
  121.5 3.5 copy-start.9
  121.5 3.5 copy-start.4
  121.5 3.5 copy-start.12
  125.0 1.4 copy-start.3
  125.0 1.9 copy-start.13
  127.0 2.2 copy-start.6
  131.9 1.4 copy-start.11
  133.4 3.9 %copy-start = (bf16[256,1280]{1,0:T(8,128)(2,1)}, bf16[256,1280]{1,0:T(8,128)(2,1)S(1)}, u32[]{:S(2)}) copy-start(bf16[256,1280]{1,0:T(8,128)(2,1)S(1)} %add_convert_fusion.gr_ref) | copy-start | bytes 1966084
  133.4 3.9 %copy-start.2 = (bf16[16,80,256]{2,1,0:T(8,128)(2,1)S(1)}, bf16[16,80,256]{2,1,0:T(8,128)(2,1)}, u32[]{:S(2)}) copy-start(bf16[16,80,256]{2,1,0:T(8,128)(2,1)} %get-tuple-element.60) | copy-start | bytes 1966084
  267.5 0.6 copy-start.8
  367.1 9.1 %slice-start = ((s8[9830400]{0:T(1024)(128)(4,1)}), s8[4194304]{0:T(1024)(128)(4,1)S(1)}, s32[]{:S(2)}) async-start(s8[9830400]{0:T(1024)(128)(4,1)} %bitcast.51), calls=%async_computation | async-start | bytes 8388608
  367.1 9.1 %slice-start.1 = ((s8[9830400]{0:T(1024)(128)(4,1)}), s8[4194304]{0:T(1024)(128)(4,1)S(1)}, s32[]{:S(2)}) async-start(s8[9830400]{0:T(1024)(128)(4,1)} %bitcast.51), calls=%async_computation.1 | async-start | bytes 8388608
  367.1 10.1 %slice-start.2 = ((s8[9830400]{0:T(1024)(128)(4,1)}), s8[1441792]{0:T(1024)(128)(4,1)S(1)}, s32[]{:S(2)}) async-start(s8[9830400]{0:T(1024)(128)(4,1)} %bitcast.51), calls=%async_computation.2 | async-start | bytes 2883584
  377.2 6.8 %copy-start.7 = (bf16[256,1280]{1,0:T(8,128)(2,1)S(1)}, bf16[256,1280]{1,0:T(8,128)(2,1)}, u32[]{:S(2)}) copy-start(bf16[256,1280]{1,0:T(8,128)(2,1)} %get-tuple-element.80) | copy-start | bytes 1966084

commit v4 on v3

--- a/solution.py
+++ b/solution.py
@@ -715,25 +715,26 @@
     return pl.ds(pl.multiple_of(start, align), size)
 
 
-def backward_kernel(
-    n_w, gt_ref, *rest,
-):
-    dense = rest[:3]
-    own = rest[3 : 3 + n_w]
-    at = 3 + n_w
-    h_ref, scale_ref, first_ref, k_ref, v_ref, kt_ref, raw_ref, q_ref, qt_ref, o_ref, lse_ref = rest[
-        at : at + 11
-    ]
-    at += 11
-    got_ref, piece_ref, ds_ref = rest[at : at + 3]
-    other = rest[at + 3 : at + 3 + n_w]
+def tail_kernel(n_w, gt_ref, *rest):
+    own = rest[:3]
+    held = rest[3 : 6 - n_w]
+    at = 6 - n_w
     (
-        g_in, g_sc, delta_sc, dq_sc, scale_sc, dk_sc, dv_sc, d_sc, dw_sc, dw_out, dw_got,
-        s1, r0, ra, rb, r2, rz,
-        gsend, grecv, qsend, qrecv, ksend, krecv, wssem, wrsem, dsend, drecv, psend, precv, lsem,
+        attn_ref, gr_ref, hid_ref, gip_ref, act_ref, cot_ref, tok_ref, gain_ref, g2_ref,
+        h_ref, scale_ref, first_ref, k_ref, v_ref, kt_ref, raw_ref, q_ref, qt_ref, o_ref, lse_ref,
+    ) = rest[at : at + 20]
+    at += 20
+    all_ref, tg_ref, sums_ref = rest[at : at + 3]
+    pulled = rest[at + 3 : at + 3 + n_w]
+    (
+        g_in, g_sc, delta_sc, dq_sc, scale_sc, dk_sc, dv_sc, d_sc, got, dw_sc, dw_out, dw_got, piece,
+        s1, r0, so, ra, rb, r2, rz, e_sc, small_out, small_in, small_y, small_got,
+        gsend, grecv, qsend, qrecv, ksend, krecv, wssem, wrsem, dsend, drecv, psend, precv,
+        asend, arecv, vsend, vrecv, lsem, wsem,
     ) = rest[at + 3 + n_w :]
     me, fs, z, x, k = place()
     sib, xn, yn = (me + 1 - 2 * k, fs), (me + 2 - 4 * x, fs), (me, 1 - fs)
+    up, dn = (me + 4, fs), (me - 4, fs)
     units, rows = h_ref.shape[:2]
     block = rows // 2
     n_g = 3
@@ -744,21 +745,6 @@
     for i in range(1, H):
         signal((lax.rem(me + i, H), fs))
     signal(yn)
-
-    def mine(g, f):
-        return pltpu.make_async_copy(
-            dense[g].at[half_rows(f * 2 * part + k * part, part, 64)], s1.at[g, f], lsem.at[g * 2 + f]
-        )
-
-    def theirs(g, f):
-        return remote(
-            dense[g].at[half_rows(f * 2 * part + (1 - k) * part, part, 64)],
-            r0.at[g, f], dsend.at[g * 2 + f], drecv.at[g * 2 + f], sib,
-        )
-
-    for g in range(n_g):
-        for f in range(2):
-            mine(g, f).start()
     pl.semaphore_wait(bar, H)
 
     def lanes(b):
@@ -774,48 +760,80 @@
         return c
 
     lax.fori_loop(1, H, g_start, 0)
-    g_here = pltpu.make_async_copy(gt_ref.at[me], g_in.at[me // 2, :, lanes(me)], lsem.at[6])
+    g_here = pltpu.make_async_copy(gt_ref.at[me], g_in.at[me // 2, :, lanes(me)], lsem.at[0])
     g_here.start()
+
+    def theirs(g):
+        return remote(so.at[g], r0.at[g], dsend.at[g], drecv.at[g], sib)
+
+    def dense_rows(g, start):
+        r = half_rows(start, part, 64)
+        if g == 0:
+            return dot(attn_ref[r, :], gr_ref[...])
+        a, b = ((hid_ref, gip_ref), (act_ref, cot_ref))[g - 1]
+        return dot(a[r, :], b[...])
+
     for g in range(n_g):
         for f in range(2):
-            theirs(g, f).start()
-    first, second = weight_pull(own, other, k, fs, me, wssem, wrsem)
-    for c in first:
-        c.start()
+            so[g, f] = dense_rows(g, f * 2 * part + (1 - k) * part).astype(BF)
+        theirs(g).start()
+    for g in range(n_g):
+        for f in range(2):
+            s1[g, f] = dense_rows(g, f * 2 * part + k * part).astype(BF)
 
     top, bottom = slice(0, part // 2), slice(part // 2, part)
     x_here = half_rows(x * cols, cols, 128)
     x_there = half_rows((1 - x) * cols, cols, 128)
-    up_a = remote(s1.at[:, 1 - fs, top, :], ra, psend.at[0], precv.at[0], yn)
-    up_b = remote(s1.at[:, :, bottom, x_there], rb, psend.at[1], precv.at[1], xn)
-    two_a = remote(s1.at[:, fs, top, x_there], r2.at[:, top], psend.at[2], precv.at[2], xn)
-    two_b = remote(s1.at[:, 1 - fs, bottom, x_here], r2.at[:, bottom], psend.at[3], precv.at[3], yn)
+
+    def stage(g, i):
+        ends = (
+            (s1.at[g, 1 - fs, top, :], ra.at[g], yn),
+            (s1.at[g, :, bottom, x_there], rb.at[g], xn),
+            (s1.at[g, fs, top, x_there], r2.at[g, top], xn),
+            (s1.at[g, 1 - fs, bottom, x_here], r2.at[g, bottom], yn),
+        )[i]
+        return remote(ends[0], ends[1], psend.at[i, g], precv.at[i, g], ends[2])
+
     slab = part // 4
 
     def z_copy(t, slot, sem):
         return remote(
             s1.at[:, fs, half_rows(t * slab, slab, 16), x_here],
-            rz.at[slot], psend.at[4 + sem], precv.at[4 + slot], (me + 4 * (t - z), fs),
+            rz.at[slot], psend.at[4, sem], precv.at[4, slot], (me + 4 * (t - z), fs),
         )
 
     for g in range(n_g):
+        theirs(g).wait()
+
+        def add(i, c, g=g):
+            r = half_rows(i * 32, 32, 32)
+            for f in range(2):
+                s1[g, f, r, :] += r0[g, f, r, :]
+            return c
+
+        lax.fori_loop(0, part // 32, add, 0)
+        stage(g, 0).start()
+        stage(g, 1).start()
+
+    loads = []
+    for w in range(3):
         for f in range(2):
-            mine(g, f).wait()
-            theirs(g, f).wait()
-
-            def add(i, c, g=g, f=f):
-                r = half_rows(i * 32, 32, 32)
-                s1[g, f, r, :] += r0[g, f, r, :]
-                return c
-
-            lax.fori_loop(0, part // 32, add, 0)
-    up_a.start()
-    up_b.start()
+            loads.append(
+                pltpu.make_async_copy(own[w].at[pl.ds(f * part, part)], r0.at[w, f], wsem.at[w * 2 + f])
+            )
+            loads[-1].start()
+    for w in range(3 - n_w):
+        for f in range(2):
+            loads.append(
+                pltpu.make_async_copy(held[w].at[pl.ds(f * part, part)], so.at[w, f], wsem.at[6 + w * 2 + f])
+            )
+            loads[-1].start()
+    first, second = weight_pull(own[3 - n_w :], pulled, k, fs, me, wssem, wrsem)
 
     def after_one():
-        up_a.wait()
-        up_b.wait()
         for g in range(n_g):
+            stage(g, 0).wait()
+            stage(g, 1).wait()
 
             def add(i, c, g=g):
                 r = half_rows(i * 32, 32, 32)
@@ -826,13 +844,15 @@
                 return c
 
             lax.fori_loop(0, part // 64, add, 0)
-        two_a.start()
-        two_b.start()
+            stage(g, 2).start()
+            stage(g, 3).start()
+        for c in first:
+            c.start()
 
     def after_two():
-        two_a.wait()
-        two_b.wait()
         for g in range(n_g):
+            stage(g, 2).wait()
+            stage(g, 3).wait()
 
             def add(i, c, g=g):
                 r = half_rows(i * 32, 32, 32)
@@ -853,7 +873,7 @@
             total = s1[g, fs, here, x_here].astype(F32)
             for d in range(1, 4):
                 total = total + rz[lax.rem(z + d, 4), g].astype(F32)
-            piece_ref[g] = total.astype(BF)
+            piece[0, g] = total.astype(BF)
 
     scale_sc[...] = jnp.zeros_like(scale_sc)
     dw_sc[...] = jnp.zeros_like(dw_sc)
@@ -890,7 +910,7 @@
         return d_sc.at[b // 2, pl.ds(lo, n), :, lanes(b)]
 
     def to(t, lo, n):
-        return got_ref.at[pl.ds(lo, n), half_rows(t * HD, HD, 16)]
+        return got.at[pl.ds(lo, n), half_rows(t * HD, HD, 16)]
 
     def kv_copy(b, t):
         return remote(out(b, 1, 2), to(t, 1, 2), ksend.at[b], krecv.at[t], (b, fs))
@@ -898,8 +918,8 @@
     def q_copy(b, t):
         return remote(out(b, 0, 1), to(t, 0, 1), qsend.at[b], qrecv.at[t], (b, fs))
 
-    kv_here = pltpu.make_async_copy(out(me, 1, 2), to(me, 1, 2), lsem.at[7])
-    q_here = pltpu.make_async_copy(out(me, 0, 1), to(me, 0, 1), lsem.at[8])
+    kv_here = pltpu.make_async_copy(out(me, 1, 2), to(me, 1, 2), lsem.at[1])
+    q_here = pltpu.make_async_copy(out(me, 0, 1), to(me, 0, 1), lsem.at[2])
 
     def column(n, c):
         j = lax.rem(me // 2 + n, units)
@@ -938,11 +958,11 @@
         for e in range(2):
             dw_sc[1 + e] += dot(d_sc[j, 1 + e], h_ref[j])
 
-        @pl.when(n == 3)
+        @pl.when(n == ONE_AT)
         def _():
             after_one()
 
-        @pl.when(n == 6)
+        @pl.when(n == TWO_AT)
         def _():
             after_two()
 
@@ -984,12 +1004,93 @@
     lax.fori_loop(0, units, query_weight, 0)
     half = dw_out.shape[2]
     dw_out[...] = dw_sc[:, :, half_rows((1 - fs) * half, half, 128)].astype(BF)
-    dw_copy = remote(dw_out, dw_got, psend.at[8], precv.at[8], yn)
+    dw_copy = remote(dw_out, dw_got, vsend.at[H], vrecv.at[H], yn)
     dw_copy.start()
-    ds_ref[...] = jnp.sum(scale_sc[...], axis=1, keepdims=True)
+    small_out[...] = jnp.zeros_like(small_out)
+    small_out[1:2, :] = g2_ref[...]
+    small_out[2:3, :HD] = jnp.sum(scale_sc[...].T, axis=0, keepdims=True)
+
+    def cp(p, s, t, si, mine=False):
+        here = all_ref.at[s, p]
+        return remote(piece.at[p] if mine else here, here, asend.at[p, si], arecv.at[p, s], t)
+
+    def keep(p):
+        return pltpu.make_async_copy(piece.at[p], all_ref.at[me, p], lsem.at[3 + p])
+
+    def begin(p):
+        keep(p).start()
+        cp(p, me, xn, 0, True).start()
+
+        @pl.when(z < 3)
+        def _():
+            cp(p, me, up, 1, True).start()
+
+        @pl.when(z > 0)
+        def _():
+            cp(p, me, dn, 2, True).start()
+
+        cp(p, me, sib, 3, True).start()
+
+    def column_arrival(p, d):
+        a = 4 + (d - 1) * 6
+
+        @pl.when(z >= d)
+        def _():
+            s = me - 4 * d
+            cp(p, s, dn, a).wait_recv()
+
+            @pl.when(z < 3)
+            def _():
+                cp(p, s, up, a).start()
+
+            cp(p, s, xn, a + 1).start()
+            cp(p, s, sib, a + 2).start()
+
+        @pl.when(z + d <= 3)
+        def _():
+            s = me + 4 * d
+            cp(p, s, up, a + 3).wait_recv()
+
+            @pl.when(z > 0)
+            def _():
+                cp(p, s, dn, a + 3).start()
+
+            cp(p, s, xn, a + 4).start()
+            cp(p, s, sib, a + 5).start()
+
+    xo = me + 2 - 4 * x
+
+    def across_arrival(p, d):
+        @pl.when(z >= d)
+        def _():
+            s = xo - 4 * d
+            cp(p, s, xn, 0).wait_recv()
+            cp(p, s, sib, 22 + z - d).start()
+
+        if d > 0:
+
+            @pl.when(z + d <= 3)
+            def _():
+                s = xo + 4 * d
+                cp(p, s, xn, 0).wait_recv()
+                cp(p, s, sib, 22 + z + d).start()
+
+    dw_copy.wait()
+    piece[1] = (dw_sc[:, :, half_rows(fs * half, half, 128)] + dw_got[...].astype(F32)).astype(BF)
+    begin(1)
     after_three()
-    dw_copy.wait()
-    piece_ref[n_g:] = (dw_sc[:, :, half_rows(fs * half, half, 128)] + dw_got[...].astype(F32)).astype(BF)
+    begin(0)
+    column_arrival(1, 1)
+
+    for w in range(3 - n_w, 3):
+        i = w - (3 - n_w)
+        second[i].wait()
+        first[i].wait_send()
+        for f in range(2):
+            loads.append(
+                pltpu.make_async_copy(pulled[i].at[pl.ds(f * part, part)], so.at[w, f], wsem.at[6 + w * 2 + f])
+            )
+            loads[-1].start()
 
     def taken(n, c):
         b = lax.rem(me + n, H)
@@ -1000,295 +1101,211 @@
     lax.fori_loop(1, H, taken, 0)
     kv_here.wait()
     q_here.wait()
-    for i in range(n_w):
-        first[i].wait_send()
-        second[i].wait()
-
-
-def backward_call(gt, dense, weights, h_all, scale_col, first_key, k, v, kt, raw, q, qt, o32, lse):
-    n_w = len(weights)
-    n, rows, width = h_all.shape
-    vm = (h_all, scale_col, first_key, k, v, kt, raw, q, qt, o32, lse)
+    for c in loads:
+        c.wait()
+
+    def input_grad(w):
+        for r, m in ((fs, r0), (1 - fs, so)):
+            for f in range(2):
+                at_rows = half_rows((r * 2 + f) * part, part, 64)
+                term = dot(m[w, f], got[w])
+                if w == 0:
+                    e_sc[at_rows, :] = term
+                else:
+                    e_sc[at_rows, :] += term
+
+    input_grad(0)
+    column_arrival(0, 1)
+    column_arrival(1, 2)
+    input_grad(1)
+    across_arrival(1, 0)
+    across_arrival(0, 0)
+    column_arrival(0, 2)
+    column_arrival(1, 3)
+    input_grad(2)
+    grad_hidden = e_sc[...].T
+    tokens = tok_ref[...].astype(F32)
+    scale = lax.rsqrt(jnp.mean(tokens * tokens, axis=-1, keepdims=True) + epsilon)
+    normed = tokens * scale
+    small_out[0:1, :] = jnp.sum(grad_hidden * normed, axis=0, keepdims=True)
+
+    def v_copy(b, t):
+        return remote(small_out, small_in.at[t], vsend.at[b], vrecv.at[t], (b, fs))
+
+    def v_start(n, c):
+        v_copy(lax.rem(me + n, H), me).start()
+        return c
+
+    lax.fori_loop(1, H, v_start, 0)
+    across_arrival(1, 1)
+    across_arrival(0, 1)
+    column_arrival(0, 3)
+    e = grad_hidden * gain_ref[0:1, :]
+    tg_ref[...] = (
+        gr_ref[...].astype(F32) + scale * (e - normed * jnp.mean(e * normed, axis=-1, keepdims=True))
+    ).astype(BF)
+
+    def v_taken(n, c):
+        b = lax.rem(me + n, H)
+        v_copy(b, b).wait()
+        return c
+
+    lax.fori_loop(1, H, v_taken, 0)
+
+    def v_add(n, total):
+        return total + small_in[lax.rem(me + n, H)]
+
+    small_y[...] = lax.fori_loop(1, H, v_add, small_out[...])
+    y_copy = remote(small_y, small_got, vsend.at[H + 1], vrecv.at[H + 1], yn)
+    y_copy.start()
+    for d in range(2, 4):
+        across_arrival(1, d)
+        across_arrival(0, d)
+    y_copy.wait()
+    sums_ref[...] = small_y[...] + small_got[...]
+
+    for p in range(2):
+
+        def from_sib(n, c, p=p):
+            cp(p, n * 2 + 1 - k, sib, 0).wait_recv()
+            return c
+
+        lax.fori_loop(0, UNITS, from_sib, 0)
+        keep(p).wait()
+        cp(p, me, xn, 0, True).wait_send()
+
+        @pl.when(z < 3)
+        def _(p=p):
+            cp(p, me, up, 1, True).wait_send()
+
+        @pl.when(z > 0)
+        def _(p=p):
+            cp(p, me, dn, 2, True).wait_send()
+
+        cp(p, me, sib, 3, True).wait_send()
+
+        def sent(d, c, p=p):
+            a = 4 + (d - 1) * 6
+
+            @pl.when(z >= d)
+            def _():
+                s = me - 4 * d
+
+                @pl.when(z < 3)
+                def _():
+                    cp(p, s, up, a).wait_send()
+
+                cp(p, s, xn, a + 1).wait_send()
+                cp(p, s, sib, a + 2).wait_send()
+
+            @pl.when(z + d <= 3)
+            def _():
+                s = me + 4 * d
+
+                @pl.when(z > 0)
+                def _():
+                    cp(p, s, dn, a + 3).wait_send()
+
+                cp(p, s, xn, a + 4).wait_send()
+                cp(p, s, sib, a + 5).wait_send()
+
+            return c
+
+        lax.fori_loop(1, 4, sent, 0)
+
+        def sent_across(zz, c, p=p):
+            cp(p, xo + 4 * (zz - z), sib, 22 + zz).wait_send()
+            return c
+
+        lax.fori_loop(0, 4, sent_across, 0)
+
+
+ONE_AT = 2
+TWO_AT = 5
+
+
+def tail_call(gt, own, held, vm):
+    n_w = 3 - len(held)
+    rows, width = vm[1].shape
+    n, ur = vm[9].shape[:2]
     half = width // 2
-    part = dense[0].shape[0] // 4
+    part = width // 4
     sem = pltpu.SemaphoreType.DMA
     return pl.pallas_call(
-        functools.partial(backward_kernel, n_w),
+        functools.partial(tail_kernel, n_w),
         out_shape=[
-            jax.ShapeDtypeStruct((3, H * HD, rows // 2), BF),
-            jax.ShapeDtypeStruct((6, part // 4, half), BF),
-            jax.ShapeDtypeStruct((HD, 1), F32),
+            jax.ShapeDtypeStruct((H, 2, 3, part // 4, half), BF),
+            jax.ShapeDtypeStruct((rows, width), BF),
+            jax.ShapeDtypeStruct((8, width), F32),
         ]
-        + [jax.ShapeDtypeStruct(w.shape, BF) for w in weights],
-        in_specs=[ANY] * (4 + n_w) + [VMEM] * len(vm),
+        + [jax.ShapeDtypeStruct(own[0].shape, BF)] * n_w,
+        in_specs=[ANY] * (4 + len(held)) + [VMEM] * len(vm),
         out_specs=[ANY, VMEM, VMEM] + [ANY] * n_w,
         scratch_shapes=[
-            pltpu.VMEM((n, HD, rows), BF),
-            pltpu.VMEM((n, rows, HD), BF),
-            pltpu.VMEM((n, 1, rows), F32),
-            pltpu.VMEM((n, HD, rows), F32),
-            pltpu.VMEM((HD, rows), F32),
-            pltpu.VMEM((rows, HD), F32),
-            pltpu.VMEM((rows, HD), F32),
-            pltpu.VMEM((n, 3, HD, rows), BF),
+            pltpu.VMEM((n, HD, ur), BF),
+            pltpu.VMEM((n, ur, HD), BF),
+            pltpu.VMEM((n, 1, ur), F32),
+            pltpu.VMEM((n, HD, ur), F32),
+            pltpu.VMEM((HD, ur), F32),
+            pltpu.VMEM((ur, HD), F32),
+            pltpu.VMEM((ur, HD), F32),
+            pltpu.VMEM((n, 3, HD, ur), BF),
+            pltpu.VMEM((3, H * HD, rows), BF),
             pltpu.VMEM((3, HD, width), F32),
             pltpu.VMEM((3, HD, half), BF),
             pltpu.VMEM((3, HD, half), BF),
+            pltpu.VMEM((2, 3, part // 4, half), BF),
+            pltpu.VMEM((3, 2, part, width), BF),
             pltpu.VMEM((3, 2, part, width), BF),
             pltpu.VMEM((3, 2, part, width), BF),
             pltpu.VMEM((3, part // 2, width), BF),
             pltpu.VMEM((3, 2, part // 2, half), BF),
             pltpu.VMEM((3, part, half), BF),
             pltpu.VMEM((4, 3, part // 4, half), BF),
+            pltpu.VMEM((width, rows), F32),
+            pltpu.VMEM((8, width), F32),
+            pltpu.VMEM((H, 8, width), F32),
+            pltpu.VMEM((8, width), F32),
+            pltpu.VMEM((8, width), F32),
             sem((H,)), sem((H,)), sem((H,)), sem((H,)), sem((H,)), sem((H,)),
-            sem((max(1, 2 * n_w),)), sem((max(1, 2 * n_w),)), sem((6,)), sem((6,)), sem((9,)), sem((9,)),
-            sem((9,)),
+            sem((max(1, 2 * n_w),)), sem((max(1, 2 * n_w),)), sem((3,)), sem((3,)), sem((5, 4)), sem((5, 4)),
+            sem((2, 26)), sem((2, H)), sem((H + 2,)), sem((H + 2,)), sem((5,)), sem((12,)),
         ],
         compiler_params=pltpu.CompilerParams(
-            collective_id=2, has_side_effects=True, vmem_limit_bytes=60 * 2**20
+            collective_id=2, has_side_effects=True, vmem_limit_bytes=62 * 2**20
         ),
-        name="backward",
-    )(gt, *dense, *weights, *vm)
-
-
-def final_kernel(
-    piece_ref, tok_ref, gr_ref, gain_ref, small_ref, d_ref,
-    qo_ref, ko_ref, vo_ref, qn_ref, kn_ref, vn_ref,
-    all_ref, tg_ref, sums_ref,
-    e_sc, small_out, small_in, small_y, small_got, ssem, rsem, vsend, vrecv, ysem, lsem,
-):
-    me, fs, z, x, k = place()
-    sib, xn, yn = (me + 1 - 2 * k, fs), (me + 2 - 4 * x, fs), (me, 1 - fs)
-    up, dn = (me + 4, fs), (me - 4, fs)
-    bar = pltpu.get_barrier_semaphore()
-    for i in range(1, H):
-        signal((lax.rem(me + i, H), fs))
-    signal(yn)
-    here = pltpu.make_async_copy(piece_ref, all_ref.at[me], lsem.at[0])
-    here.start()
-    pl.semaphore_wait(bar, H)
-
-    def cp(s, t, si, mine=False):
-        return remote(
-            piece_ref if mine else all_ref.at[s], all_ref.at[s], ssem.at[si], rsem.at[s], t
-        )
-
-    cp(me, xn, 0, True).start()
-
-    @pl.when(z < 3)
-    def _():
-        cp(me, up, 1, True).start()
-
-    @pl.when(z > 0)
-    def _():
-        cp(me, dn, 2, True).start()
-
-    cp(me, sib, 3, True).start()
-
-    half = qo_ref.shape[0]
-    for w, (a, b) in enumerate(((qo_ref, qn_ref), (ko_ref, kn_ref), (vo_ref, vn_ref))):
-        for r, m in ((fs, a), (1 - fs, b)):
-            rows = half_rows(r * half, half, 128)
-            term = dot(m[...], d_ref[w])
-            if w == 0:
-                e_sc[rows, :] = term
-            else:
-                e_sc[rows, :] += term
-    grad_hidden = e_sc[...].T
-    tokens = tok_ref[...].astype(F32)
-    scale = lax.rsqrt(jnp.mean(tokens * tokens, axis=-1, keepdims=True) + epsilon)
-    normed = tokens * scale
-    small_out[...] = small_ref[...]
-    small_out[0:1, :] = jnp.sum(grad_hidden * normed, axis=0, keepdims=True)
-
-    def v_copy(b, t):
-        return remote(small_out, small_in.at[t], vsend.at[b], vrecv.at[t], (b, fs))
-
-    def v_start(n, c):
-        v_copy(lax.rem(me + n, H), me).start()
-        return c
-
-    lax.fori_loop(1, H, v_start, 0)
-    e = grad_hidden * gain_ref[0:1, :]
-    tg_ref[...] = (
-        gr_ref[...].astype(F32) + scale * (e - normed * jnp.mean(e * normed, axis=-1, keepdims=True))
-    ).astype(BF)
-
-    xo = me + 2 - 4 * x
-
-    def column_arrival(d):
-        a = 4 + (d - 1) * 6
-
-        @pl.when(z >= d)
-        def _():
-            s = me - 4 * d
-            cp(s, dn, a).wait_recv()
-
-            @pl.when(z < 3)
-            def _():
-                cp(s, up, a).start()
-
-            cp(s, xn, a + 1).start()
-            cp(s, sib, a + 2).start()
-
-        @pl.when(z + d <= 3)
-        def _():
-            s = me + 4 * d
-            cp(s, up, a + 3).wait_recv()
-
-            @pl.when(z > 0)
-            def _():
-                cp(s, dn, a + 3).start()
-
-            cp(s, xn, a + 4).start()
-            cp(s, sib, a + 5).start()
-
-    def across_arrival(d):
-        @pl.when(z >= d)
-        def _():
-            s = xo - 4 * d
-            cp(s, xn, 0).wait_recv()
-            cp(s, sib, 22 + z - d).start()
-
-        @pl.when((z + d <= 3) & (d > 0))
-        def _():
-            s = xo + 4 * d
-            cp(s, xn, 0).wait_recv()
-            cp(s, sib, 22 + z + d).start()
-
-    column_arrival(1)
-
-    def v_taken(n, c):
-        b = lax.rem(me + n, H)
-        v_copy(b, b).wait()
-        return c
-
-    lax.fori_loop(1, H, v_taken, 0)
-
-    def v_add(n, total):
-        return total + small_in[lax.rem(me + n, H)]
-
-    small_y[...] = lax.fori_loop(1, H, v_add, small_out[...])
-    y_copy = remote(small_y, small_got, ysem.at[0], ysem.at[1], yn)
-    y_copy.start()
-    across_arrival(0)
-    column_arrival(2)
-    across_arrival(1)
-    y_copy.wait()
-    sums_ref[...] = small_y[...] + small_got[...]
-    column_arrival(3)
-    across_arrival(2)
-    across_arrival(3)
-
-    def from_sib(n, c):
-        cp(n * 2 + 1 - k, sib, 0).wait_recv()
-        return c
-
-    lax.fori_loop(0, UNITS, from_sib, 0)
-    here.wait()
-    cp(me, xn, 0, True).wait_send()
-
-    @pl.when(z < 3)
-    def _():
-        cp(me, up, 1, True).wait_send()
-
-    @pl.when(z > 0)
-    def _():
-        cp(me, dn, 2, True).wait_send()
-
-    cp(me, sib, 3, True).wait_send()
-
-    def sent(d, c):
-        a = 4 + (d - 1) * 6
-
-        @pl.when(z >= d)
-        def _():
-            s = me - 4 * d
-
-            @pl.when(z < 3)
-            def _():
-                cp(s, up, a).wait_send()
-
-            cp(s, xn, a + 1).wait_send()
-            cp(s, sib, a + 2).wait_send()
-
-        @pl.when(z + d <= 3)
-        def _():
-            s = me + 4 * d
-
-            @pl.when(z > 0)
-            def _():
-                cp(s, dn, a + 3).wait_send()
-
-            cp(s, xn, a + 4).wait_send()
-            cp(s, sib, a + 5).wait_send()
-
-        return c
-
-    lax.fori_loop(1, 4, sent, 0)
-
-    def sent_across(zz, c):
-        cp(xo + 4 * (zz - z), sib, 22 + zz).wait_send()
-        return c
-
-    lax.fori_loop(0, 4, sent_across, 0)
-
-
-def final_call(piece, tok, grad_resid, gain_full, small, d_all, own, other):
-    rows, width = tok.shape
-    sem = pltpu.SemaphoreType.DMA
-    return pl.pallas_call(
-        final_kernel,
-        out_shape=[
-            jax.ShapeDtypeStruct((H, *piece.shape), BF),
-            jax.ShapeDtypeStruct((rows, width), BF),
-            jax.ShapeDtypeStruct(small.shape, F32),
-        ],
-        in_specs=[VMEM] * 12,
-        out_specs=[ANY, VMEM, VMEM],
-        scratch_shapes=[
-            pltpu.VMEM((width, rows), F32),
-            pltpu.VMEM(small.shape, F32),
-            pltpu.VMEM((H, *small.shape), F32),
-            pltpu.VMEM(small.shape, F32),
-            pltpu.VMEM(small.shape, F32),
-            sem((26,)), sem((H,)), sem((H,)), sem((H,)), sem((2,)), sem((1,)),
-        ],
-        compiler_params=pltpu.CompilerParams(
-            collective_id=3, has_side_effects=True, vmem_limit_bytes=56 * 2**20
-        ),
-        name="final",
-    )(piece, tok, grad_resid, gain_full, small, d_all, *own, *other)
-
-
-def spread_kernel(dense_ref, heads_ref, dense_out, heads_out):
+        name="tail",
+    )(gt, *own, *held, *vm)
+
+
+def spread_kernel(dense_ref, heads_ref, *outs):
+    slab, cols = dense_ref.shape[-2:]
+    n, _, _, hd, _ = heads_ref.shape
     for zz in range(4):
         for xx in range(2):
-            slab, cols = dense_ref.shape[-2:]
-            dense_out[0, zz * slab : (zz + 1) * slab, xx * cols : (xx + 1) * cols] = dense_ref[
-                zz, xx, 0, 0
+            outs[0][zz * slab : (zz + 1) * slab, xx * cols : (xx + 1) * cols] = dense_ref[
+                zz, xx, 0, 0, 0
             ].astype(F32)
-    n, _, hd, cols = heads_ref.shape
-    heads_out[0] = heads_ref[...].reshape(n * hd, cols).astype(F32).T
-
-
-def spread_call(pieces):
-    n, parts, slab, cols = pieces.shape
-    split = pieces.reshape(4, 2, 2, parts, slab, cols)
+    outs[1][...] = heads_ref[...].reshape(n * hd, cols).astype(F32).T
+
+
+def spread_call(pieces, w):
+    n, _, _, slab, cols = pieces.shape
+    split = pieces.reshape(4, 2, 2, 2, 3, slab, cols)
     return pl.pallas_call(
         spread_kernel,
-        grid=(3, 2),
+        grid=(2,),
         out_shape=[
-            jax.ShapeDtypeStruct((3, 8 * slab, 2 * cols), F32),
-            jax.ShapeDtypeStruct((3, cols, n * slab), F32),
+            jax.ShapeDtypeStruct((8 * slab, 2 * cols), F32),
+            jax.ShapeDtypeStruct((cols, n * slab), F32),
         ],
         in_specs=[
-            pl.BlockSpec((4, 2, 1, 1, slab, cols), lambda w, h: (0, 0, h, w, 0, 0)),
-            pl.BlockSpec((n // 2, 1, slab, cols), lambda w, h: (h, 3 + w, 0, 0)),
+            pl.BlockSpec((4, 2, 1, 1, 1, slab, cols), lambda h: (0, 0, h, 0, w, 0, 0)),
+            pl.BlockSpec((n // 2, 1, 1, slab, cols), lambda h: (h, 1, w, 0, 0)),
         ],
         out_specs=[
-            pl.BlockSpec((1, 4 * slab, 2 * cols), lambda w, h: (w, h, 0)),
-            pl.BlockSpec((1, cols, n * slab // 2), lambda w, h: (w, 0, h)),
+            pl.BlockSpec((4 * slab, 2 * cols), lambda h: (h, 0)),
+            pl.BlockSpec((cols, n * slab // 2), lambda h: (0, h)),
         ],
         compiler_params=pltpu.CompilerParams(vmem_limit_bytes=48 * 2**20),
         name="spread",
@@ -1324,10 +1341,10 @@
 
     (
         h_all, gain_full, attn_t, o32, lse, qt, q, kt, k, v, raw,
-        out_o, inner_o, outer_o, query_o, key_o,
+        out_o, inner_o, outer_o, query_o,
     ) = forward_call(
         tok, gains, wt, scale_col, first_key,
-        (out_weight, inner_weight, outer_weight, query_weight, key_weight),
+        (out_weight, inner_weight, outer_weight, query_weight),
     )
     attn_t = attn_t.reshape(width, rows)
 
@@ -1352,23 +1369,18 @@
         cot.astype(F32) + norm_back(grad_hidden_two * gain_two, normed_two, scale_two)
     ).astype(BF)
     grad_att_t = dot(out_full, grad_resid, NT).astype(BF).reshape(H, HD, rows)
-    grad_outer = dot(active, cot, TN).astype(BF)
-    grad_inner = dot(hidden_two, grad_inner_pre, TN).astype(BF)
-    grad_outw = dot(attn_t, grad_resid).astype(BF)
-    d_all, piece, dscale, value_o = backward_call(
-        grad_att_t, (grad_outw, grad_inner, grad_outer), (value_weight,),
-        h_all, scale_col, first_key, k, v, kt, raw, q, qt, o32, lse,
-    )
     half = width // 2
-    small = jnp.zeros((8, width), F32).at[1].set(grad_gain_two).at[2, :HD].set(dscale[:, 0])
-    pieces, grad_tokens, sums = final_call(
-        piece, tok, grad_resid, gain_full, small, d_all,
-        (query_weight, key_weight, value_weight), (query_o, key_o, value_o),
-    )
-    dense, heads = spread_call(pieces)
+    pieces, grad_tokens, sums, *_ = tail_call(
+        grad_att_t, (query_weight, key_weight, value_weight), (query_o,),
+        (
+            attn_t, grad_resid, hidden_two.T, grad_inner_pre, active.T, cot, tok, gain_full,
+            grad_gain_two[None], h_all, scale_col, first_key, k, v, kt, raw, q, qt, o32, lse,
+        ),
+    )
+    (out_g, query_g), (inner_g, key_g), (outer_g, value_g) = [spread_call(pieces, w) for w in range(3)]
     gain_sums = lax.dynamic_slice(sums, (0, fs * half), (2, half))
     return (
-        result[None], grad_tokens[None], heads[0], heads[1], heads[2], dense[0], dense[1], dense[2],
+        result[None], grad_tokens[None], query_g, key_g, value_g, out_g, inner_g, outer_g,
         gain_sums[0], gain_sums[1], sums[2, :HD] / math.sqrt(HD),
     )
 

time: 385 us -> 336 us (0.87)
  Pallas kernels: 333 us -> 302 us
  local copies, waits for them, and re-layouts: 24 us -> 12 us
  matrix products: 22.2 us -> 13.4 us
    pallas_call x3 -> x4, Pallas kernels: 219 us -> 191 us  [the longest x1 177 us: tail_call(): pl.pallas_call(functools.partial(tail_kernel, n_w), out_shape=[jax.ShapeD...]
    squeeze x2 -> x0, local copies, waits for them, and re-layouts: 13.2 us -> none  [the longest x1 9.11 us: fast_local(): heads[2]]
    dot_general x9 -> x6, matrix products: 22.2 us -> 13.4 us  [dot(): return lax.dot_general(a, b, (dims, ((), ())), preferred_element_type=F32)]
where the time goes in v4:
time: 336 us; the launch traced here: 333 us
  Pallas kernels  302 us (90%)
  matrix products  13.4 us (4%)
  local copies, waits for them, and re-layouts  12 us (4%)
  other arithmetic  5.38 us (2%)
    pallas_call x1, Pallas kernels, tail_call(): pl.pallas_call(functools.partial(tail_kernel, n_w), out_shape=[jax.ShapeD...  177 us
    pallas_call x1, Pallas kernels, forward_call(): pl.pallas_call(functools.partial(forward_kernel, n_w), out_shape=shapes,...  111 us
    pallas_call x3, Pallas kernels, spread_call(): pl.pallas_call(spread_kernel, grid=(2,), out_shape=[jax.ShapeDtypeStruct(...  13.7 us
    dot_general x6, matrix products, dot(): return lax.dot_general(a, b, (dims, ((), ())), preferred_element_type=F32)  13.4 us

profile of v4, /device:TPU:0, one launch (start us, length us, event | category | flops | bytes accessed | tf_op | source)
XLA Modules:
  0.0 333.1 jit_solution(7186027758331457536)
XLA Ops:
  0.6 0.0 copy-start.16
  0.7 0.0 copy-start.12
  0.7 0.7 stack.10
  1.4 0.7 stack.9
  2.0 0.6 pad_maximum_fusion.1.gain_ref
  2.6 1.2 constant_dynamic-slice_fusion
  3.9 0.1 copy.42
  4.0 0.1 copy.41
  4.2 1.1 constant_dynamic-slice_fusion.2
  5.3 0.1 copy.40
  5.4 0.8 pad_maximum_fusion.wt_ref
  6.2 0.0 copy-done.16
  6.2 0.7 copy.34.scale_ref.rest_14_
  6.9 0.7 select_reduce_fusion
  7.6 110.8 %forward.1 = (bf16[8,512,1280]{2,1,0:T(8,128)(2,1)}, f32[2,1280]{1,0:T(2,128)}, bf16[16,80,256]{2,1,0:T(8,128)(2,1)}, f32[8,80,512]{2,1,0:T(8,128)}, f32[8,1,512...) custom-call(bf16[256,1280]{1,0:T(8,128)(2,1)} %bitcast.51, ...), custom_call_target="tpu_custom_call" | custom-call | tf_op jit(solution)/shard_map/forward/pallas_call | solution.py:684
  118.5 0.0 copy-start.4
  118.5 3.4 %multiply_reduce_fusion.2 = (f32[256]{0:T(256)S(1)}, f32[256,1280]{1,0:T(8,128)S(1)}) fusion(bf16[1280,256]{1,0:T(8,128)(2,1)} %bitcast.54, bf16[640,1280]{1,0:T(8,128)(2,1)} %get-tuple-element.36, bf16[640,1280]{1,0:T(8,128)(2,1)S(1)} %copy-done.5, pred[]{:T(512)S(6)} %eq.2, bf16[1,256,1280]{2,1,0:T(8,128)(2,1)S(1)} %copy-done.2), kind=kOutput, calls=%fused_computation.23 | convolution fusion | flops 854916864 | bytes 5899265 | tf_op jit(solution)/shard_map/dot_general | solution.py:354
  122.0 0.0 copy-done.11
  122.0 0.0 copy-done.4
  122.0 0.0 copy-done.14
  122.0 0.0 copy-start.3
  122.0 1.2 fusion.11
  123.3 0.0 copy-start.7
  123.3 0.2 copy-done.3
  123.5 0.5 copy-done.15
  124.0 2.2 fusion.4
  126.1 1.4 fusion.2.rest_7_
  127.5 0.0 copy-start.10
  127.5 1.2 fusion.10
  128.7 0.5 multiply_reduce_fusion
  129.2 0.0 copy-start.6
  129.2 0.4 add_convert_fusion.rest_5_
  129.7 1.0 copy-done.6
  130.7 0.5 copy-done.13
  131.2 4.0 %convolution_convert_fusion = bf16[1280,256]{1,0:T(8,128)(2,1)} fusion(bf16[256,1280]{1,0:T(8,128)(2,1)S(1)} %add_convert_fusion.rest_5_, bf16[640,1280]{1,0:T(8,128)(2,1)S(1)} %copy-done.13, bf16[640,1280]{1,0:T(8,128)(2,1)S(1)} %copy-done.6, pred[]{:T(512)S(6)} %eq.2), kind=kOutput, calls=%fused_computation.10 | convolution fusion | flops 853934080 | bytes 4587521 | tf_op jit(solution)/shard_map/dot_general | solution.py:354
  135.1 0.0 copy-done.1
  135.2 1.1 copy.37.rest_6_
  136.2 0.5 copy-done.8
  136.7 0.4 copy.36
  137.1 1.2 fusion.8.rest_8_
  138.3 0.6 broadcast_in_dim.28.rest_12_
  138.9 177.0 %tail.1 = (bf16[16,2,3,80,640]{4,3,2,1,0:T(8,128)(2,1)}, bf16[256,1280]{1,0:T(8,128)(2,1)}, f32[8,1280]{1,0:T(8,128)}, bf16[640,1280]{1,0:T(8,128)(2,1)}, bf16[640,1280]{1,0:T(8,128)(2,1)}) custom-call(bf16[16,80,256]{2,1,0:T(8,128)(2,1)} %bitcast.56, bf16[640,1280]{1,0:T(8,128)(2,1)} %rest_0_.3, bf16[640,1280]{1,0:T(8,128)(2,1)} %rest_1_.3, ...), custom_call_target="tpu_custom_call" | custom-call | tf_op jit(solution)/shard_map/tail/pallas_call | solution.py:1234
  315.9 4.5 %spread.3 = (f32[640,1280]{1,0:T(8,128)}, f32[640,1280]{1,0:T(8,128)}) custom-call(bf16[4,2,2,2,3,80,640]{6,5,4,3,2,1,0:T(8,128)(2,1)} %bitcast.47, bf16[16,2,3,80,640]{4,3,2,1,0:T(8,128)(2,1)} %get-tuple-element.51.heads_ref), custom_call_target="tpu_custom_call" | custom-call | tf_op jit(solution)/shard_map/spread/pallas_call | solution.py:1295
  320.5 4.5 %spread.4 = (f32[640,1280]{1,0:T(8,128)}, f32[640,1280]{1,0:T(8,128)}) custom-call(bf16[4,2,2,2,3,80,640]{6,5,4,3,2,1,0:T(8,128)(2,1)} %bitcast.48, bf16[16,2,3,80,640]{4,3,2,1,0:T(8,128)(2,1)} %get-tuple-element.51.heads_ref), custom_call_target="tpu_custom_call" | custom-call | tf_op jit(solution)/shard_map/spread/pallas_call | solution.py:1295
  325.0 4.6 %spread.5 = (f32[640,1280]{1,0:T(8,128)}, f32[640,1280]{1,0:T(8,128)}) custom-call(bf16[4,2,2,2,3,80,640]{6,5,4,3,2,1,0:T(8,128)(2,1)} %bitcast.49, bf16[16,2,3,80,640]{4,3,2,1,0:T(8,128)(2,1)} %get-tuple-element.51.heads_ref), custom_call_target="tpu_custom_call" | custom-call | tf_op jit(solution)/shard_map/spread/pallas_call | solution.py:1295
  329.6 1.5 dynamic-slice_reduce_fusion
  331.1 1.2 multiply_bitcast_fusion
  332.3 0.8 copy.44
  (21 shorter events, 0.1 us)
Async XLA Ops:
  0.6 5.5 %copy-start.16 = (f32[80]{0:T(128)S(1)}, f32[80]{0:T(128)}, u32[]{:S(2)}) copy-start(f32[80]{0:T(128)} %param.21) | copy-start | bytes 964
  0.7 6.2 %copy-start.12 = (s32[1,8]{1,0:T(1,128)S(1)}, s32[1,8]{1,0:T(1,128)}, u32[]{:S(2)}) copy-start(s32[1,8]{1,0:T(1,128)} %param.22) | copy-start | bytes 100
  7.6 110.8 %copy-start.2 = (bf16[1,256,1280]{2,1,0:T(8,128)(2,1)S(1)}, bf16[1,256,1280]{2,1,0:T(8,128)(2,1)}, u32[]{:S(2)}) copy-start(bf16[1,256,1280]{2,1,0:T(8,128)(2,1)} %param.12) | copy-start | bytes 1966084
  7.6 110.8 %copy-start.5 = (bf16[640,1280]{1,0:T(8,128)(2,1)S(1)}, bf16[640,1280]{1,0:T(8,128)(2,1)}, u32[]{:S(2)}) copy-start(bf16[640,1280]{1,0:T(8,128)(2,1)} %rest_0_.2) | copy-start | bytes 4915204
  118.5 3.5 %copy-start.11 = (f32[2,1280]{1,0:T(2,128)S(1)}, f32[2,1280]{1,0:T(2,128)}, u32[]{:S(2)}) copy-start(f32[2,1280]{1,0:T(2,128)} %get-tuple-element.37.rest_11_) | copy-start | bytes 30724
  118.5 3.5 %copy-start.4 = (bf16[640,1280]{1,0:T(8,128)(2,1)S(1)}, bf16[640,1280]{1,0:T(8,128)(2,1)}, u32[]{:S(2)}) copy-start(bf16[640,1280]{1,0:T(8,128)(2,1)} %rest_1_.2) | copy-start | bytes 4915204
  118.5 3.5 %copy-start.14 = (bf16[640,1280]{1,0:T(8,128)(2,1)S(1)}, bf16[640,1280]{1,0:T(8,128)(2,1)}, u32[]{:S(2)}) copy-start(bf16[640,1280]{1,0:T(8,128)(2,1)} %get-tuple-element.38) | copy-start | bytes 4915204
  122.0 1.4 copy-start.3
  122.0 1.9 copy-start.15
  123.3 2.9 copy-start.7
  124.0 2.2 copy-start
  127.5 1.2 copy-start.10
  129.2 1.4 copy-start.6
  129.2 1.9 copy-start.13
  131.1 4.0 %copy-start.1 = (bf16[256,1280]{1,0:T(8,128)(2,1)}, bf16[256,1280]{1,0:T(8,128)(2,1)S(1)}, u32[]{:S(2)}) copy-start(bf16[256,1280]{1,0:T(8,128)(2,1)S(1)} %add_convert_fusion.rest_5_) | copy-start | bytes 1966084
  135.2 1.6 copy-start.8
  325.0 7.3 %copy-start.9 = (bf16[256,1280]{1,0:T(8,128)(2,1)S(1)}, bf16[256,1280]{1,0:T(8,128)(2,1)}, u32[]{:S(2)}) copy-start(bf16[256,1280]{1,0:T(8,128)(2,1)} %get-tuple-element.50) | copy-start | bytes 1966084

commit v5 on v4

--- a/solution.py
+++ b/solution.py
@@ -359,6 +359,8 @@
 
 
 LOG2E = math.log2(math.e)
+N_SHARED = 0
+PULL = (1, 0)
 UNITS = H // 2
 
 
@@ -368,12 +370,36 @@
     yn = (me, 1 - fs)
     sib = (me + 1 - 2 * k, fs)
     n = len(own)
-    first = [remote(own[i].at[rows], other[i].at[rows], ssem.at[i], rsem.at[i], yn) for i in range(n)]
-    second = [
-        remote(other[i].at[rows], other[i].at[rows], ssem.at[n + i], rsem.at[n + i], sib)
-        for i in range(n)
-    ]
+
+    def first(i):
+        return remote(own[i].at[rows], other[i].at[rows], ssem.at[i], rsem.at[i], yn)
+
+    def second(i):
+        return remote(other[i].at[rows], other[i].at[rows], ssem.at[n + i], rsem.at[n + i], sib)
+
     return first, second
+
+
+def weight_share(own, other, k, x, fs, me, ssem, rsem):
+    quarter = own[0].shape[0] // 4 if own else 32
+    yn, sib, xn = (me, 1 - fs), (me + 1 - 2 * k, fs), (me + 2 - 4 * x, fs)
+
+    def rows(c, a):
+        return pl.ds(pl.multiple_of((c * 2 + a) * quarter, 32), quarter)
+
+    def over_y(i):
+        r = rows(k, x)
+        return remote(own[i].at[r], other[i].at[r], ssem.at[i, 0], rsem.at[i, 0], yn)
+
+    def over_x(i, a):
+        r = rows(k, a)
+        return remote(other[i].at[r], other[i].at[r], ssem.at[i, 1], rsem.at[i, 1], xn)
+
+    def over_core(i, c, a, n):
+        r = rows(c, a)
+        return remote(other[i].at[r], other[i].at[r], ssem.at[i, 2 + n], rsem.at[i, 2 + n], sib)
+
+    return over_y, over_x, over_core
 
 
 def visible(j, i, rows, first_key):
@@ -382,20 +408,26 @@
     return (kpos <= qpos) & (kpos >= first_key)
 
 
-def forward_kernel(n_w, tok_ref, gain_ref, wt_ref, scale_ref, first_ref, *rest):
+def forward_kernel(n_w, n_x, tok_ref, gain_ref, wt_ref, scale_ref, first_ref, *rest):
     own = rest[:n_w]
     at = n_w
-    h_all, gain_full, attn_ref = rest[at : at + 3]
-    o32_ref, lse_ref, qt_ref, q_ref, kt_ref, k_ref, v_ref, raw_ref = rest[at + 3 : at + 11]
+    gain_full, attn_ref = rest[at : at + 2]
+    kept = rest[at + 2 : at + 11]
     other = rest[at + 11 : at + 11 + n_w]
     (
         wt_all, gain_own, gain_other, o_sc, vt_sc, m_sc, l_sc, acc_sc,
-        ssem, rsem, osend, orecv, wssem, wrsem, ysem, lsem,
+        h_all, o32_ref, lse_ref, qt_ref, q_ref, kt_ref, k_ref, v_ref, raw_ref,
+        ssem, rsem, osend, orecv, wssem, wrsem, xssem, xrsem, ysem, lsem, ksem,
     ) = rest[at + 11 + n_w :]
     me, fs, z, x, k = place()
     sib, xn, yn = (me + 1 - 2 * k, fs), (me + 2 - 4 * x, fs), (me, 1 - fs)
     up, dn = (me + 4, fs), (me - 4, fs)
     rows = tok_ref.shape[0]
+    here = (h_all, o32_ref, lse_ref, qt_ref, q_ref, kt_ref, k_ref, v_ref, raw_ref)
+
+    def keep(i, u):
+        return pltpu.make_async_copy(here[i].at[u], kept[i].at[u], ksem.at[i, u])
+
     unit_rows = 2 * rows
     bar = pltpu.get_barrier_semaphore()
     for i in range(1, H):
@@ -414,7 +446,9 @@
     wt_copy.start()
     wt_here = pltpu.make_async_copy(wt_ref, wt_all.at[:, columns], lsem.at[0])
     wt_here.start()
-    first, second = weight_pull(own, other, k, fs, me, wssem, wrsem)
+    n_y = n_w - n_x
+    first, second = weight_pull(own[:n_y], other[:n_y], k, fs, me, wssem, wrsem)
+    over_y, over_x, over_core = weight_share(own[n_y:], other[n_y:], k, x, fs, me, xssem, xrsem)
     gain_copy.wait()
     g_here = gain_own[...].astype(F32)
     g_there = gain_other[...].astype(F32)
@@ -444,8 +478,10 @@
         cp(me, dn, 2).start()
 
     cp(me, sib, 3).start()
-    for c in first:
-        c.start()
+    for i in range(n_y):
+        first(i).start()
+    for i in range(n_x):
+        over_y(i).start()
     wt_here.wait()
     wt_copy.wait()
 
@@ -484,6 +520,8 @@
         u = uz * 2 + ux
         cp(u * 2 + 1 - k, sib, 0).wait_recv()
         project(u)
+        for i in (0, 3, 4, 5, 6, 7, 8):
+            keep(i, u).start()
         pair(u, u)
         mine = when_here(uz, ux)
 
@@ -547,13 +585,12 @@
         def _():
             across_arrival(d - 1)
 
-        for i in range(n_w):
-            if i < 4:
-
-                @pl.when(d == i + 1)
-                def _(i=i):
-                    first[i].wait_recv()
-                    second[i].start()
+        for i in range(min(n_y, 4)):
+
+            @pl.when(d == i + 1)
+            def _(i=i):
+                first(i).wait_recv()
+                second(i).start()
 
         def compute(n, c2):
             across = 1 - n // 2
@@ -585,6 +622,8 @@
         o32_ref[u] = out
         o_sc[u] = out.astype(BF)
         lse_ref[u] = m_sc[u] + jnp.log2(l_sc[u])
+        keep(1, u).start()
+        keep(2, u).start()
 
         def send(e, c2):
             b = u * 2 + e
@@ -602,9 +641,13 @@
         return lax.fori_loop(0, 2, send, c)
 
     lax.fori_loop(0, UNITS, finish, 0)
-    for i in range(4, n_w):
-        first[i].wait_recv()
-        second[i].start()
+    for i in range(4, n_y):
+        first(i).wait_recv()
+        second(i).start()
+    for i in range(n_x):
+        over_y(i).wait_recv()
+        over_x(i, x).start()
+        over_core(i, k, x, 0).start()
 
     def taken(b, c):
         @pl.when(b != me)
@@ -615,6 +658,13 @@
 
     lax.fori_loop(0, H, taken, 0)
     pltpu.make_async_copy(out_copy(me), attn_ref.at[me], lsem.at[1]).wait()
+
+    def all_kept(u, c):
+        for i in range(9):
+            keep(i, u).wait()
+        return c
+
+    lax.fori_loop(0, UNITS, all_kept, 0)
     cp(me, xn, 0).wait_send()
 
     @pl.when(z < 3)
@@ -661,12 +711,22 @@
         return c
 
     lax.fori_loop(0, 4, sent_across, 0)
-    for i in range(n_w):
-        first[i].wait_send()
-        second[i].wait()
-
-
-def forward_call(tok, gains, wt, scale_col, first_key, weights):
+    for i in range(n_x):
+        over_x(i, 1 - x).wait_recv()
+        over_core(i, k, 1 - x, 1).start()
+    for i in range(n_y):
+        first(i).wait_send()
+        second(i).wait()
+    for i in range(n_x):
+        over_y(i).wait_send()
+        over_x(i, x).wait_send()
+        over_core(i, k, x, 0).wait_send()
+        over_core(i, k, 1 - x, 1).wait_send()
+        over_core(i, 1 - k, x, 0).wait_recv()
+        over_core(i, 1 - k, 1 - x, 1).wait_recv()
+
+
+def forward_call(tok, gains, wt, scale_col, first_key, weights, n_x):
     n_w = len(weights)
     rows, width = tok.shape
     ur = 2 * rows
@@ -674,18 +734,20 @@
     def out(dtype, *shape):
         return jax.ShapeDtypeStruct((UNITS, *shape), dtype)
 
+    kept = [
+        out(BF, ur, width), out(F32, HD, ur), out(F32, 1, ur), out(BF, HD, ur), out(BF, ur, HD),
+        out(BF, HD, ur), out(BF, ur, HD), out(BF, ur, HD), out(F32, HD, ur),
+    ]
     shapes = [
-        out(BF, ur, width),
         jax.ShapeDtypeStruct((gains.shape[0], 2 * gains.shape[1]), F32),
         jax.ShapeDtypeStruct((H, HD, rows), BF),
-        out(F32, HD, ur), out(F32, 1, ur), out(BF, HD, ur), out(BF, ur, HD), out(BF, HD, ur),
-        out(BF, ur, HD), out(BF, ur, HD), out(F32, HD, ur),
+        *kept,
     ] + [jax.ShapeDtypeStruct(w.shape, BF) for w in weights]
     return pl.pallas_call(
-        functools.partial(forward_kernel, n_w),
+        functools.partial(forward_kernel, n_w, n_x),
         out_shape=shapes,
         in_specs=[VMEM] * 5 + [ANY] * n_w,
-        out_specs=[VMEM, VMEM, ANY] + [VMEM] * 8 + [ANY] * n_w,
+        out_specs=[VMEM] + [ANY] * (10 + n_w),
         scratch_shapes=[
             pltpu.VMEM((wt.shape[0], 2 * wt.shape[1]), BF),
             pltpu.VMEM(gains.shape, BF),
@@ -695,14 +757,18 @@
             pltpu.VMEM((UNITS, 1, ur), F32),
             pltpu.VMEM((UNITS, 1, ur), F32),
             pltpu.VMEM((UNITS, HD, ur), F32),
+            *[pltpu.VMEM(a.shape, a.dtype) for a in kept],
             pltpu.SemaphoreType.DMA((26,)),
             pltpu.SemaphoreType.DMA((H,)),
             pltpu.SemaphoreType.DMA((H,)),
             pltpu.SemaphoreType.DMA((H,)),
             pltpu.SemaphoreType.DMA((2 * n_w,)),
             pltpu.SemaphoreType.DMA((2 * n_w,)),
+            pltpu.SemaphoreType.DMA((max(1, n_x), 4)),
+            pltpu.SemaphoreType.DMA((max(1, n_x), 4)),
             pltpu.SemaphoreType.DMA((4,)),
             pltpu.SemaphoreType.DMA((2,)),
+            pltpu.SemaphoreType.DMA((9, UNITS)),
         ],
         compiler_params=pltpu.CompilerParams(
             collective_id=1, has_side_effects=True, vmem_limit_bytes=56 * 2**20
@@ -715,22 +781,25 @@
     return pl.ds(pl.multiple_of(start, align), size)
 
 
-def tail_kernel(n_w, gt_ref, *rest):
+def tail_kernel(gt_ref, *rest):
     own = rest[:3]
+    n_w = len(PULL)
     held = rest[3 : 6 - n_w]
     at = 6 - n_w
     (
         attn_ref, gr_ref, hid_ref, gip_ref, act_ref, cot_ref, tok_ref, gain_ref, g2_ref,
-        h_ref, scale_ref, first_ref, k_ref, v_ref, kt_ref, raw_ref, q_ref, qt_ref, o_ref, lse_ref,
-    ) = rest[at : at + 20]
+        scale_ref, first_ref,
+    ) = rest[at : at + 11]
+    kept = rest[at + 11 : at + 20]
     at += 20
     all_ref, tg_ref, sums_ref = rest[at : at + 3]
     pulled = rest[at + 3 : at + 3 + n_w]
     (
+        h_ref, o_ref, lse_ref, qt_ref, q_ref, kt_ref, k_ref, v_ref, raw_ref,
         g_in, g_sc, delta_sc, dq_sc, scale_sc, dk_sc, dv_sc, d_sc, got, dw_sc, dw_out, dw_got, piece,
-        s1, r0, so, ra, rb, r2, rz, e_sc, small_out, small_in, small_y, small_got,
-        gsend, grecv, qsend, qrecv, ksend, krecv, wssem, wrsem, dsend, drecv, psend, precv,
-        asend, arecv, vsend, vrecv, lsem, wsem,
+        s1, r0, so, ra, rb, r2, rz, e_sc, small_out, small_in, small_z,
+        gsend, grecv, qsend, qrecv, ksend, krecv, dsend, drecv, psend, precv,
+        asend, arecv, vsend, vrecv, lsem, wsem, ksem, wssem, wrsem,
     ) = rest[at + 3 + n_w :]
     me, fs, z, x, k = place()
     sib, xn, yn = (me + 1 - 2 * k, fs), (me + 2 - 4 * x, fs), (me, 1 - fs)
@@ -745,6 +814,11 @@
     for i in range(1, H):
         signal((lax.rem(me + i, H), fs))
     signal(yn)
+    here = (h_ref, o_ref, lse_ref, qt_ref, q_ref, kt_ref, k_ref, v_ref, raw_ref)
+    back = [pltpu.make_async_copy(kept[i], here[i], ksem.at[i]) for i in range(9)]
+    for c in back[1:]:
+        c.start()
+    back[0].start()
     pl.semaphore_wait(bar, H)
 
     def lanes(b):
@@ -762,6 +836,7 @@
     lax.fori_loop(1, H, g_start, 0)
     g_here = pltpu.make_async_copy(gt_ref.at[me], g_in.at[me // 2, :, lanes(me)], lsem.at[0])
     g_here.start()
+    first, second = weight_pull([own[w] for w in PULL], pulled, k, fs, me, wssem, wrsem)
 
     def theirs(g):
         return remote(so.at[g], r0.at[g], dsend.at[g], drecv.at[g], sib)
@@ -796,10 +871,18 @@
 
     slab = part // 4
 
-    def z_copy(t, slot, sem):
+    zb = lax.rem(z, 2)
+    near, far = (me + 4 - 8 * zb, fs), (me + 8 - 16 * (z // 2), fs)
+
+    def z_rows(t):
+        return s1.at[:, fs, half_rows(t * slab, slab, 16), x_here]
+
+    def z_near(i):
+        return remote(z_rows(1 - zb + 2 * i), rz.at[i], psend.at[4, i], precv.at[4, i], near)
+
+    def z_far():
         return remote(
-            s1.at[:, fs, half_rows(t * slab, slab, 16), x_here],
-            rz.at[slot], psend.at[4, sem], precv.at[4, slot], (me + 4 * (t - z), fs),
+            z_rows(zb + 2 * (1 - z // 2)), rz.at[2], psend.at[4, 2], precv.at[4, 2], far
         )
 
     for g in range(n_g):
@@ -822,13 +905,17 @@
                 pltpu.make_async_copy(own[w].at[pl.ds(f * part, part)], r0.at[w, f], wsem.at[w * 2 + f])
             )
             loads[-1].start()
-    for w in range(3 - n_w):
+
+
+    def load_other(src, w, f):
+        return pltpu.make_async_copy(
+            src.at[pl.ds(f * part, part)], so.at[w, f], wsem.at[6 + w * 2 + f]
+        )
+
+    for i, w in enumerate(w for w in range(3) if w not in PULL):
         for f in range(2):
-            loads.append(
-                pltpu.make_async_copy(held[w].at[pl.ds(f * part, part)], so.at[w, f], wsem.at[6 + w * 2 + f])
-            )
+            loads.append(load_other(held[i], w, f))
             loads[-1].start()
-    first, second = weight_pull(own[3 - n_w :], pulled, k, fs, me, wssem, wrsem)
 
     def after_one():
         for g in range(n_g):
@@ -846,8 +933,8 @@
             lax.fori_loop(0, part // 64, add, 0)
             stage(g, 2).start()
             stage(g, 3).start()
-        for c in first:
-            c.start()
+        for i in range(n_w):
+            first(i).start()
 
     def after_two():
         for g in range(n_g):
@@ -860,20 +947,22 @@
                 return c
 
             lax.fori_loop(0, part // 32, add, 0)
-        for d in range(1, 4):
-            t = lax.rem(z + d, 4)
-            z_copy(t, z, d).start()
-
-    def after_three():
-        for d in range(1, 4):
-            t = lax.rem(z + d, 4)
-            z_copy(t, t, d).wait()
-        here = half_rows(z * slab, slab, 16)
+        for i in range(2):
+            z_near(i).start()
+
+    def after_near():
+        for i in range(2):
+            z_near(i).wait()
+            r = half_rows((zb + 2 * i) * slab, slab, 16)
+            for g in range(n_g):
+                s1[g, fs, r, x_here] += rz[i, g]
+        z_far().start()
+
+    def after_far():
+        z_far().wait()
+        r = half_rows(z * slab, slab, 16)
         for g in range(n_g):
-            total = s1[g, fs, here, x_here].astype(F32)
-            for d in range(1, 4):
-                total = total + rz[lax.rem(z + d, 4), g].astype(F32)
-            piece[0, g] = total.astype(BF)
+            piece[g] = s1[g, fs, r, x_here] + rz[2, g]
 
     scale_sc[...] = jnp.zeros_like(scale_sc)
     dw_sc[...] = jnp.zeros_like(dw_sc)
@@ -883,6 +972,8 @@
         g_copy(b, b).wait()
         return c
 
+    for c in back[1:]:
+        c.wait()
     g_here.wait()
     lax.fori_loop(1, H, g_taken, 0)
 
@@ -894,6 +985,8 @@
         return c
 
     lax.fori_loop(0, units, prepare, 0)
+
+    back[0].wait()
 
     def pair(masked, j, i):
         s = dot(k_ref[j], qt_ref[i])
@@ -969,6 +1062,25 @@
         return c
 
     lax.fori_loop(0, units, column, 0)
+    half = dw_out.shape[2]
+
+    def dw_copy(n, lo, size):
+        return remote(
+            dw_out.at[pl.ds(lo, size)], dw_got.at[pl.ds(lo, size)], vsend.at[6 + n], vrecv.at[6 + n], yn
+        )
+
+    def dw_send(n, lo, size):
+        away = half_rows((1 - fs) * half, half, 128)
+        dw_out[lo : lo + size] = dw_sc[lo : lo + size, :, away].astype(BF)
+        dw_copy(n, lo, size).start()
+
+    def dw_take(n, lo, size):
+        dw_copy(n, lo, size).wait()
+        keep = half_rows(fs * half, half, 128)
+        total = dw_sc[lo : lo + size, :, keep] + dw_got[lo : lo + size].astype(F32)
+        piece[3 + lo : 3 + lo + size] = total.astype(BF)
+
+    dw_send(0, 1, 2)
 
     def queries(n, c):
         i = lax.rem(me // 2 + n, units)
@@ -993,29 +1105,26 @@
         return c
 
     lax.fori_loop(0, units, queries, 0)
-    for i in range(n_w):
-        first[i].wait_recv()
-        second[i].start()
-
     def query_weight(i, c):
         dw_sc[0] += dot(d_sc[i, 0], h_ref[i])
         return c
 
     lax.fori_loop(0, units, query_weight, 0)
-    half = dw_out.shape[2]
-    dw_out[...] = dw_sc[:, :, half_rows((1 - fs) * half, half, 128)].astype(BF)
-    dw_copy = remote(dw_out, dw_got, vsend.at[H], vrecv.at[H], yn)
-    dw_copy.start()
+    dw_send(1, 0, 1)
     small_out[...] = jnp.zeros_like(small_out)
     small_out[1:2, :] = g2_ref[...]
     small_out[2:3, :HD] = jnp.sum(scale_sc[...].T, axis=0, keepdims=True)
 
+    spans = (pl.ds(0, 3), pl.ds(4, 2), pl.ds(3, 1))
+
     def cp(p, s, t, si, mine=False):
-        here = all_ref.at[s, p]
-        return remote(piece.at[p] if mine else here, here, asend.at[p, si], arecv.at[p, s], t)
+        here = all_ref.at[s, spans[p]]
+        return remote(piece.at[spans[p]] if mine else here, here, asend.at[p, si], arecv.at[p, s], t)
 
     def keep(p):
-        return pltpu.make_async_copy(piece.at[p], all_ref.at[me, p], lsem.at[3 + p])
+        return pltpu.make_async_copy(
+            piece.at[spans[p]], all_ref.at[me, spans[p]], lsem.at[3 + p]
+        )
 
     def begin(p):
         keep(p).start()
@@ -1075,96 +1184,118 @@
                 cp(p, s, xn, 0).wait_recv()
                 cp(p, s, sib, 22 + z + d).start()
 
-    dw_copy.wait()
-    piece[1] = (dw_sc[:, :, half_rows(fs * half, half, 128)] + dw_got[...].astype(F32)).astype(BF)
-    begin(1)
-    after_three()
-    begin(0)
-    column_arrival(1, 1)
-
-    for w in range(3 - n_w, 3):
-        i = w - (3 - n_w)
-        second[i].wait()
-        first[i].wait_send()
-        for f in range(2):
-            loads.append(
-                pltpu.make_async_copy(pulled[i].at[pl.ds(f * part, part)], so.at[w, f], wsem.at[6 + w * 2 + f])
-            )
-            loads[-1].start()
-
-    def taken(n, c):
+
+    def kv_taken(n, c):
         b = lax.rem(me + n, H)
         kv_copy(b, b).wait()
+        return c
+
+    def q_taken(n, c):
+        b = lax.rem(me + n, H)
         q_copy(b, b).wait()
         return c
 
-    lax.fori_loop(1, H, taken, 0)
-    kv_here.wait()
-    q_here.wait()
-    for c in loads:
-        c.wait()
-
-    def input_grad(w):
+    def input_grad(w, start):
         for r, m in ((fs, r0), (1 - fs, so)):
             for f in range(2):
                 at_rows = half_rows((r * 2 + f) * part, part, 64)
                 term = dot(m[w, f], got[w])
-                if w == 0:
+                if start:
                     e_sc[at_rows, :] = term
                 else:
                     e_sc[at_rows, :] += term
 
-    input_grad(0)
+    def pass_on(i):
+        first(i).wait_recv()
+        second(i).start()
+
+    def load_pulled(i):
+        second(i).wait()
+        first(i).wait_send()
+        late = [load_other(pulled[i], PULL[i], f) for f in range(2)]
+        for c in late:
+            c.start()
+        for c in late:
+            c.wait()
+
+    def v_copy(i, t):
+        n = (0, 1, 8)[i]
+        return remote(small_out, small_in.at[i], vsend.at[n], vrecv.at[n], t)
+
+    def v_column(d):
+        t = lax.rem(z + d, 4)
+        return t, remote(
+            small_z.at[z], small_z.at[z], vsend.at[2 + d], vrecv.at[2 + z], (me + 4 * (t - z), fs)
+        )
+
+    dw_take(0, 1, 2)
+    begin(1)
+    after_near()
+    dw_take(1, 0, 1)
+    begin(2)
+    pass_on(0)
+    lax.fori_loop(1, H, kv_taken, 0)
+    kv_here.wait()
+    for c in loads:
+        c.wait()
+    input_grad(2, True)
+    column_arrival(1, 1)
+    column_arrival(2, 1)
+    load_pulled(0)
+    input_grad(1, False)
+    across_arrival(1, 0)
+    across_arrival(2, 0)
+    after_far()
+    begin(0)
+    column_arrival(1, 2)
+    column_arrival(2, 2)
+    pass_on(1)
+    across_arrival(1, 1)
+    across_arrival(2, 1)
+    lax.fori_loop(1, H, q_taken, 0)
+    q_here.wait()
+    load_pulled(1)
+    input_grad(0, False)
     column_arrival(0, 1)
-    column_arrival(1, 2)
-    input_grad(1)
-    across_arrival(1, 0)
+    column_arrival(1, 3)
+    column_arrival(2, 3)
     across_arrival(0, 0)
-    column_arrival(0, 2)
-    column_arrival(1, 3)
-    input_grad(2)
     grad_hidden = e_sc[...].T
     tokens = tok_ref[...].astype(F32)
     scale = lax.rsqrt(jnp.mean(tokens * tokens, axis=-1, keepdims=True) + epsilon)
     normed = tokens * scale
     small_out[0:1, :] = jnp.sum(grad_hidden * normed, axis=0, keepdims=True)
-
-    def v_copy(b, t):
-        return remote(small_out, small_in.at[t], vsend.at[b], vrecv.at[t], (b, fs))
-
-    def v_start(n, c):
-        v_copy(lax.rem(me + n, H), me).start()
-        return c
-
-    lax.fori_loop(1, H, v_start, 0)
-    across_arrival(1, 1)
-    across_arrival(0, 1)
-    column_arrival(0, 3)
+    v_copy(0, sib).start()
+    across_arrival(1, 2)
+    across_arrival(2, 2)
+    column_arrival(0, 2)
     e = grad_hidden * gain_ref[0:1, :]
     tg_ref[...] = (
         gr_ref[...].astype(F32) + scale * (e - normed * jnp.mean(e * normed, axis=-1, keepdims=True))
     ).astype(BF)
-
-    def v_taken(n, c):
-        b = lax.rem(me + n, H)
-        v_copy(b, b).wait()
-        return c
-
-    lax.fori_loop(1, H, v_taken, 0)
-
-    def v_add(n, total):
-        return total + small_in[lax.rem(me + n, H)]
-
-    small_y[...] = lax.fori_loop(1, H, v_add, small_out[...])
-    y_copy = remote(small_y, small_got, vsend.at[H + 1], vrecv.at[H + 1], yn)
-    y_copy.start()
-    for d in range(2, 4):
-        across_arrival(1, d)
-        across_arrival(0, d)
-    y_copy.wait()
-    sums_ref[...] = small_y[...] + small_got[...]
-
-    for p in range(2):
+    v_copy(0, sib).wait()
+    small_out[...] += small_in[0]
+    v_copy(1, xn).start()
+    across_arrival(0, 1)
+    v_copy(1, xn).wait()
+    small_z[z] = small_out[...] + small_in[1]
+    for d in range(1, 4):
+        v_column(d)[1].start()
+    across_arrival(1, 3)
+    across_arrival(2, 3)
+    for d in range(1, 4):
+        t, c = v_column(d)
+        c.wait_send()
+        remote(small_z.at[t], small_z.at[t], vsend.at[2 + d], vrecv.at[2 + t], xn).wait_recv()
+    small_out[...] = (small_z[0] + small_z[1]) + (small_z[2] + small_z[3])
+    v_copy(2, yn).start()
+    column_arrival(0, 3)
+    across_arrival(0, 2)
+    v_copy(2, yn).wait()
+    sums_ref[...] = small_out[...] + small_in[2]
+    across_arrival(0, 3)
+
+    for p in (1, 2, 0):
 
         def from_sib(n, c, p=p):
             cp(p, n * 2 + 1 - k, sib, 0).wait_recv()
@@ -1220,28 +1351,29 @@
         lax.fori_loop(0, 4, sent_across, 0)
 
 
-ONE_AT = 2
-TWO_AT = 5
-
-
-def tail_call(gt, own, held, vm):
-    n_w = 3 - len(held)
+ONE_AT = 3
+TWO_AT = 6
+
+
+def tail_call(gt, own, held, vm, kept):
+    n_w = len(PULL)
     rows, width = vm[1].shape
-    n, ur = vm[9].shape[:2]
+    n, ur = kept[0].shape[:2]
     half = width // 2
     part = width // 4
     sem = pltpu.SemaphoreType.DMA
     return pl.pallas_call(
-        functools.partial(tail_kernel, n_w),
+        tail_kernel,
         out_shape=[
-            jax.ShapeDtypeStruct((H, 2, 3, part // 4, half), BF),
+            jax.ShapeDtypeStruct((H, 6, part // 4, half), BF),
             jax.ShapeDtypeStruct((rows, width), BF),
             jax.ShapeDtypeStruct((8, width), F32),
         ]
         + [jax.ShapeDtypeStruct(own[0].shape, BF)] * n_w,
-        in_specs=[ANY] * (4 + len(held)) + [VMEM] * len(vm),
+        in_specs=[ANY] * (4 + len(held)) + [VMEM] * len(vm) + [ANY] * len(kept),
         out_specs=[ANY, VMEM, VMEM] + [ANY] * n_w,
         scratch_shapes=[
+            *[pltpu.VMEM(a.shape, a.dtype) for a in kept],
             pltpu.VMEM((n, HD, ur), BF),
             pltpu.VMEM((n, ur, HD), BF),
             pltpu.VMEM((n, 1, ur), F32),
@@ -1254,44 +1386,44 @@
             pltpu.VMEM((3, HD, width), F32),
             pltpu.VMEM((3, HD, half), BF),
             pltpu.VMEM((3, HD, half), BF),
-            pltpu.VMEM((2, 3, part // 4, half), BF),
+            pltpu.VMEM((6, part // 4, half), BF),
             pltpu.VMEM((3, 2, part, width), BF),
             pltpu.VMEM((3, 2, part, width), BF),
             pltpu.VMEM((3, 2, part, width), BF),
             pltpu.VMEM((3, part // 2, width), BF),
             pltpu.VMEM((3, 2, part // 2, half), BF),
             pltpu.VMEM((3, part, half), BF),
-            pltpu.VMEM((4, 3, part // 4, half), BF),
+            pltpu.VMEM((3, 3, part // 4, half), BF),
             pltpu.VMEM((width, rows), F32),
             pltpu.VMEM((8, width), F32),
-            pltpu.VMEM((H, 8, width), F32),
-            pltpu.VMEM((8, width), F32),
-            pltpu.VMEM((8, width), F32),
+            pltpu.VMEM((3, 8, width), F32),
+            pltpu.VMEM((4, 8, width), F32),
             sem((H,)), sem((H,)), sem((H,)), sem((H,)), sem((H,)), sem((H,)),
-            sem((max(1, 2 * n_w),)), sem((max(1, 2 * n_w),)), sem((3,)), sem((3,)), sem((5, 4)), sem((5, 4)),
-            sem((2, 26)), sem((2, H)), sem((H + 2,)), sem((H + 2,)), sem((5,)), sem((12,)),
+            sem((3,)), sem((3,)), sem((5, 4)), sem((5, 4)),
+            sem((3, 26)), sem((3, H)), sem((9,)), sem((9,)), sem((6,)), sem((12,)),
+            sem((9,)), sem((max(1, 2 * n_w),)), sem((max(1, 2 * n_w),)),
         ],
         compiler_params=pltpu.CompilerParams(
             collective_id=2, has_side_effects=True, vmem_limit_bytes=62 * 2**20
         ),
         name="tail",
-    )(gt, *own, *held, *vm)
+    )(gt, *own, *held, *vm, *kept)
 
 
 def spread_kernel(dense_ref, heads_ref, *outs):
     slab, cols = dense_ref.shape[-2:]
-    n, _, _, hd, _ = heads_ref.shape
+    n, _, hd, _ = heads_ref.shape
     for zz in range(4):
         for xx in range(2):
             outs[0][zz * slab : (zz + 1) * slab, xx * cols : (xx + 1) * cols] = dense_ref[
-                zz, xx, 0, 0, 0
+                zz, xx, 0, 0
             ].astype(F32)
     outs[1][...] = heads_ref[...].reshape(n * hd, cols).astype(F32).T
 
 
 def spread_call(pieces, w):
-    n, _, _, slab, cols = pieces.shape
-    split = pieces.reshape(4, 2, 2, 2, 3, slab, cols)
+    n, parts, slab, cols = pieces.shape
+    split = pieces.reshape(4, 2, 2, parts, slab, cols)
     return pl.pallas_call(
         spread_kernel,
         grid=(2,),
@@ -1300,8 +1432,8 @@
             jax.ShapeDtypeStruct((cols, n * slab), F32),
         ],
         in_specs=[
-            pl.BlockSpec((4, 2, 1, 1, 1, slab, cols), lambda h: (0, 0, h, 0, w, 0, 0)),
-            pl.BlockSpec((n // 2, 1, 1, slab, cols), lambda h: (h, 1, w, 0, 0)),
+            pl.BlockSpec((4, 2, 1, 1, slab, cols), lambda h: (0, 0, h, w, 0, 0)),
+            pl.BlockSpec((n // 2, 1, slab, cols), lambda h: (h, 3 + w, 0, 0)),
         ],
         out_specs=[
             pl.BlockSpec((4 * slab, 2 * cols), lambda h: (h, 0)),
@@ -1340,11 +1472,11 @@
     scale_col = (query_scale / math.sqrt(HD))[:, None]
 
     (
-        h_all, gain_full, attn_t, o32, lse, qt, q, kt, k, v, raw,
-        out_o, inner_o, outer_o, query_o,
+        gain_full, attn_t, h_all, o32, lse, qt, q, kt, k, v, raw,
+        out_o, inner_o, outer_o, value_o,
     ) = forward_call(
         tok, gains, wt, scale_col, first_key,
-        (out_weight, inner_weight, outer_weight, query_weight),
+        (out_weight, inner_weight, outer_weight, value_weight), N_SHARED,
     )
     attn_t = attn_t.reshape(width, rows)
 
@@ -1371,11 +1503,12 @@
     grad_att_t = dot(out_full, grad_resid, NT).astype(BF).reshape(H, HD, rows)
     half = width // 2
     pieces, grad_tokens, sums, *_ = tail_call(
-        grad_att_t, (query_weight, key_weight, value_weight), (query_o,),
+        grad_att_t, (query_weight, key_weight, value_weight), (value_o,),
         (
             attn_t, grad_resid, hidden_two.T, grad_inner_pre, active.T, cot, tok, gain_full,
-            grad_gain_two[None], h_all, scale_col, first_key, k, v, kt, raw, q, qt, o32, lse,
+            grad_gain_two[None], scale_col, first_key,
         ),
+        (h_all, o32, lse, qt, q, kt, k, v, raw),
     )
     (out_g, query_g), (inner_g, key_g), (outer_g, value_g) = [spread_call(pieces, w) for w in range(3)]
     gain_sums = lax.dynamic_slice(sums, (0, fs * half), (2, half))

time: 336 us -> 321 us (0.955)
  Pallas kernels: 302 us -> 289 us
    pallas_call x2, Pallas kernels: 288 us -> 276 us  [the longest x1 169 us: tail_call(): pl.pallas_call(tail_kernel, out_shape=[jax.ShapeDtypeStruct((H, 6, part /...]
where the time goes in v5:
time: 321 us
  Pallas kernels  289 us (90%)
  matrix products  13.4 us (4%)
  local copies, waits for them, and re-layouts  12 us (4%)
  other arithmetic  5.38 us (2%)
    pallas_call x1, Pallas kernels, tail_call(): pl.pallas_call(tail_kernel, out_shape=[jax.ShapeDtypeStruct((H, 6, part /...  169 us
    pallas_call x1, Pallas kernels, forward_call(): pl.pallas_call(functools.partial(forward_kernel, n_w, n_x), out_shape=sha...  106 us
    pallas_call x3, Pallas kernels, spread_call(): pl.pallas_call(spread_kernel, grid=(2,), out_shape=[jax.ShapeDtypeStruct(...  13.7 us
    dot_general x6, matrix products, dot(): return lax.dot_general(a, b, (dims, ((), ())), preferred_element_type=F32)  13.4 us

profile of v5, /device:TPU:0, one launch (start us, length us, event | category | flops | bytes accessed | tf_op | source)
XLA Modules:
  0.0 320.9 jit_solution(17678511920229604842)
XLA Ops:
  0.6 0.0 copy-start.16
  0.7 0.0 copy-start.12
  0.7 0.7 stack.10
  1.4 0.7 stack.9
  2.0 0.6 pad_maximum_fusion.1.gain_ref
  2.6 1.2 constant_dynamic-slice_fusion
  3.9 0.1 copy.42
  4.0 0.1 copy.41
  4.2 1.1 constant_dynamic-slice_fusion.2
  5.3 0.1 copy.40
  5.4 0.8 pad_maximum_fusion.wt_ref
  6.2 0.0 copy-done.16
  6.2 0.7 copy.34.scale_ref.rest_13_
  6.9 0.0 copy-done.12
  6.9 0.7 select_reduce_fusion
  7.6 106.1 %forward.1 = (f32[2,1280]{1,0:T(2,128)}, bf16[16,80,256]{2,1,0:T(8,128)(2,1)}, bf16[8,512,1280]{2,1,0:T(8,128)(2,1)}, f32[8,80,512]{2,1,0:T(8,128)}, f32[8,1,512...) custom-call(bf16[256,1280]{1,0:T(8,128)(2,1)} %bitcast.51, ...), custom_call_target="tpu_custom_call" | custom-call | tf_op jit(solution)/shard_map/forward/pallas_call | solution.py:746
  113.7 0.0 copy-done.2
  113.8 0.0 copy-start.4
  113.8 3.4 %multiply_reduce_fusion.2 = (f32[256]{0:T(256)S(1)}, f32[256,1280]{1,0:T(8,128)S(1)}) fusion(bf16[1280,256]{1,0:T(8,128)(2,1)} %bitcast.54, bf16[640,1280]{1,0:T(8,128)(2,1)} %get-tuple-element.36, bf16[640,1280]{1,0:T(8,128)(2,1)S(1)} %copy-done.5, pred[]{:T(512)S(6)} %eq.2, bf16[1,256,1280]{2,1,0:T(8,128)(2,1)S(1)} %copy-done.2), kind=kOutput, calls=%fused_computation.23 | convolution fusion | flops 854916864 | bytes 5899265 | tf_op jit(solution)/shard_map/dot_general | solution.py:354
  117.3 0.0 copy-start.3
  117.3 1.2 fusion.11
  118.6 0.0 copy-start.7
  118.6 0.2 copy-done.3
  118.7 0.5 copy-done.15
  119.2 2.2 fusion.4
  121.4 0.0 copy-done.7
  121.4 1.4 fusion.2.rest_7_
  122.8 0.0 copy-start.10
  122.8 1.2 fusion.10
  124.0 0.5 multiply_reduce_fusion
  124.5 0.0 copy-start.6
  124.5 0.0 copy-start.13
  124.5 0.4 add_convert_fusion.rest_5_
  125.0 1.0 copy-done.6
  126.0 0.5 copy-done.13
  126.5 4.0 %convolution_convert_fusion = bf16[1280,256]{1,0:T(8,128)(2,1)} fusion(bf16[256,1280]{1,0:T(8,128)(2,1)S(1)} %add_convert_fusion.rest_5_, bf16[640,1280]{1,0:T(8,128)(2,1)S(1)} %copy-done.13, bf16[640,1280]{1,0:T(8,128)(2,1)S(1)} %copy-done.6, pred[]{:T(512)S(6)} %eq.2), kind=kOutput, calls=%fused_computation.10 | convolution fusion | flops 853934080 | bytes 4587521 | tf_op jit(solution)/shard_map/dot_general | solution.py:354
  130.5 1.1 copy.37.rest_6_
  131.5 0.5 copy-done.8
  132.0 0.4 copy.36
  132.4 1.2 fusion.8.rest_8_
  133.6 0.6 broadcast_in_dim.28.rest_12_
  134.2 169.5 %tail.1 = (bf16[16,6,80,640]{3,2,1,0:T(8,128)(2,1)}, bf16[256,1280]{1,0:T(8,128)(2,1)}, f32[8,1280]{1,0:T(8,128)}, bf16[640,1280]{1,0:T(8,128)(2,1)}, bf16[640,1280]{1,0:T(8,128)(2,1)}) custom-call(bf16[16,80,256]{2,1,0:T(8,128)(2,1)} %bitcast.56, bf16[640,1280]{1,0:T(8,128)(2,1)} %rest_0_.3, bf16[640,1280]{1,0:T(8,128)(2,1)} %rest_1_.3, ...), custom_call_target="tpu_custom_call" | custom-call | tf_op jit(solution)/shard_map/tail/pallas_call | solution.py:1365
  303.7 4.5 %spread.3 = (f32[640,1280]{1,0:T(8,128)}, f32[640,1280]{1,0:T(8,128)}) custom-call(bf16[4,2,2,6,80,640]{5,4,3,2,1,0:T(8,128)(2,1)} %bitcast.47, bf16[16,6,80,640]{3,2,1,0:T(8,128)(2,1)} %get-tuple-element.51.heads_ref), custom_call_target="tpu_custom_call" | custom-call | tf_op jit(solution)/shard_map/spread/pallas_call | solution.py:1427
  308.3 4.5 %spread.4 = (f32[640,1280]{1,0:T(8,128)}, f32[640,1280]{1,0:T(8,128)}) custom-call(bf16[4,2,2,6,80,640]{5,4,3,2,1,0:T(8,128)(2,1)} %bitcast.48, bf16[16,6,80,640]{3,2,1,0:T(8,128)(2,1)} %get-tuple-element.51.heads_ref), custom_call_target="tpu_custom_call" | custom-call | tf_op jit(solution)/shard_map/spread/pallas_call | solution.py:1427
  312.8 4.6 %spread.5 = (f32[640,1280]{1,0:T(8,128)}, f32[640,1280]{1,0:T(8,128)}) custom-call(bf16[4,2,2,6,80,640]{5,4,3,2,1,0:T(8,128)(2,1)} %bitcast.49, bf16[16,6,80,640]{3,2,1,0:T(8,128)(2,1)} %get-tuple-element.51.heads_ref), custom_call_target="tpu_custom_call" | custom-call | tf_op jit(solution)/shard_map/spread/pallas_call | solution.py:1427
  317.4 1.5 dynamic-slice_reduce_fusion
  318.9 1.2 multiply_bitcast_fusion
  320.1 0.8 copy.44
  (21 shorter events, 0.1 us)
Async XLA Ops:
  0.6 5.5 %copy-start.16 = (f32[80]{0:T(128)S(1)}, f32[80]{0:T(128)}, u32[]{:S(2)}) copy-start(f32[80]{0:T(128)} %param.21) | copy-start | bytes 964
  0.7 6.2 %copy-start.12 = (s32[1,8]{1,0:T(1,128)S(1)}, s32[1,8]{1,0:T(1,128)}, u32[]{:S(2)}) copy-start(s32[1,8]{1,0:T(1,128)} %param.22) | copy-start | bytes 100
  7.6 106.1 %copy-start.2 = (bf16[1,256,1280]{2,1,0:T(8,128)(2,1)S(1)}, bf16[1,256,1280]{2,1,0:T(8,128)(2,1)}, u32[]{:S(2)}) copy-start(bf16[1,256,1280]{2,1,0:T(8,128)(2,1)} %param.12) | copy-start | bytes 1966084
  7.6 106.1 %copy-start.5 = (bf16[640,1280]{1,0:T(8,128)(2,1)S(1)}, bf16[640,1280]{1,0:T(8,128)(2,1)}, u32[]{:S(2)}) copy-start(bf16[640,1280]{1,0:T(8,128)(2,1)} %rest_0_.2) | copy-start | bytes 4915204
  113.8 3.5 %copy-start.11 = (f32[2,1280]{1,0:T(2,128)S(1)}, f32[2,1280]{1,0:T(2,128)}, u32[]{:S(2)}) copy-start(f32[2,1280]{1,0:T(2,128)} %get-tuple-element.37.rest_11_) | copy-start | bytes 30724
  113.8 3.5 %copy-start.4 = (bf16[640,1280]{1,0:T(8,128)(2,1)S(1)}, bf16[640,1280]{1,0:T(8,128)(2,1)}, u32[]{:S(2)}) copy-start(bf16[640,1280]{1,0:T(8,128)(2,1)} %rest_1_.2) | copy-start | bytes 4915204
  113.8 3.5 %copy-start.14 = (bf16[640,1280]{1,0:T(8,128)(2,1)S(1)}, bf16[640,1280]{1,0:T(8,128)(2,1)}, u32[]{:S(2)}) copy-start(bf16[640,1280]{1,0:T(8,128)(2,1)} %get-tuple-element.38) | copy-start | bytes 4915204
  117.3 1.4 copy-start.3
  117.3 1.9 copy-start.15
  118.6 2.9 copy-start.7
  119.2 2.2 copy-start
  122.8 1.2 copy-start.10
  124.5 1.4 copy-start.6
  124.5 1.9 copy-start.13
  126.5 4.0 %copy-start.1 = (bf16[256,1280]{1,0:T(8,128)(2,1)}, bf16[256,1280]{1,0:T(8,128)(2,1)S(1)}, u32[]{:S(2)}) copy-start(bf16[256,1280]{1,0:T(8,128)(2,1)S(1)} %add_convert_fusion.rest_5_) | copy-start | bytes 1966084
  130.5 1.6 copy-start.8
  312.8 7.3 %copy-start.9 = (bf16[256,1280]{1,0:T(8,128)(2,1)S(1)}, bf16[256,1280]{1,0:T(8,128)(2,1)}, u32[]{:S(2)}) copy-start(bf16[256,1280]{1,0:T(8,128)(2,1)} %get-tuple-element.50) | copy-start | bytes 1966084

commit v6 on v5

--- a/solution.py
+++ b/solution.py
@@ -585,9 +585,9 @@
         def _():
             across_arrival(d - 1)
 
-        for i in range(min(n_y, 4)):
-
-            @pl.when(d == i + 1)
+        for i in range(1):
+
+            @pl.when(d == i + 2)
             def _(i=i):
                 first(i).wait_recv()
                 second(i).start()
@@ -641,7 +641,7 @@
         return lax.fori_loop(0, 2, send, c)
 
     lax.fori_loop(0, UNITS, finish, 0)
-    for i in range(4, n_y):
+    for i in range(1, n_y):
         first(i).wait_recv()
         second(i).start()
     for i in range(n_x):
@@ -1234,13 +1234,13 @@
     dw_take(1, 0, 1)
     begin(2)
     pass_on(0)
+    column_arrival(1, 1)
+    column_arrival(2, 1)
     lax.fori_loop(1, H, kv_taken, 0)
     kv_here.wait()
     for c in loads:
         c.wait()
     input_grad(2, True)
-    column_arrival(1, 1)
-    column_arrival(2, 1)
     load_pulled(0)
     input_grad(1, False)
     across_arrival(1, 0)
@@ -1249,26 +1249,26 @@
     begin(0)
     column_arrival(1, 2)
     column_arrival(2, 2)
-    pass_on(1)
+    column_arrival(0, 1)
+    across_arrival(0, 0)
     across_arrival(1, 1)
     across_arrival(2, 1)
+    pass_on(1)
     lax.fori_loop(1, H, q_taken, 0)
     q_here.wait()
     load_pulled(1)
     input_grad(0, False)
-    column_arrival(0, 1)
     column_arrival(1, 3)
     column_arrival(2, 3)
-    across_arrival(0, 0)
     grad_hidden = e_sc[...].T
     tokens = tok_ref[...].astype(F32)
     scale = lax.rsqrt(jnp.mean(tokens * tokens, axis=-1, keepdims=True) + epsilon)
     normed = tokens * scale
     small_out[0:1, :] = jnp.sum(grad_hidden * normed, axis=0, keepdims=True)
     v_copy(0, sib).start()
+    column_arrival(0, 2)
     across_arrival(1, 2)
     across_arrival(2, 2)
-    column_arrival(0, 2)
     e = grad_hidden * gain_ref[0:1, :]
     tg_ref[...] = (
         gr_ref[...].astype(F32) + scale * (e - normed * jnp.mean(e * normed, axis=-1, keepdims=True))
@@ -1281,6 +1281,7 @@
     small_z[z] = small_out[...] + small_in[1]
     for d in range(1, 4):
         v_column(d)[1].start()
+    column_arrival(0, 3)
     across_arrival(1, 3)
     across_arrival(2, 3)
     for d in range(1, 4):
@@ -1289,7 +1290,6 @@
         remote(small_z.at[t], small_z.at[t], vsend.at[2 + d], vrecv.at[2 + t], xn).wait_recv()
     small_out[...] = (small_z[0] + small_z[1]) + (small_z[2] + small_z[3])
     v_copy(2, yn).start()
-    column_arrival(0, 3)
     across_arrival(0, 2)
     v_copy(2, yn).wait()
     sums_ref[...] = small_out[...] + small_in[2]
@@ -1413,41 +1413,107 @@
 def spread_kernel(dense_ref, heads_ref, *outs):
     slab, cols = dense_ref.shape[-2:]
     n, _, hd, _ = heads_ref.shape
-    for zz in range(4):
-        for xx in range(2):
-            outs[0][zz * slab : (zz + 1) * slab, xx * cols : (xx + 1) * cols] = dense_ref[
-                zz, xx, 0, 0
-            ].astype(F32)
-    outs[1][...] = heads_ref[...].reshape(n * hd, cols).astype(F32).T
-
-
-def spread_call(pieces, w):
+    for w in range(3):
+
+        @pl.when(pl.program_id(0) // 2 == w)
+        def _(w=w):
+            for zz in range(4):
+                for xx in range(2):
+                    outs[w][zz * slab : (zz + 1) * slab, xx * cols : (xx + 1) * cols] = dense_ref[
+                        zz, xx, 0, 0
+                    ].astype(F32)
+            outs[3 + w][...] = heads_ref[...].reshape(n * hd, cols).astype(F32).T
+
+
+def spread_call(pieces):
     n, parts, slab, cols = pieces.shape
     split = pieces.reshape(4, 2, 2, parts, slab, cols)
+
+    def half(w):
+        return lambda i: jnp.clip(i - 2 * w, 0, 1)
+
+    def dense_spec(w):
+        return pl.BlockSpec((4 * slab, 2 * cols), lambda i: (half(w)(i), 0))
+
+    def heads_spec(w):
+        return pl.BlockSpec((cols, n * slab // 2), lambda i: (0, half(w)(i)))
+
     return pl.pallas_call(
         spread_kernel,
-        grid=(2,),
-        out_shape=[
-            jax.ShapeDtypeStruct((8 * slab, 2 * cols), F32),
-            jax.ShapeDtypeStruct((cols, n * slab), F32),
+        grid=(6,),
+        out_shape=[jax.ShapeDtypeStruct((8 * slab, 2 * cols), F32)] * 3
+        + [jax.ShapeDtypeStruct((cols, n * slab), F32)] * 3,
+        in_specs=[
+            pl.BlockSpec((4, 2, 1, 1, slab, cols), lambda i: (0, 0, lax.rem(i, 2), i // 2, 0, 0)),
+            pl.BlockSpec((n // 2, 1, slab, cols), lambda i: (lax.rem(i, 2), 3 + i // 2, 0, 0)),
         ],
-        in_specs=[
-            pl.BlockSpec((4, 2, 1, 1, slab, cols), lambda h: (0, 0, h, w, 0, 0)),
-            pl.BlockSpec((n // 2, 1, slab, cols), lambda h: (h, 3 + w, 0, 0)),
-        ],
-        out_specs=[
-            pl.BlockSpec((4 * slab, 2 * cols), lambda h: (h, 0)),
-            pl.BlockSpec((cols, n * slab // 2), lambda h: (0, h)),
-        ],
+        out_specs=[dense_spec(w) for w in range(3)] + [heads_spec(w) for w in range(3)],
         compiler_params=pltpu.CompilerParams(vmem_limit_bytes=48 * 2**20),
         name="spread",
     )(split, pieces)
 
 
-def joined(own, other, fs):
-    return jnp.where(
-        fs == 0, jnp.concatenate([own, other], axis=0), jnp.concatenate([other, own], axis=0)
-    )
+def dense_kernel(attn_ref, tok_ref, cot_ref, gain_ref, *rest):
+    weights = rest[:6]
+    out_ref, gr_ref, hid_ref, gip_ref, act_ref, ga_ref, g2_ref, w_sc, sem = rest[6:]
+    fs = lax.axis_index("fs")
+    half = weights[0].shape[0]
+    loads = []
+    for n, w in enumerate((0, 1, 2)):
+        for o in range(2):
+            r = pl.ds(pl.multiple_of((fs if o == 0 else 1 - fs) * half, 128), half)
+            loads.append(pltpu.make_async_copy(weights[2 * w + o], w_sc.at[w, r], sem.at[n, o]))
+            loads[-1].start()
+    gain = gain_ref[1:2, :]
+    tokens = tok_ref[...].astype(F32)
+    cot = cot_ref[...]
+    for c in loads[:2]:
+        c.wait()
+    resid = tokens + dot(attn_ref[...], w_sc[0], TN)
+    scale = lax.rsqrt(jnp.mean(resid * resid, axis=-1, keepdims=True) + epsilon)
+    normed = resid * scale
+    hidden32 = normed * gain
+    hidden = hidden32.astype(BF)
+    hid_ref[...] = hidden32.T.astype(BF)
+    for c in loads[2:4]:
+        c.wait()
+    pre = dot(hidden, w_sc[1])
+    sig = 1.0 / (1.0 + jnp.exp(-pre))
+    active32 = pre * sig
+    active = active32.astype(BF)
+    act_ref[...] = active32.T.astype(BF)
+    for c in loads[4:]:
+        c.wait()
+    grad_active = dot(cot, w_sc[2], NT)
+    gip = (grad_active * sig * (1.0 + pre * (1.0 - sig))).astype(BF)
+    gip_ref[...] = gip
+    grad_hidden = dot(gip, w_sc[1], NT)
+    g2_ref[...] = jnp.sum(grad_hidden * normed, axis=0, keepdims=True)
+    g = grad_hidden * gain
+    gr = (
+        cot.astype(F32) + scale * (g - normed * jnp.mean(g * normed, axis=-1, keepdims=True))
+    ).astype(BF)
+    gr_ref[...] = gr
+    ga_ref[...] = dot(w_sc[0], gr, NT).astype(BF)
+    out_ref[...] = (resid + dot(active, w_sc[2])).astype(BF)
+
+
+def dense_call(attn_t, tok, cot, gain_full, weights):
+    rows, width = tok.shape
+    tall = jax.ShapeDtypeStruct((width, rows), BF)
+    wide = jax.ShapeDtypeStruct((rows, width), BF)
+    return pl.pallas_call(
+        dense_kernel,
+        out_shape=[wide, wide, tall, wide, tall, tall, jax.ShapeDtypeStruct((1, width), F32)],
+        in_specs=[VMEM] * 4 + [ANY] * 6,
+        out_specs=[VMEM] * 7,
+        scratch_shapes=[
+            pltpu.VMEM((3, 2 * weights[0].shape[0], width), BF),
+            pltpu.SemaphoreType.DMA((3, 2)),
+        ],
+        compiler_params=pltpu.CompilerParams(vmem_limit_bytes=56 * 2**20),
+        name="dense",
+    )(attn_t, tok, cot, gain_full, *weights)
 
 
 def fast_local(
@@ -1480,37 +1546,21 @@
     )
     attn_t = attn_t.reshape(width, rows)
 
-    out_full = joined(out_weight, out_o, fs)
-    inner_full = joined(inner_weight, inner_o, fs)
-    outer_full = joined(outer_weight, outer_o, fs)
-    gain_one, gain_two = gain_full[0:1], gain_full[1:2]
-    token_rows = tok.astype(F32)
-    resid = token_rows + dot(attn_t, out_full, TN)
-    scale_two = rms_scale(resid)
-    normed_two = resid * scale_two
-    hidden_two = (normed_two * gain_two).astype(BF)
-    inner_pre = dot(hidden_two, inner_full)
-    active = jax.nn.silu(inner_pre).astype(BF)
-    result = (resid + dot(active, outer_full)).astype(BF)
-    grad_active = dot(cot, outer_full, NT)
-    sig = jax.nn.sigmoid(inner_pre)
-    grad_inner_pre = (grad_active * sig * (1.0 + inner_pre * (1.0 - sig))).astype(BF)
-    grad_hidden_two = dot(grad_inner_pre, inner_full, NT)
-    grad_gain_two = jnp.sum(grad_hidden_two * normed_two, axis=0)
-    grad_resid = (
-        cot.astype(F32) + norm_back(grad_hidden_two * gain_two, normed_two, scale_two)
-    ).astype(BF)
-    grad_att_t = dot(out_full, grad_resid, NT).astype(BF).reshape(H, HD, rows)
+    result, grad_resid, hidden_t, grad_inner_pre, active_t, grad_att_t, grad_gain_two = dense_call(
+        attn_t, tok, cot, gain_full,
+        (out_weight, out_o, inner_weight, inner_o, outer_weight, outer_o),
+    )
+    grad_att_t = grad_att_t.reshape(H, HD, rows)
     half = width // 2
     pieces, grad_tokens, sums, *_ = tail_call(
         grad_att_t, (query_weight, key_weight, value_weight), (value_o,),
         (
-            attn_t, grad_resid, hidden_two.T, grad_inner_pre, active.T, cot, tok, gain_full,
-            grad_gain_two[None], scale_col, first_key,
+            attn_t, grad_resid, hidden_t, grad_inner_pre, active_t, cot, tok, gain_full,
+            grad_gain_two, scale_col, first_key,
         ),
         (h_all, o32, lse, qt, q, kt, k, v, raw),
     )
-    (out_g, query_g), (inner_g, key_g), (outer_g, value_g) = [spread_call(pieces, w) for w in range(3)]
+    out_g, inner_g, outer_g, query_g, key_g, value_g = spread_call(pieces)
     gain_sums = lax.dynamic_slice(sums, (0, fs * half), (2, half))
     return (
         result[None], grad_tokens[None], query_g, key_g, value_g, out_g, inner_g, outer_g,

time: 321 us -> 297 us (0.925)
  matrix products: 13.4 us -> 0 us
  local copies, waits for them, and re-layouts: 12 us -> 7.21 us
  Pallas kernels: 289 us -> 285 us
    pallas_call x1, Pallas kernels: 106 us -> 91.1 us  [forward_call(): pl.pallas_call(functools.partial(forward_kernel, n_w, n_x), out_shape=sha...]
    dot_general x6 -> x0, matrix products: 13.4 us -> none  [dot(): return lax.dot_general(a, b, (dims, ((), ())), preferred_element_type=F32)]
    pallas_call x3 -> x2, Pallas kernels: 13.7 us -> 23.9 us  [the longest x1 12.6 us: spread_call(): pl.pallas_call(spread_kernel, grid=(6,), out_shape=[jax.ShapeDtypeStruct(...]
where the time goes in v6:
time: 297 us; the launch traced here: 296 us
  Pallas kernels  285 us (96%)
  local copies, waits for them, and re-layouts  7.21 us (2%)
  other arithmetic  3.26 us (1%)
    pallas_call x1, Pallas kernels, tail_call(): pl.pallas_call(tail_kernel, out_shape=[jax.ShapeDtypeStruct((H, 6, part /...  170 us
    pallas_call x1, Pallas kernels, forward_call(): pl.pallas_call(functools.partial(forward_kernel, n_w, n_x), out_shape=sha...  91.1 us
    pallas_call x1, Pallas kernels, spread_call(): pl.pallas_call(spread_kernel, grid=(6,), out_shape=[jax.ShapeDtypeStruct(...  12.6 us
    pallas_call x1, Pallas kernels, dense_call(): pl.pallas_call(dense_kernel, out_shape=[wide, wide, tall, wide, tall, tal...  11.3 us

profile of v6, /device:TPU:0, one launch (start us, length us, event | category | flops | bytes accessed | tf_op | source)
XLA Modules:
  0.0 296.3 jit_solution(10798890090527292304)
XLA Ops:
  0.6 0.0 copy-start.2
  0.7 0.0 copy-start.1
  0.7 0.7 stack.10
  1.4 0.7 stack.9
  2.0 0.6 pad_maximum_fusion.1.gain_ref
  2.6 1.2 constant_dynamic-slice_fusion
  3.9 0.1 copy.35
  4.0 0.1 copy.34
  4.2 1.1 constant_dynamic-slice_fusion.2
  5.3 0.1 copy.33
  5.4 0.8 pad_maximum_fusion.wt_ref
  6.2 0.0 copy-done.2
  6.2 0.7 copy.31.scale_ref.rest_13_
  6.9 0.0 copy-done.1
  6.9 0.7 select_reduce_fusion
  7.6 91.1 %forward.1 = (f32[2,1280]{1,0:T(2,128)}, bf16[16,80,256]{2,1,0:T(8,128)(2,1)}, bf16[8,512,1280]{2,1,0:T(8,128)(2,1)}, f32[8,80,512]{2,1,0:T(8,128)}, f32[8,1,512...) custom-call(bf16[256,1280]{1,0:T(8,128)(2,1)} %bitcast.17, ...), custom_call_target="tpu_custom_call" | custom-call | tf_op jit(solution)/shard_map/forward/pallas_call | solution.py:746
  98.8 11.3 %dense.1 = (bf16[256,1280]{1,0:T(8,128)(2,1)}, bf16[256,1280]{1,0:T(8,128)(2,1)}, bf16[1280,256]{1,0:T(8,128)(2,1)}, bf16[256,1280]{1,0:T(8,128)(2,1)}, bf16[128...) custom-call(bf16[1280,256]{1,0:T(8,128)(2,1)} %bitcast.22, bf16[256,1280]{1,0:T(8,128)(2,1)} %bitcast.18, ...), custom_call_target="tpu_custom_call" | custom-call | tf_op jit(solution)/shard_map/dense/pallas_call | solution.py:1505
  110.0 170.2 %tail.1 = (bf16[16,6,80,640]{3,2,1,0:T(8,128)(2,1)}, bf16[256,1280]{1,0:T(8,128)(2,1)}, f32[8,1280]{1,0:T(8,128)}, bf16[640,1280]{1,0:T(8,128)(2,1)}, bf16[640,1280]{1,0:T(8,128)(2,1)}) custom-call(bf16[16,80,256]{2,1,0:T(8,128)(2,1)} %bitcast.25, bf16[640,1280]{1,0:T(8,128)(2,1)} %rest_0_.5, bf16[640,1280]{1,0:T(8,128)(2,1)} %rest_1_.3, ...), custom_call_target="tpu_custom_call" | custom-call | tf_op jit(solution)/shard_map/tail/pallas_call | solution.py:1365
  280.2 0.0 copy-start
  280.2 12.6 %spread.1 = (f32[640,1280]{1,0:T(8,128)}, f32[640,1280]{1,0:T(8,128)}, f32[640,1280]{1,0:T(8,128)}, f32[640,1280]{1,0:T(8,128)}, f32[640,1280]{1,0:T(8,128)}, /*index=5*/f32[640,1280]{1,0:T(8,128)}) custom-call(bf16[4,2,2,6,80,640]{5,4,3,2,1,0:T(8,128)(2,1)} %bitcast.16, bf16[16,6,80,640]{3,2,1,0:T(8,128)(2,1)} %get-tuple-element.65.heads_ref), custom_call_target="tpu_custom_call" | custom-call | tf_op jit(solution)/shard_map/spread/pallas_call | solution.py:1441
  292.8 1.5 dynamic-slice_reduce_fusion
  294.3 1.2 multiply_bitcast_fusion
  295.5 0.0 copy-done
  295.5 0.8 copy.37
  (1 shorter events, 0.0 us)
Async XLA Ops:
  0.6 5.5 %copy-start.2 = (f32[80]{0:T(128)S(1)}, f32[80]{0:T(128)}, u32[]{:S(2)}) copy-start(f32[80]{0:T(128)} %param.21) | copy-start | bytes 964
  0.7 6.2 %copy-start.1 = (s32[1,8]{1,0:T(1,128)S(1)}, s32[1,8]{1,0:T(1,128)}, u32[]{:S(2)}) copy-start(s32[1,8]{1,0:T(1,128)} %param.22) | copy-start | bytes 100
  280.2 15.3 %copy-start = (bf16[256,1280]{1,0:T(8,128)(2,1)S(1)}, bf16[256,1280]{1,0:T(8,128)(2,1)}, u32[]{:S(2)}) copy-start(bf16[256,1280]{1,0:T(8,128)(2,1)} %get-tuple-element.64) | copy-start | bytes 1966084

commit v7 on v6

--- a/solution.py
+++ b/solution.py
@@ -781,52 +781,92 @@
     return pl.ds(pl.multiple_of(start, align), size)
 
 
-def tail_kernel(gt_ref, *rest):
+def tail_kernel(*rest):
     own = rest[:3]
     n_w = len(PULL)
     held = rest[3 : 6 - n_w]
     at = 6 - n_w
-    (
-        attn_ref, gr_ref, hid_ref, gip_ref, act_ref, cot_ref, tok_ref, gain_ref, g2_ref,
-        scale_ref, first_ref,
-    ) = rest[at : at + 11]
-    kept = rest[at + 11 : at + 20]
-    at += 20
-    all_ref, tg_ref, sums_ref = rest[at : at + 3]
-    pulled = rest[at + 3 : at + 3 + n_w]
+    mats = rest[at : at + 6]
+    attn_ref, cot_ref, tok_ref, gain_ref, scale_ref, first_ref = rest[at + 6 : at + 12]
+    kept = rest[at + 12 : at + 21]
+    at += 21
+    all_ref, tg_ref, sums_ref, out_ref = rest[at : at + 4]
+    pulled = rest[at + 4 : at + 4 + n_w]
     (
         h_ref, o_ref, lse_ref, qt_ref, q_ref, kt_ref, k_ref, v_ref, raw_ref,
-        g_in, g_sc, delta_sc, dq_sc, scale_sc, dk_sc, dv_sc, d_sc, got, dw_sc, dw_out, dw_got, piece,
-        s1, r0, so, ra, rb, r2, rz, e_sc, small_out, small_in, small_z,
+        g_in, g_sc, delta_sc, scale_sc, dk_sc, dv_sc, d_sc, got, dw_sc, dw_out, dw_got, piece,
+        ws, r0, ra, rb, r2, rz, small_out, small_in, small_z,
         gsend, grecv, qsend, qrecv, ksend, krecv, dsend, drecv, psend, precv,
         asend, arecv, vsend, vrecv, lsem, wsem, ksem, wssem, wrsem,
-    ) = rest[at + 3 + n_w :]
+        gt_ref, gr_ref, hid_ref, gip_ref, act_ref, g2_ref, msem,
+    ) = rest[at + 4 + n_w :]
     me, fs, z, x, k = place()
     sib, xn, yn = (me + 1 - 2 * k, fs), (me + 2 - 4 * x, fs), (me, 1 - fs)
     up, dn = (me + 4, fs), (me - 4, fs)
     units, rows = h_ref.shape[:2]
     block = rows // 2
     n_g = 3
-    part = s1.shape[2]
-    width = s1.shape[3]
+    part, width = ws.shape[2:]
+    so, s1 = ws.at[:, pl.ds(0, 2)], ws.at[:, pl.ds(2, 2)]
     cols = width // 2
     bar = pltpu.get_barrier_semaphore()
     for i in range(1, H):
         signal((lax.rem(me + i, H), fs))
     signal(yn)
+    dq_sc = o_ref
     here = (h_ref, o_ref, lse_ref, qt_ref, q_ref, kt_ref, k_ref, v_ref, raw_ref)
     back = [pltpu.make_async_copy(kept[i], here[i], ksem.at[i]) for i in range(9)]
     for c in back[1:]:
         c.start()
     back[0].start()
+    loads = []
+    for n in range(3):
+        for o in range(2):
+            for f in range(2):
+                to = ws.at[n, 2 * (fs if o == 0 else 1 - fs) + f]
+                src = mats[2 * n + o].at[pl.ds(f * part, part)]
+                loads.append(pltpu.make_async_copy(src, to, msem.at[n, 2 * o + f]))
+                loads[-1].start()
+
+    def mat(n):
+        return ws[n].reshape(4 * part, width)
+
     pl.semaphore_wait(bar, H)
+    first, second = weight_pull([own[w] for w in PULL], pulled, k, fs, me, wssem, wrsem)
+    for i in range(EARLY):
+        first(i).start()
+    gain = gain_ref[1:2, :]
+    for c in loads[:4]:
+        c.wait()
+    resid = tok_ref[...].astype(F32) + dot(attn_ref[...], mat(0), TN)
+    scale_two = lax.rsqrt(jnp.mean(resid * resid, axis=-1, keepdims=True) + epsilon)
+    normed_two = resid * scale_two
+    hidden32 = normed_two * gain
+    for c in loads[4:8]:
+        c.wait()
+    pre = dot(hidden32.astype(BF), mat(1))
+    sig = 1.0 / (1.0 + jnp.exp(-pre))
+    active32 = pre * sig
+    for c in loads[8:]:
+        c.wait()
+    grad_active = dot(cot_ref[...], mat(2), NT)
+    gip_ref[...] = (grad_active * sig * (1.0 + pre * (1.0 - sig))).astype(BF)
+    grad_two = dot(gip_ref[...], mat(1), NT)
+    g2_ref[...] = jnp.sum(grad_two * normed_two, axis=0, keepdims=True)
+    g = grad_two * gain
+    gr_ref[...] = (
+        cot_ref[...].astype(F32)
+        + scale_two * (g - normed_two * jnp.mean(g * normed_two, axis=-1, keepdims=True))
+    ).astype(BF)
+    gt_ref[...] = dot(mat(0), gr_ref[...], NT).astype(BF)
 
     def lanes(b):
         return half_rows(lax.rem(b, 2) * block, block, 128)
 
     def g_copy(b, t):
         return remote(
-            gt_ref.at[b], g_in.at[t // 2, :, lanes(t)], gsend.at[b], grecv.at[t], (b, fs)
+            gt_ref.at[half_rows(b * HD, HD, 16)], g_in.at[t // 2, :, lanes(t)],
+            gsend.at[b], grecv.at[t], (b, fs),
         )
 
     def g_start(n, c):
@@ -834,9 +874,13 @@
         return c
 
     lax.fori_loop(1, H, g_start, 0)
-    g_here = pltpu.make_async_copy(gt_ref.at[me], g_in.at[me // 2, :, lanes(me)], lsem.at[0])
+    g_here = pltpu.make_async_copy(
+        gt_ref.at[half_rows(me * HD, HD, 16)], g_in.at[me // 2, :, lanes(me)], lsem.at[0]
+    )
     g_here.start()
-    first, second = weight_pull([own[w] for w in PULL], pulled, k, fs, me, wssem, wrsem)
+    hid_ref[...] = hidden32.T.astype(BF)
+    act_ref[...] = active32.T.astype(BF)
+    out_ref[...] = (resid + dot(active32.astype(BF), mat(2))).astype(BF)
 
     def theirs(g):
         return remote(so.at[g], r0.at[g], dsend.at[g], drecv.at[g], sib)
@@ -933,7 +977,7 @@
             lax.fori_loop(0, part // 64, add, 0)
             stage(g, 2).start()
             stage(g, 3).start()
-        for i in range(n_w):
+        for i in range(EARLY, n_w):
             first(i).start()
 
     def after_two():
@@ -1198,12 +1242,13 @@
     def input_grad(w, start):
         for r, m in ((fs, r0), (1 - fs, so)):
             for f in range(2):
-                at_rows = half_rows((r * 2 + f) * part, part, 64)
-                term = dot(m[w, f], got[w])
+                side = half_rows(r * block, block, 128)
+                term = dot(m[w, f], got[w]).reshape(units // 2, HD, block)
+                span = pl.ds(f * (units // 2), units // 2)
                 if start:
-                    e_sc[at_rows, :] = term
+                    raw_ref[span, :, side] = term
                 else:
-                    e_sc[at_rows, :] += term
+                    raw_ref[span, :, side] += term
 
     def pass_on(i):
         first(i).wait_recv()
@@ -1260,7 +1305,10 @@
     input_grad(0, False)
     column_arrival(1, 3)
     column_arrival(2, 3)
-    grad_hidden = e_sc[...].T
+    grad_hidden = jnp.concatenate(
+        [raw_ref[:, :, r * block : (r + 1) * block].reshape(width // 2, block).T for r in range(2)],
+        axis=1,
+    )
     tokens = tok_ref[...].astype(F32)
     scale = lax.rsqrt(jnp.mean(tokens * tokens, axis=-1, keepdims=True) + epsilon)
     normed = tokens * scale
@@ -1351,13 +1399,14 @@
         lax.fori_loop(0, 4, sent_across, 0)
 
 
-ONE_AT = 3
-TWO_AT = 6
-
-
-def tail_call(gt, own, held, vm, kept):
+EARLY = 1
+ONE_AT = 4
+TWO_AT = 7
+
+
+def tail_call(own, held, mats, vm, kept):
     n_w = len(PULL)
-    rows, width = vm[1].shape
+    rows, width = vm[2].shape
     n, ur = kept[0].shape[:2]
     half = width // 2
     part = width // 4
@@ -1368,16 +1417,16 @@
             jax.ShapeDtypeStruct((H, 6, part // 4, half), BF),
             jax.ShapeDtypeStruct((rows, width), BF),
             jax.ShapeDtypeStruct((8, width), F32),
+            jax.ShapeDtypeStruct((rows, width), BF),
         ]
         + [jax.ShapeDtypeStruct(own[0].shape, BF)] * n_w,
-        in_specs=[ANY] * (4 + len(held)) + [VMEM] * len(vm) + [ANY] * len(kept),
-        out_specs=[ANY, VMEM, VMEM] + [ANY] * n_w,
+        in_specs=[ANY] * (9 + len(held)) + [VMEM] * len(vm) + [ANY] * len(kept),
+        out_specs=[ANY, VMEM, VMEM, VMEM] + [ANY] * n_w,
         scratch_shapes=[
             *[pltpu.VMEM(a.shape, a.dtype) for a in kept],
             pltpu.VMEM((n, HD, ur), BF),
             pltpu.VMEM((n, ur, HD), BF),
             pltpu.VMEM((n, 1, ur), F32),
-            pltpu.VMEM((n, HD, ur), F32),
             pltpu.VMEM((HD, ur), F32),
             pltpu.VMEM((ur, HD), F32),
             pltpu.VMEM((ur, HD), F32),
@@ -1387,14 +1436,12 @@
             pltpu.VMEM((3, HD, half), BF),
             pltpu.VMEM((3, HD, half), BF),
             pltpu.VMEM((6, part // 4, half), BF),
-            pltpu.VMEM((3, 2, part, width), BF),
-            pltpu.VMEM((3, 2, part, width), BF),
+            pltpu.VMEM((3, 4, part, width), BF),
             pltpu.VMEM((3, 2, part, width), BF),
             pltpu.VMEM((3, part // 2, width), BF),
             pltpu.VMEM((3, 2, part // 2, half), BF),
             pltpu.VMEM((3, part, half), BF),
             pltpu.VMEM((3, 3, part // 4, half), BF),
-            pltpu.VMEM((width, rows), F32),
             pltpu.VMEM((8, width), F32),
             pltpu.VMEM((3, 8, width), F32),
             pltpu.VMEM((4, 8, width), F32),
@@ -1402,12 +1449,15 @@
             sem((3,)), sem((3,)), sem((5, 4)), sem((5, 4)),
             sem((3, 26)), sem((3, H)), sem((9,)), sem((9,)), sem((6,)), sem((12,)),
             sem((9,)), sem((max(1, 2 * n_w),)), sem((max(1, 2 * n_w),)),
+            pltpu.VMEM((H * HD, rows), BF), pltpu.VMEM((rows, width), BF), pltpu.VMEM((width, rows), BF),
+            pltpu.VMEM((rows, width), BF), pltpu.VMEM((width, rows), BF), pltpu.VMEM((1, width), F32),
+            sem((3, 4)),
         ],
         compiler_params=pltpu.CompilerParams(
-            collective_id=2, has_side_effects=True, vmem_limit_bytes=62 * 2**20
+            collective_id=2, has_side_effects=True, vmem_limit_bytes=63 * 2**20
         ),
         name="tail",
-    )(gt, *own, *held, *vm, *kept)
+    )(*own, *held, *mats, *vm, *kept)
 
 
 def spread_kernel(dense_ref, heads_ref, *outs):
@@ -1453,69 +1503,6 @@
     )(split, pieces)
 
 
-def dense_kernel(attn_ref, tok_ref, cot_ref, gain_ref, *rest):
-    weights = rest[:6]
-    out_ref, gr_ref, hid_ref, gip_ref, act_ref, ga_ref, g2_ref, w_sc, sem = rest[6:]
-    fs = lax.axis_index("fs")
-    half = weights[0].shape[0]
-    loads = []
-    for n, w in enumerate((0, 1, 2)):
-        for o in range(2):
-            r = pl.ds(pl.multiple_of((fs if o == 0 else 1 - fs) * half, 128), half)
-            loads.append(pltpu.make_async_copy(weights[2 * w + o], w_sc.at[w, r], sem.at[n, o]))
-            loads[-1].start()
-    gain = gain_ref[1:2, :]
-    tokens = tok_ref[...].astype(F32)
-    cot = cot_ref[...]
-    for c in loads[:2]:
-        c.wait()
-    resid = tokens + dot(attn_ref[...], w_sc[0], TN)
-    scale = lax.rsqrt(jnp.mean(resid * resid, axis=-1, keepdims=True) + epsilon)
-    normed = resid * scale
-    hidden32 = normed * gain
-    hidden = hidden32.astype(BF)
-    hid_ref[...] = hidden32.T.astype(BF)
-    for c in loads[2:4]:
-        c.wait()
-    pre = dot(hidden, w_sc[1])
-    sig = 1.0 / (1.0 + jnp.exp(-pre))
-    active32 = pre * sig
-    active = active32.astype(BF)
-    act_ref[...] = active32.T.astype(BF)
-    for c in loads[4:]:
-        c.wait()
-    grad_active = dot(cot, w_sc[2], NT)
-    gip = (grad_active * sig * (1.0 + pre * (1.0 - sig))).astype(BF)
-    gip_ref[...] = gip
-    grad_hidden = dot(gip, w_sc[1], NT)
-    g2_ref[...] = jnp.sum(grad_hidden * normed, axis=0, keepdims=True)
-    g = grad_hidden * gain
-    gr = (
-        cot.astype(F32) + scale * (g - normed * jnp.mean(g * normed, axis=-1, keepdims=True))
-    ).astype(BF)
-    gr_ref[...] = gr
-    ga_ref[...] = dot(w_sc[0], gr, NT).astype(BF)
-    out_ref[...] = (resid + dot(active, w_sc[2])).astype(BF)
-
-
-def dense_call(attn_t, tok, cot, gain_full, weights):
-    rows, width = tok.shape
-    tall = jax.ShapeDtypeStruct((width, rows), BF)
-    wide = jax.ShapeDtypeStruct((rows, width), BF)
-    return pl.pallas_call(
-        dense_kernel,
-        out_shape=[wide, wide, tall, wide, tall, tall, jax.ShapeDtypeStruct((1, width), F32)],
-        in_specs=[VMEM] * 4 + [ANY] * 6,
-        out_specs=[VMEM] * 7,
-        scratch_shapes=[
-            pltpu.VMEM((3, 2 * weights[0].shape[0], width), BF),
-            pltpu.SemaphoreType.DMA((3, 2)),
-        ],
-        compiler_params=pltpu.CompilerParams(vmem_limit_bytes=56 * 2**20),
-        name="dense",
-    )(attn_t, tok, cot, gain_full, *weights)
-
-
 def fast_local(
     tokens, query_weight, key_weight, value_weight, out_weight, inner_weight, outer_weight,
     attn_gain, mlp_gain, query_scale, doc_starts, cotangent,
@@ -1546,18 +1533,11 @@
     )
     attn_t = attn_t.reshape(width, rows)
 
-    result, grad_resid, hidden_t, grad_inner_pre, active_t, grad_att_t, grad_gain_two = dense_call(
-        attn_t, tok, cot, gain_full,
+    half = width // 2
+    pieces, grad_tokens, sums, result, *_ = tail_call(
+        (query_weight, key_weight, value_weight), (value_o,),
         (out_weight, out_o, inner_weight, inner_o, outer_weight, outer_o),
-    )
-    grad_att_t = grad_att_t.reshape(H, HD, rows)
-    half = width // 2
-    pieces, grad_tokens, sums, *_ = tail_call(
-        grad_att_t, (query_weight, key_weight, value_weight), (value_o,),
-        (
-            attn_t, grad_resid, hidden_t, grad_inner_pre, active_t, cot, tok, gain_full,
-            grad_gain_two, scale_col, first_key,
-        ),
+        (attn_t, cot, tok, gain_full, scale_col, first_key),
         (h_all, o32, lse, qt, q, kt, k, v, raw),
     )
     out_g, inner_g, outer_g, query_g, key_g, value_g = spread_call(pieces)

time: 297 us -> 289 us (0.973)
  Pallas kernels: 285 us -> 278 us
    pallas_call x1 -> x0, Pallas kernels: 11.3 us -> none  [dense_call(): pl.pallas_call(dense_kernel, out_shape=[wide, wide, tall, wide, tall, tal...]
    pallas_call x1, Pallas kernels: 170 us -> 174 us  [tail_call(): pl.pallas_call(tail_kernel, out_shape=[jax.ShapeDtypeStruct((H, 6, part /...]
where the time goes in v7:
time: 289 us; the launch traced here: 288 us
  Pallas kernels  278 us (96%)
  local copies, waits for them, and re-layouts  6.71 us (2%)
  other arithmetic  3.27 us (1%)
    pallas_call x1, Pallas kernels, tail_call(): pl.pallas_call(tail_kernel, out_shape=[jax.ShapeDtypeStruct((H, 6, part /...  174 us
    pallas_call x1, Pallas kernels, forward_call(): pl.pallas_call(functools.partial(forward_kernel, n_w, n_x), out_shape=sha...  91.1 us
    pallas_call x1, Pallas kernels, spread_call(): pl.pallas_call(spread_kernel, grid=(6,), out_shape=[jax.ShapeDtypeStruct(...  12.6 us

profile of v7, /device:TPU:0, one launch (start us, length us, event | category | flops | bytes accessed | tf_op | source)
XLA Modules:
  0.0 288.3 jit_solution(5623092510387142944)
XLA Ops:
  0.6 0.0 copy-start.5
  0.7 0.0 copy-start.4
  0.7 0.0 copy-start.2
  0.7 0.0 copy-start.3
  0.7 1.3 constant_dynamic-slice_fusion
  1.9 0.1 copy.34
  2.1 0.1 copy.35
  2.2 1.1 constant_dynamic-slice_fusion.2
  3.3 0.1 copy.33
  3.5 0.8 pad_maximum_fusion.wt_ref
  4.2 0.0 copy-done.5
  4.2 0.7 copy.31.scale_ref.rest_14_
  5.0 0.0 copy-done.4
  5.0 0.7 select_reduce_fusion
  5.7 0.0 copy-done.2
  5.7 0.0 copy-done.3
  5.7 0.6 pad_maximum_fusion.1.gain_ref
  6.3 91.1 %forward.1 = (f32[2,1280]{1,0:T(2,128)}, bf16[16,80,256]{2,1,0:T(8,128)(2,1)}, bf16[8,512,1280]{2,1,0:T(8,128)(2,1)}, f32[8,80,512]{2,1,0:T(8,128)}, f32[8,1,512...) custom-call(bf16[256,1280]{1,0:T(8,128)(2,1)} %bitcast.16, ...), custom_call_target="tpu_custom_call" | custom-call | tf_op jit(solution)/shard_map/forward/pallas_call | solution.py:746
  97.5 173.9 %tail.1 = (bf16[16,6,80,640]{3,2,1,0:T(8,128)(2,1)}, bf16[256,1280]{1,0:T(8,128)(2,1)}, f32[8,1280]{1,0:T(8,128)}, bf16[256,1280]{1,0:T(8,128)(2,1)}, bf16[640,1...) custom-call(bf16[640,1280]{1,0:T(8,128)(2,1)} %rest_0_.3, bf16[640,1280]{1,0:T(8,128)(2,1)} %rest_1_.3, ...), custom_call_target="tpu_custom_call" | custom-call | tf_op jit(solution)/shard_map/tail/pallas_call | solution.py:1414
  271.3 0.0 copy-start.1
  271.3 12.6 %spread.1 = (f32[640,1280]{1,0:T(8,128)}, f32[640,1280]{1,0:T(8,128)}, f32[640,1280]{1,0:T(8,128)}, f32[640,1280]{1,0:T(8,128)}, f32[640,1280]{1,0:T(8,128)}, /*index=5*/f32[640,1280]{1,0:T(8,128)}) custom-call(bf16[4,2,2,6,80,640]{5,4,3,2,1,0:T(8,128)(2,1)} %bitcast.15, bf16[16,6,80,640]{3,2,1,0:T(8,128)(2,1)} %get-tuple-element.53.heads_ref), custom_call_target="tpu_custom_call" | custom-call | tf_op jit(solution)/shard_map/spread/pallas_call | solution.py:1491
  283.9 0.0 copy-start
  283.9 1.5 dynamic-slice_reduce_fusion
  285.4 1.2 multiply_bitcast_fusion
  286.6 0.0 copy-done.1
  286.6 0.8 copy.38
  287.5 0.0 copy-done
  287.5 0.8 copy.39
  (3 shorter events, 0.0 us)
Async XLA Ops:
  0.6 3.6 %copy-start.5 = (f32[80]{0:T(128)S(1)}, f32[80]{0:T(128)}, u32[]{:S(2)}) copy-start(f32[80]{0:T(128)} %param.21) | copy-start | bytes 964
  0.7 4.3 %copy-start.4 = (s32[1,8]{1,0:T(1,128)S(1)}, s32[1,8]{1,0:T(1,128)}, u32[]{:S(2)}) copy-start(s32[1,8]{1,0:T(1,128)} %param.22) | copy-start | bytes 100
  0.7 5.0 %copy-start.2 = (bf16[640]{0:T(1024)(128)(2,1)S(1)}, bf16[640]{0:T(1024)(128)(2,1)}, u32[]{:S(2)}) copy-start(bf16[640]{0:T(1024)(128)(2,1)} %param.20) | copy-start | bytes 3844
  0.7 5.0 %copy-start.3 = (bf16[640]{0:T(1024)(128)(2,1)S(1)}, bf16[640]{0:T(1024)(128)(2,1)}, u32[]{:S(2)}) copy-start(bf16[640]{0:T(1024)(128)(2,1)} %param.19) | copy-start | bytes 3844
  271.3 15.3 %copy-start.1 = (bf16[256,1280]{1,0:T(8,128)(2,1)S(1)}, bf16[256,1280]{1,0:T(8,128)(2,1)}, u32[]{:S(2)}) copy-start(bf16[256,1280]{1,0:T(8,128)(2,1)} %get-tuple-element.51) | copy-start | bytes 1966084
  283.9 3.5 %copy-start = (bf16[256,1280]{1,0:T(8,128)(2,1)S(1)}, bf16[256,1280]{1,0:T(8,128)(2,1)}, u32[]{:S(2)}) copy-start(bf16[256,1280]{1,0:T(8,128)(2,1)} %get-tuple-element.52) | copy-start | bytes 1966084

commit v8 on v7

--- a/solution.py
+++ b/solution.py
@@ -790,8 +790,8 @@
     attn_ref, cot_ref, tok_ref, gain_ref, scale_ref, first_ref = rest[at + 6 : at + 12]
     kept = rest[at + 12 : at + 21]
     at += 21
-    all_ref, tg_ref, sums_ref, out_ref = rest[at : at + 4]
-    pulled = rest[at + 4 : at + 4 + n_w]
+    all_ref, tg_ref, sums_ref, scale_out, out_ref = rest[at : at + 5]
+    pulled = rest[at + 5 : at + 5 + n_w]
     (
         h_ref, o_ref, lse_ref, qt_ref, q_ref, kt_ref, k_ref, v_ref, raw_ref,
         g_in, g_sc, delta_sc, scale_sc, dk_sc, dv_sc, d_sc, got, dw_sc, dw_out, dw_got, piece,
@@ -799,7 +799,7 @@
         gsend, grecv, qsend, qrecv, ksend, krecv, dsend, drecv, psend, precv,
         asend, arecv, vsend, vrecv, lsem, wsem, ksem, wssem, wrsem,
         gt_ref, gr_ref, hid_ref, gip_ref, act_ref, g2_ref, msem,
-    ) = rest[at + 4 + n_w :]
+    ) = rest[at + 5 + n_w :]
     me, fs, z, x, k = place()
     sib, xn, yn = (me + 1 - 2 * k, fs), (me + 2 - 4 * x, fs), (me, 1 - fs)
     up, dn = (me + 4, fs), (me - 4, fs)
@@ -1340,7 +1340,9 @@
     v_copy(2, yn).start()
     across_arrival(0, 2)
     v_copy(2, yn).wait()
-    sums_ref[...] = small_out[...] + small_in[2]
+    small_out[...] += small_in[2]
+    sums_ref[...] = small_out[0:2, half_rows(fs * cols, cols, 128)]
+    scale_out[...] = small_out[2:3, :HD] * (1.0 / math.sqrt(HD))
     across_arrival(0, 3)
 
     for p in (1, 2, 0):
@@ -1416,12 +1418,13 @@
         out_shape=[
             jax.ShapeDtypeStruct((H, 6, part // 4, half), BF),
             jax.ShapeDtypeStruct((rows, width), BF),
-            jax.ShapeDtypeStruct((8, width), F32),
+            jax.ShapeDtypeStruct((2, half), F32),
+            jax.ShapeDtypeStruct((1, HD), F32),
             jax.ShapeDtypeStruct((rows, width), BF),
         ]
         + [jax.ShapeDtypeStruct(own[0].shape, BF)] * n_w,
         in_specs=[ANY] * (9 + len(held)) + [VMEM] * len(vm) + [ANY] * len(kept),
-        out_specs=[ANY, VMEM, VMEM, VMEM] + [ANY] * n_w,
+        out_specs=[ANY, VMEM, VMEM, VMEM, VMEM] + [ANY] * n_w,
         scratch_shapes=[
             *[pltpu.VMEM(a.shape, a.dtype) for a in kept],
             pltpu.VMEM((n, HD, ur), BF),
@@ -1533,18 +1536,16 @@
     )
     attn_t = attn_t.reshape(width, rows)
 
-    half = width // 2
-    pieces, grad_tokens, sums, result, *_ = tail_call(
+    pieces, grad_tokens, gain_sums, scale_sum, result, *_ = tail_call(
         (query_weight, key_weight, value_weight), (value_o,),
         (out_weight, out_o, inner_weight, inner_o, outer_weight, outer_o),
         (attn_t, cot, tok, gain_full, scale_col, first_key),
         (h_all, o32, lse, qt, q, kt, k, v, raw),
     )
     out_g, inner_g, outer_g, query_g, key_g, value_g = spread_call(pieces)
-    gain_sums = lax.dynamic_slice(sums, (0, fs * half), (2, half))
     return (
         result[None], grad_tokens[None], query_g, key_g, value_g, out_g, inner_g, outer_g,
-        gain_sums[0], gain_sums[1], sums[2, :HD] / math.sqrt(HD),
+        gain_sums[0], gain_sums[1], scale_sum[0],
     )
 
 

time: 289 us -> 291 us (level)
  no operation moved by 1% of the time
where the time goes in v8:
time: 291 us
  Pallas kernels  278 us (96%)
  local copies, waits for them, and re-layouts  8.9 us (3%)
  other arithmetic  3.38 us (1%)
    pallas_call x1, Pallas kernels, tail_call(): pl.pallas_call(tail_kernel, out_shape=[jax.ShapeDtypeStruct((H, 6, part /...  174 us
    pallas_call x1, Pallas kernels, forward_call(): pl.pallas_call(functools.partial(forward_kernel, n_w, n_x), out_shape=sha...  91.1 us
    pallas_call x1, Pallas kernels, spread_call(): pl.pallas_call(spread_kernel, grid=(6,), out_shape=[jax.ShapeDtypeStruct(...  12.6 us

profile of v8, /device:TPU:0, one launch (start us, length us, event | category | flops | bytes accessed | tf_op | source)
XLA Modules:
  0.0 290.5 jit_solution(7989823646326480403)
XLA Ops:
  0.6 0.7 multiply_bitcast_fusion
  1.3 0.7 stack.9
  2.0 0.7 stack.10
  2.7 0.6 pad_maximum_fusion.1.gain_ref
  3.3 1.4 select_reduce_fusion
  4.7 0.7 copy.31.scale_ref.rest_14_
  5.4 1.1 constant_dynamic-slice_fusion.2
  6.5 0.1 copy.33
  6.6 1.2 constant_dynamic-slice_fusion
  7.8 0.1 copy.35
  8.0 0.1 copy.34
  8.1 0.7 pad_maximum_fusion.wt_ref
  8.9 91.1 %forward.1 = (f32[2,1280]{1,0:T(2,128)}, bf16[16,80,256]{2,1,0:T(8,128)(2,1)}, bf16[8,512,1280]{2,1,0:T(8,128)(2,1)}, f32[8,80,512]{2,1,0:T(8,128)}, f32[8,1,512...) custom-call(bf16[256,1280]{1,0:T(8,128)(2,1)} %bitcast.15, ...), custom_call_target="tpu_custom_call" | custom-call | tf_op jit(solution)/shard_map/forward/pallas_call | solution.py:746
  100.0 173.8 %tail.1 = (bf16[16,6,80,640]{3,2,1,0:T(8,128)(2,1)}, bf16[256,1280]{1,0:T(8,128)(2,1)}, f32[2,640]{1,0:T(2,128)}, f32[1,80]{1,0:T(1,128)}, bf16[256,1280]{1,0:T(...) custom-call(bf16[640,1280]{1,0:T(8,128)(2,1)} %rest_0_.3, bf16[640,1280]{1,0:T(8,128)(2,1)} %rest_1_.3, ...), custom_call_target="tpu_custom_call" | custom-call | tf_op jit(solution)/shard_map/tail/pallas_call | solution.py:1416
  273.9 1.4 slice_reduce_fusion
  275.3 0.0 copy-start.1
  275.3 12.6 %spread.1 = (f32[640,1280]{1,0:T(8,128)}, f32[640,1280]{1,0:T(8,128)}, f32[640,1280]{1,0:T(8,128)}, f32[640,1280]{1,0:T(8,128)}, f32[640,1280]{1,0:T(8,128)}, /*index=5*/f32[640,1280]{1,0:T(8,128)}) custom-call(bf16[4,2,2,6,80,640]{5,4,3,2,1,0:T(8,128)(2,1)} %bitcast.14, bf16[16,6,80,640]{3,2,1,0:T(8,128)(2,1)} %get-tuple-element.54.heads_ref), custom_call_target="tpu_custom_call" | custom-call | tf_op jit(solution)/shard_map/spread/pallas_call | solution.py:1494
  287.9 0.0 copy-start
  287.9 0.0 copy-start.2
  287.9 0.0 copy-done.1
  287.9 0.8 copy.39
  288.7 0.5 copy-done
  289.2 0.8 copy.40
  290.0 0.0 copy-done.2
  290.0 0.5 copy.41
Async XLA Ops:
  275.3 12.6 %copy-start.1 = (bf16[256,1280]{1,0:T(8,128)(2,1)S(1)}, bf16[256,1280]{1,0:T(8,128)(2,1)}, u32[]{:S(2)}) copy-start(bf16[256,1280]{1,0:T(8,128)(2,1)} %get-tuple-element.52) | copy-start | bytes 1966084
  287.9 1.3 copy-start
  287.9 2.2 copy-start.2
